TPU v7x, 32 devices: a whole 2x2x4 slice. The times are simulated.
32 devices in a mesh: expert: 8 (over z, x), dp: 2 (over core), tensor: 2 (over y).
Axes of the slice: x: 2, y: 2, z: 4, core: 2. Of those that a mesh axis runs over, the one named last changes fastest.
Arguments:
- tokens: bfloat16 [3072, 3584], P(('expert', 'dp'), 'tensor'), may hold values from -6 to 6
- routes: int32 [3072, 8], P(('expert', 'dp')), may hold values from 0 to 255, all different within a row
- gates: bfloat16 [3072, 8], P(('expert', 'dp')), may hold values from 0.049804688 to 1
- cotangent: bfloat16 [3072, 3584], P(('expert', 'dp'), 'tensor'), may hold values from -6 to 6
- placement: int32 [8], replicated, may hold values from 0 to 7, each once
- swap_flag: int32 [8], replicated, may hold values from 0 to 1, as said below
- w_gate: bfloat16 [8, 3584, 1024], P('expert', 'dp', 'tensor'), may hold values from -0.09375 to 0.09375
- w_up: bfloat16 [8, 3584, 1024], P('expert', 'dp', 'tensor'), may hold values from -0.09375 to 0.09375
- w_down: bfloat16 [8, 3584, 1024], P('expert', 'dp', 'tensor'), may hold values from -0.1875 to 0.1875
Outputs:
- layer_out: bfloat16 [3072, 3584], P(('expert', 'dp'), 'tensor')
- input_grad: bfloat16 [3072, 3584], P(('expert', 'dp'), 'tensor')
- gate_grad: float32 [3072, 8], P(('expert', 'dp'))
- grad_gate_w: bfloat16 [8, 3584, 1024], P('expert', 'dp', 'tensor')
- grad_up_w: bfloat16 [8, 3584, 1024], P('expert', 'dp', 'tensor')
- grad_down_w: bfloat16 [8, 3584, 1024], P('expert', 'dp', 'tensor')
Inputs may be any that keep to these rules, and one draw needn't show every extreme that they name: `swap_flag`: entry i equals entry (i + 4) mod 8; some pair has 1 and some pair 0. `placement`: a permutation of the positions. `routes`: each row names 8 different experts.
All inputs are finite; a program needn't handle non-finite values.
Results may differ from a plain program's by a relative error of at most 0.0095.
Values may be sent and summed in bfloat16 or wider, within the bound.
No kernel may reach another device: no remote copies, remote signals or barrier semaphores. Data moves between devices by JAX's collectives and lax.ppermute only.
A program may use at most 128 MiB of HBM per device.

v0:
```python
import jax
import jax.numpy as jnp
from jax import lax
from jax.sharding import PartitionSpec as P

CAP = 9
BF = jnp.bfloat16
F32 = jnp.float32
LANES = 128

contract = (((0,), (0,)), ((), ()))
inner = (((1,), (1,)), ((), ()))


def dot(a, b, dims):
    return lax.dot_general(a, b, dims, preferred_element_type=F32)


def pick(stack, index, count):
    return stack[0] if count == 1 else lax.dynamic_index_in_dim(stack, index, 0, keepdims=False)


class Layout:
    def __init__(self):
        self.n_d = lax.axis_size("dp")
        self.n_t = lax.axis_size("tensor")
        self.group = self.n_d // self.n_t
        self.d = lax.axis_index("dp")
        self.t = lax.axis_index("tensor")
        self.order = (self.d % self.group) * self.n_t + self.t

    def pairs(self, step):
        route = []
        for d in range(self.n_d):
            for t in range(self.n_t):
                half = d // self.group
                data = ((d % self.group) * self.n_t + t + step) % self.n_d
                route.append((data * self.n_t + half, d * self.n_t + t))
        return route

    def canonical(self, blocks):
        if self.group == 1:
            return jnp.stack(blocks)
        whole = jnp.stack(blocks)
        return jnp.take(whole, (jnp.arange(self.n_d) - self.order) % self.n_d, axis=0)

    def spread(self, rows):
        blocks = []
        for step in range(self.n_d):
            target = (self.d - step) % self.n_d
            chunk = pick(rows, target // self.n_t, self.group)
            blocks.append(lax.ppermute(chunk, ("dp", "tensor"), self.pairs(step)))
        return self.canonical(blocks)

    def collect(self, blocks):
        parts = []
        for step in range(self.n_d):
            if self.group == 1:
                block = blocks[step]
            else:
                block = pick(blocks, (self.order + step) % self.n_d, self.n_d)
            route = [(b, a) for a, b in self.pairs(step)]
            got = lax.ppermute(block, ("dp", "tensor"), route)
            got = got.astype(F32)
            source = (self.d - step) % self.n_d
            parts.append(
                jnp.stack([jnp.where(source // self.n_t == c, got, 0.0) for c in range(self.group)])
                if self.group > 1
                else got[None]
            )
        total = parts[0]
        for part in parts[1:]:
            total = total + part
        return total.astype(BF)

    def summed(self, value):
        total = value
        for step in range(1, self.n_d):
            route = [(i, (i + step) % self.n_d) for i in range(self.n_d)]
            other = lax.ppermute(value, "dp", route)
            total = total + other
        return total

    def gathered(self, value):
        if self.n_d == 2:
            other = lax.ppermute(value, "dp", [(0, 1), (1, 0)])
            first = self.d == 0
            return jnp.stack([jnp.where(first, value, other), jnp.where(first, other, value)])
        return lax.all_gather(value, "dp", axis=0)


def exchanged(rows, experts):
    cols = rows.shape[1]
    flat = rows.reshape(experts, CAP * cols // LANES, LANES)
    got = lax.all_to_all(flat, "expert", split_axis=0, concat_axis=0, tiled=True)
    return got.reshape(experts * CAP, cols)


def on_device(tokens, routes, gates, cotangent, placement, swap_flag, w_gate, w_up, w_down):
    experts = lax.axis_size("expert")
    myself = lax.axis_index("expert")
    lay = Layout()
    places = jnp.arange(experts, dtype=jnp.int32)
    my_flag = jnp.sum(jnp.where(places == myself, swap_flag, 0)) == 1
    wg, wu, wd = w_gate[0], w_up[0], w_down[0]
    chunk, units = wg.shape
    tok_count, top_count = routes.shape
    slots_all = experts * CAP
    half_width = tokens.shape[1]

    slot_ids = lax.broadcasted_iota(jnp.int32, (1, slots_all), 1)
    wanted = jnp.repeat(placement, CAP)[None, :]
    match = [routes[:, k : k + 1] == wanted for k in range(top_count)]
    hit = match[0]
    for m in match[1:]:
        hit = hit | m
    weight = jnp.zeros((tok_count, slots_all), F32)
    for k in range(top_count):
        weight = weight + jnp.where(match[k], gates[:, k : k + 1].astype(F32), 0.0)
    row_id = lax.broadcasted_iota(jnp.int32, (tok_count, tok_count), 0)
    col_id = lax.broadcasted_iota(jnp.int32, (tok_count, tok_count), 1)
    before = (col_id < row_id).astype(BF)
    earlier = jnp.dot(before, hit.astype(BF), preferred_element_type=F32)
    live = hit & (earlier == (slot_ids % CAP).astype(F32))
    select = live.astype(BF)
    weighted = jnp.where(live, weight, 0.0).astype(BF)

    outgoing = jnp.concatenate(
        [dot(select, tokens, contract).astype(BF), dot(weighted, cotangent, contract).astype(BF)],
        axis=1,
    )
    arrived = exchanged(outgoing, experts)

    def chunks(rows):
        both = rows.reshape(slots_all, 2, lay.group, chunk)
        if lay.group == 1:
            return rows[None]
        return jnp.moveaxis(both, 2, 0).reshape(lay.group, slots_all, 2 * chunk)

    mine = lay.spread(chunks(arrived)).reshape(lay.n_d * slots_all, 2 * chunk)
    x_rows, d_rows = mine[:, :chunk], mine[:, chunk:]
    pre_gate = lay.summed(jnp.dot(x_rows, wg, preferred_element_type=F32))
    pre_up = lay.summed(jnp.dot(x_rows, wu, preferred_element_type=F32))
    d_hidden = lay.summed(jnp.dot(d_rows, wd, preferred_element_type=F32))
    sig = jax.nn.sigmoid(pre_gate)
    hidden = (pre_gate * sig * pre_up).astype(BF)
    d_pre_gate = (d_hidden * pre_up * sig * (1.0 + pre_gate * (1.0 - sig))).astype(BF)
    d_pre_up = (d_hidden * pre_gate * sig).astype(BF)
    out_terms = dot(hidden, wd, inner).astype(BF)
    in_terms = (dot(d_pre_gate, wg, inner) + dot(d_pre_up, wu, inner)).astype(BF)
    terms = jnp.concatenate([out_terms, in_terms], axis=1).reshape(lay.n_d, slots_all, 2 * chunk)
    sums = lay.collect(terms)
    if lay.group == 1:
        home = sums[0]
    else:
        home = jnp.moveaxis(sums.reshape(lay.group, slots_all, 2, chunk), 0, 2).reshape(
            slots_all, 2 * half_width
        )
    partner = [(i, (i + experts // 2) % experts) for i in range(experts)]
    moved = lax.ppermute(arrived, "expert", partner)
    held_rows = jnp.where(my_flag, moved, arrived)
    back = exchanged(home, experts)
    out_rows, in_rows = back[:, :half_width], back[:, half_width:]
    scores = dot(cotangent, out_rows, inner)
    scores = jnp.where(live, scores, 0.0)
    gate_part = jnp.stack(
        [jnp.sum(jnp.where(m, scores, 0.0), axis=1) for m in match], axis=0
    )
    gate_grad = gate_part
    for step in range(1, lay.n_t):
        gate_grad = gate_grad + lax.ppermute(
            gate_part, "tensor", [(i, (i + step) % lay.n_t) for i in range(lay.n_t)]
        )
    gate_grad = gate_grad.T
    layer_out = jnp.dot(weighted, out_rows, preferred_element_type=F32).astype(BF)
    input_grad = jnp.dot(select, in_rows, preferred_element_type=F32).astype(BF)

    held_rows = lay.spread(chunks(held_rows)).reshape(lay.n_d * slots_all, 2 * chunk)
    units_all = jnp.concatenate([d_pre_gate, d_pre_up, hidden], axis=1)
    units_own = pick(
        units_all.reshape(lay.n_d, slots_all, 3 * units), lay.d, lay.n_d
    )
    units_moved = lax.ppermute(units_own, "expert", partner)
    units_held = lay.gathered(jnp.where(my_flag, units_moved, units_own)).reshape(
        lay.n_d * slots_all, 3 * units
    )
    hx, hd = held_rows[:, :chunk], held_rows[:, chunk:]
    grads = (
        dot(hx, units_held[:, :units], contract).astype(BF)[None],
        dot(hx, units_held[:, units : 2 * units], contract).astype(BF)[None],
        dot(hd, units_held[:, 2 * units :], contract).astype(BF)[None],
    )
    return (layer_out, input_grad, gate_grad, grads[0], grads[1], grads[2])


def solution(mesh):
    placed = (
        P(("expert", "dp"), "tensor"),
        P(("expert", "dp"), None),
        P(("expert", "dp"), None),
        P(("expert", "dp"), "tensor"),
        P(),
        P(),
        P("expert", "dp", "tensor"),
        P("expert", "dp", "tensor"),
        P("expert", "dp", "tensor"),
    )

    return jax.shard_map(
        on_device,
        mesh=mesh,
        in_specs=placed,
        out_specs=(
            P(("expert", "dp"), "tensor"),
            P(("expert", "dp"), "tensor"),
            P(("expert", "dp"), None),
            P("expert", "dp", "tensor"),
            P("expert", "dp", "tensor"),
            P("expert", "dp", "tensor"),
        ),
        check_vma=False,
    )
```

profile of v0, /device:TPU:0, one launch (start us, length us, event | category | flops | bytes accessed | tf_op | source)
XLA Modules:
  0.0 112.9 jit_solution(12545719855614279224)
XLA Ops:
  0.7 1.0 fusion.59
  1.7 0.7 broadcast_in_dim.123
  2.5 1.0 slice_convert_fusion.7
  3.7 1.3 %convolution_convert_fusion.7 = bf16[72,1792]{1,0:T(8,128)(2,1)S(1)} fusion(pred[192,72]{0,1:T(8,128)(4,1)S(1)} %fusion.15, bf16[192,1792]{1,0:T(8,128)(2,1)} %param.9), kind=kOutput, calls=%fused_computation.12 | convolution fusion | flops 49674240 | bytes 960000 | tf_op jit(solution)/shard_map/dot_general | solution.py:16
  5.1 1.4 %convolution_convert_fusion.6 = bf16[72,1792]{1,0:T(8,128)(2,1)S(1)} fusion(bf16[192,1792]{1,0:T(8,128)(2,1)} %param.12, pred[192,72]{0,1:T(8,128)(4,1)S(1)} %fusion.15, f32[192]{0:T(256)S(1)} %bitcast.134, f32[192]{0:T(256)S(1)} %bitcast.136, f32[192]{0:T(256)S(1)} %bitcast.124, f32[192]{0:T(256)S(1)} %bitcast.126, f32[192]{0:T(256)S(1)} %bitcast.128, ...), kind=kOutput, calls=%fused_computation.11 | convolution fusion | flops 50019840 | bytes 972576 | tf_op jit(solution)/shard_map/dot_general | solution.py:16
  7.2 21.6 %all_to_all.10 = bf16[8,252,128]{2,1,0:T(8,128)(2,1)S(1)} all-to-all(bf16[8,252,128]{2,1,0:T(8,128)(2,1)S(1)} %reshape.57), channel_id=1, replica_groups=mesh['expert'=8,'dp'=2,'tensor'=2] {'expert'}, dimensions={0} | all-to-all | bytes 1032192 | tf_op jit(solution)/shard_map/all_to_all | solution.py:95
  30.1 2.8 %collective-permute-start.1 = (bf16[72,3584]{1,0:T(8,128)(2,1)S(1)}, bf16[72,3584]{1,0:T(8,128)(2,1)S(1)}, u32[]{:S(2)}, u32[]{:S(2)}) collective-permute-start(bf16[72,3584]{1,0:T(8,128)(2,1)S(1)} %squeeze_broadcast_in_dim_reshape.4), channel_id=1, source_target_pairs={{2,0},{0,1},{3,2},{1,3},{6,4},{4,5},{7,6},{5,7},{10,8},{8,9},{11,1... | collective-permute-start | bytes 1548296 | tf_op jit(solution)/shard_map/ppermute | solution.py:52
  34.2 1.1 %collective-permute-start.8 = (bf16[72,3584]{1,0:T(8,128)(2,1)S(1)}, bf16[72,3584]{1,0:T(8,128)(2,1)S(1)}, u32[]{:S(2)}, u32[]{:S(2)}) collective-permute-start(bf16[72,3584]{1,0:T(8,128)(2,1)S(1)} %squeeze_broadcast_in_dim_reshape.4), channel_id=1, source_target_pairs={{0,16},{4,20},{8,24},{12,28},{16,0},{20,4},{24,8},{28,12},{1,17},{... | collective-permute-start | bytes 1548296 | tf_op jit(solution)/shard_map/ppermute | solution.py:160
  35.3 9.1 %collective-permute-done.1 = bf16[72,3584]{1,0:T(8,128)(2,1)S(1)} collective-permute-done((bf16[72,3584]{1,0:T(8,128)(2,1)S(1)}, bf16[72,3584]{1,0:T(8,128)(2,1)S(1)}, u32[]{:S(2)}, u32[]{:S(2)}) %collective-permute-start.1) | collective-permute-done | bytes 516128 | tf_op jit(solution)/shard_map/ppermute | solution.py:52
  45.0 0.9 collective-permute-start.2
  46.5 0.9 collective-permute-start.3
  48.1 11.9 %collective-permute-done.8 = bf16[72,3584]{1,0:T(8,128)(2,1)S(1)} collective-permute-done((bf16[72,3584]{1,0:T(8,128)(2,1)S(1)}, bf16[72,3584]{1,0:T(8,128)(2,1)S(1)}, u32[]{:S(2)}, u32[]{:S(2)}) %collective-permute-start.8) | collective-permute-done | bytes 516128 | tf_op jit(solution)/shard_map/ppermute | solution.py:160
  60.1 0.7 collective-permute-start.9
  60.8 2.4 %collective-permute-start.10 = (bf16[72,3584]{1,0:T(8,128)(2,1)S(1)}, bf16[72,3584]{1,0:T(8,128)(2,1)S(1)}, u32[]{:S(2)}, u32[]{:S(2)}) collective-permute-start(bf16[72,3584]{1,0:T(8,128)(2,1)S(1)} %broadcast_select_fusion), channel_id=1, source_target_pairs={{2,0},{0,1},{3,2},{1,3},{6,4},{4,5},{7,6},{5,7},{10,8},{8,9},{11,1... | collective-permute-start | bytes 1548296 | tf_op jit(solution)/shard_map/ppermute | solution.py:52
  63.4 0.7 fusion.10
  64.2 0.7 convolution_convert_fusion.5
  65.1 0.7 fusion.3
  66.6 1.4 %collective-permute-start.6 = (bf16[72,3584]{1,0:T(8,128)(2,1)S(1)}, bf16[72,3584]{1,0:T(8,128)(2,1)S(1)}, u32[]{:S(2)}, u32[]{:S(2)}) collective-permute-start(bf16[72,3584]{1,0:T(8,128)(2,1)S(1)} %get-tuple-element.18), channel_id=1, source_target_pairs={{0,2},{1,0},{2,3},{3,1},{4,6},{5,4},{6,7},{7,5},{8,10},{9,8},{10,1... | collective-permute-start | bytes 1548296 | tf_op jit(solution)/shard_map/ppermute | solution.py:63
  68.0 7.6 %collective-permute-done.11 = bf16[72,1536]{1,0:T(8,128)(2,1)S(1)} collective-permute-done((bf16[72,1536]{1,0:T(8,128)(2,1)S(1)}, bf16[72,1536]{1,0:T(8,128)(2,1)S(1)}, u32[]{:S(2)}, u32[]{:S(2)}) %collective-permute-start.11) | collective-permute-done | bytes 221216 | tf_op jit(solution)/shard_map/ppermute | solution.py:183
  75.6 0.7 broadcast_select_fusion.1
  76.4 10.3 %collective-permute-done.6 = bf16[72,3584]{1,0:T(8,128)(2,1)S(1)} collective-permute-done((bf16[72,3584]{1,0:T(8,128)(2,1)S(1)}, bf16[72,3584]{1,0:T(8,128)(2,1)S(1)}, u32[]{:S(2)}, u32[]{:S(2)}) %collective-permute-start.6) | collective-permute-done | bytes 516128 | tf_op jit(solution)/shard_map/ppermute | solution.py:63
  86.9 1.5 %reshape_squeeze.3 = bf16[8,252,128]{2,1,0:T(8,128)(2,1)} reshape(bf16[72,3584]{1,0:T(8,128)(2,1)S(1)} %add_convert_fusion) | data formatting | bytes 1032192 | tf_op jit(solution)/shard_map/reshape;squeeze | solution.py:94
  88.3 3.9 %all-to-all-start.1 = ((bf16[8,252,128]{2,1,0:T(8,128)(2,1)}), bf16[8,252,128]{2,1,0:T(8,128)(2,1)S(1)}, u32[]{:S(2)}, u32[]{:S(2)}) async-start(bf16[8,252,128]{2,1,0:T(8,128)(2,1)} %reshape_squeeze.3), calls=%async_computation.1 | async-start | bytes 1048576 | tf_op jit(solution)/shard_map/all_to_all | solution.py:95
  92.2 1.1 select_bitcast_fusion.1
  93.3 1.9 %fusion.2 = bf16[1,1792,512]{2,1,0:T(8,128)(2,1)} fusion(bf16[144,3584]{1,0:T(8,128)(2,1)S(1)} %bitcast.75, bf16[144,1536]{1,0:T(8,128)(2,1)S(1)} %bitcast.81), kind=kOutput, calls=%fused_computation.5 | convolution fusion | flops 265158656 | bytes 2498560 | tf_op jit(solution)/shard_map/dot_general | solution.py:16
  95.3 1.9 %fusion.1 = bf16[1,1792,512]{2,1,0:T(8,128)(2,1)} fusion(bf16[144,3584]{1,0:T(8,128)(2,1)S(1)} %bitcast.76, bf16[144,1536]{1,0:T(8,128)(2,1)S(1)} %bitcast.82), kind=kOutput, calls=%fused_computation.4 | convolution fusion | flops 265158656 | bytes 2498560 | tf_op jit(solution)/shard_map/dot_general | solution.py:16
  97.2 1.9 %fusion = bf16[1,1792,512]{2,1,0:T(8,128)(2,1)} fusion(bf16[144,3584]{1,0:T(8,128)(2,1)S(1)} %bitcast.77, bf16[144,1536]{1,0:T(8,128)(2,1)S(1)} %bitcast.83), kind=kOutput, calls=%fused_computation.3 | convolution fusion | flops 265158656 | bytes 2498560 | tf_op jit(solution)/shard_map/dot_general | solution.py:16
  99.1 5.8 %all-to-all-done.1 = bf16[8,252,128]{2,1,0:T(8,128)(2,1)S(1)} async-done(((bf16[8,252,128]{2,1,0:T(8,128)(2,1)}), bf16[8,252,128]{2,1,0:T(8,128)(2,1)S(1)}, u32[]{:S(2)}, u32[]{:S(2)}) %all-to-all-start.1) | async-done | bytes 516128 | tf_op jit(solution)/shard_map/all_to_all | solution.py:95
  105.5 1.6 %fusion.45 = (f32[192]{0:T(256)S(1)}, f32[192]{0:T(256)S(1)}, f32[192]{0:T(256)S(1)}, f32[192]{0:T(256)S(1)}, f32[192]{0:T(256)S(1)}, /*index=5*/f32[192]{0:T(256)S(1)}, f32[192]{0:T(256)S(1)}, f32[192]{0:T(256)S(1)}) fusion(s32[192]{0:T(256)S(1)} %bitcast.116, s32[72]{0:T(128)S(1)} %eq.132, s32[192]{0:T(256)S(1)} %bitcast.120, s32[192]{0:T(256)S(1)} %bitcast.96, ...), kind=kOutput, calls=%fused_computation.98 | convolution fusion | flops 49889280 | bytes 979456 | tf_op jit(solution)/shard_map/dot_general | solution.py:16
  107.1 1.4 %convolution_convert_fusion.4 = bf16[192,1792]{1,0:T(8,128)(2,1)} fusion(bf16[72,3584]{1,0:T(8,128)(2,1)S(1)} %reshape.59, pred[192,72]{0,1:T(8,128)(4,1)S(1)} %fusion.15, f32[192]{0:T(256)S(1)} %bitcast.135, f32[192]{0:T(256)S(1)} %bitcast.137, f32[192]{0:T(256)S(1)} %bitcast.125, f32[192]{0:T(256)S(1)} %bitcast.127, f32[192]{0:T(256)S(1)} %bitcast.129, ...), kind=kOutput, calls=%fused_computation.8 | convolution fusion | flops 50234880 | bytes 981504 | tf_op jit(solution)/shard_map/dot_general | solution.py:175
  108.5 2.2 %collective-permute-start.7 = (f32[8,192]{1,0:T(8,128)S(1)}, f32[8,192]{1,0:T(8,128)S(1)}, u32[]{:S(2)}, u32[]{:S(2)}) collective-permute-start(f32[8,192]{1,0:T(8,128)S(1)} %stack.65), channel_id=1, source_target_pairs={{0,1},{1,0},{2,3},{3,2},{4,5},{5,4},{6,7},{7,6},{8,9},{9,8},{10,11... | collective-permute-start | bytes 18440 | tf_op jit(solution)/shard_map/ppermute | solution.py:171
  110.7 1.2 %convolution_convert_fusion.3 = bf16[192,1792]{1,0:T(8,128)(2,1)} fusion(pred[192,72]{0,1:T(8,128)(4,1)S(1)} %fusion.15, bf16[72,3584]{1,0:T(8,128)(2,1)S(1)} %reshape.59), kind=kOutput, calls=%fused_computation.7 | convolution fusion | flops 49889280 | bytes 964608 | tf_op jit(solution)/shard_map/dot_general | solution.py:176
  (44 shorter events, 7.8 us)
Async XLA Ops:
  0.6 43.9 %copy-start = (bf16[1,1792,512]{2,1,0:T(8,128)(2,1)S(1)}, bf16[1,1792,512]{2,1,0:T(8,128)(2,1)}, u32[]{:S(2)}) copy-start(bf16[1,1792,512]{2,1,0:T(8,128)(2,1)} %param.15) | copy-start | bytes 5505028
  6.5 26.4 %copy-start.3 = (s32[8]{0:T(128)S(1)}, s32[8]{0:T(128)}, u32[]{:S(2)}) copy-start(s32[8]{0:T(128)} %param.14) | copy-start | bytes 100
  29.4 5.9 %collective-permute-start = (bf16[72,3584]{1,0:T(8,128)(2,1)S(1)}, bf16[72,3584]{1,0:T(8,128)(2,1)S(1)}, u32[]{:S(2)}, u32[]{:S(2)}) collective-permute-start(bf16[72,3584]{1,0:T(8,128)(2,1)S(1)} %squeeze_broadcast_in_dim_reshape.4), channel_id=1, source_target_pairs={{0,0},{2,1},{1,2},{3,3},{4,4},{6,5},{5,6},{7,7},{8,8},{10,9},{9,10... | collective-permute-start | bytes 1548296 | tf_op jit(solution)/shard_map/ppermute | solution.py:52
  30.1 14.3 %collective-permute-start.1 = (bf16[72,3584]{1,0:T(8,128)(2,1)S(1)}, bf16[72,3584]{1,0:T(8,128)(2,1)S(1)}, u32[]{:S(2)}, u32[]{:S(2)}) collective-permute-start(bf16[72,3584]{1,0:T(8,128)(2,1)S(1)} %squeeze_broadcast_in_dim_reshape.4), channel_id=1, source_target_pairs={{2,0},{0,1},{3,2},{1,3},{6,4},{4,5},{7,6},{5,7},{10,8},{8,9},{11,1... | collective-permute-start | bytes 1548296 | tf_op jit(solution)/shard_map/ppermute | solution.py:52
  34.2 25.8 %collective-permute-start.8 = (bf16[72,3584]{1,0:T(8,128)(2,1)S(1)}, bf16[72,3584]{1,0:T(8,128)(2,1)S(1)}, u32[]{:S(2)}, u32[]{:S(2)}) collective-permute-start(bf16[72,3584]{1,0:T(8,128)(2,1)S(1)} %squeeze_broadcast_in_dim_reshape.4), channel_id=1, source_target_pairs={{0,16},{4,20},{8,24},{12,28},{16,0},{20,4},{24,8},{28,12},{1,17},{... | collective-permute-start | bytes 1548296 | tf_op jit(solution)/shard_map/ppermute | solution.py:160
  44.5 1.5 %copy-start.2 = (bf16[1,1792,512]{2,1,0:T(8,128)(2,1)S(1)}, bf16[1,1792,512]{2,1,0:T(8,128)(2,1)}, u32[]{:S(2)}) copy-start(bf16[1,1792,512]{2,1,0:T(8,128)(2,1)} %param.16) | copy-start | bytes 5505028
  45.0 2.4 %copy-start.1 = (bf16[1,1792,512]{2,1,0:T(8,128)(2,1)S(1)}, bf16[1,1792,512]{2,1,0:T(8,128)(2,1)}, u32[]{:S(2)}) copy-start(bf16[1,1792,512]{2,1,0:T(8,128)(2,1)} %param.17) | copy-start | bytes 5505028
  45.0 18.1 %collective-permute-start.2 = (f32[144,512]{1,0:T(8,128)S(1)}, f32[144,512]{1,0:T(8,128)S(1)}, u32[]{:S(2)}, u32[]{:S(2)}) collective-permute-start(f32[144,512]{1,0:T(8,128)S(1)} %fusion.12), channel_id=1, source_target_pairs={{0,2},{2,0},{1,3},{3,1},{4,6},{6,4},{5,7},{7,5},{8,10},{10,8},{9,1... | collective-permute-start | bytes 884744 | tf_op jit(solution)/shard_map/ppermute | solution.py:80
  46.5 16.7 %collective-permute-start.3 = (f32[144,512]{1,0:T(8,128)S(1)}, f32[144,512]{1,0:T(8,128)S(1)}, u32[]{:S(2)}, u32[]{:S(2)}) collective-permute-start(f32[144,512]{1,0:T(8,128)S(1)} %fusion.8), channel_id=1, source_target_pairs={{0,2},{2,0},{1,3},{3,1},{4,6},{6,4},{5,7},{7,5},{8,10},{10,8},{9,1... | collective-permute-start | bytes 884744 | tf_op jit(solution)/shard_map/ppermute | solution.py:80
  47.8 15.3 %collective-permute-start.4 = (f32[144,512]{1,0:T(8,128)S(1)}, f32[144,512]{1,0:T(8,128)S(1)}, u32[]{:S(2)}, u32[]{:S(2)}) collective-permute-start(f32[144,512]{1,0:T(8,128)S(1)} %fusion.4), channel_id=1, source_target_pairs={{0,2},{2,0},{1,3},{3,1},{4,6},{6,4},{5,7},{7,5},{8,10},{10,8},{9,1... | collective-permute-start | bytes 884744 | tf_op jit(solution)/shard_map/ppermute | solution.py:80
  60.1 16.2 %collective-permute-start.9 = (bf16[72,3584]{1,0:T(8,128)(2,1)S(1)}, bf16[72,3584]{1,0:T(8,128)(2,1)S(1)}, u32[]{:S(2)}, u32[]{:S(2)}) collective-permute-start(bf16[72,3584]{1,0:T(8,128)(2,1)S(1)} %broadcast_select_fusion), channel_id=1, source_target_pairs={{0,0},{2,1},{1,2},{3,3},{4,4},{6,5},{5,6},{7,7},{8,8},{10,9},{9,10... | collective-permute-start | bytes 1548296 | tf_op jit(solution)/shard_map/ppermute | solution.py:52
  60.8 15.5 %collective-permute-start.10 = (bf16[72,3584]{1,0:T(8,128)(2,1)S(1)}, bf16[72,3584]{1,0:T(8,128)(2,1)S(1)}, u32[]{:S(2)}, u32[]{:S(2)}) collective-permute-start(bf16[72,3584]{1,0:T(8,128)(2,1)S(1)} %broadcast_select_fusion), channel_id=1, source_target_pairs={{2,0},{0,1},{3,2},{1,3},{6,4},{4,5},{7,6},{5,7},{10,8},{8,9},{11,1... | collective-permute-start | bytes 1548296 | tf_op jit(solution)/shard_map/ppermute | solution.py:52
  65.0 10.6 %collective-permute-start.11 = (bf16[72,1536]{1,0:T(8,128)(2,1)S(1)}, bf16[72,1536]{1,0:T(8,128)(2,1)S(1)}, u32[]{:S(2)}, u32[]{:S(2)}) collective-permute-start(bf16[72,1536]{1,0:T(8,128)(2,1)S(1)} %dynamic-slice_bitcast_fusion), channel_id=1, source_target_pairs={{0,16},{4,20},{8,24},{12,28},{16,0},{20,4},{24,8},{28,12},{1,17},{... | collective-permute-start | bytes 663560 | tf_op jit(solution)/shard_map/ppermute | solution.py:183
  65.9 10.5 %collective-permute-start.5 = (bf16[72,3584]{1,0:T(8,128)(2,1)S(1)}, bf16[72,3584]{1,0:T(8,128)(2,1)S(1)}, u32[]{:S(2)}, u32[]{:S(2)}) collective-permute-start(bf16[72,3584]{1,0:T(8,128)(2,1)S(1)} %get-tuple-element.17), channel_id=1, source_target_pairs={{0,0},{1,2},{2,1},{3,3},{4,4},{5,6},{6,5},{7,7},{8,8},{9,10},{10,9... | collective-permute-start | bytes 1548296 | tf_op jit(solution)/shard_map/ppermute | solution.py:63
  66.6 20.2 %collective-permute-start.6 = (bf16[72,3584]{1,0:T(8,128)(2,1)S(1)}, bf16[72,3584]{1,0:T(8,128)(2,1)S(1)}, u32[]{:S(2)}, u32[]{:S(2)}) collective-permute-start(bf16[72,3584]{1,0:T(8,128)(2,1)S(1)} %get-tuple-element.18), channel_id=1, source_target_pairs={{0,2},{1,0},{2,3},{3,1},{4,6},{5,4},{6,7},{7,5},{8,10},{9,8},{10,1... | collective-permute-start | bytes 1548296 | tf_op jit(solution)/shard_map/ppermute | solution.py:63
  76.3 15.9 %collective-permute-start.12 = (bf16[72,1536]{1,0:T(8,128)(2,1)}, bf16[72,1536]{1,0:T(8,128)(2,1)}, u32[]{:S(2)}, u32[]{:S(2)}) collective-permute-start(bf16[72,1536]{1,0:T(8,128)(2,1)} %broadcast_select_fusion.1), channel_id=1, source_target_pairs={{0,2},{2,0},{1,3},{3,1},{4,6},{6,4},{5,7},{7,5},{8,10},{10,8},{9,1... | collective-permute-start | bytes 663560 | tf_op jit(solution)/shard_map/ppermute | solution.py:86
  88.3 16.6 %all-to-all-start.1 = ((bf16[8,252,128]{2,1,0:T(8,128)(2,1)}), bf16[8,252,128]{2,1,0:T(8,128)(2,1)S(1)}, u32[]{:S(2)}, u32[]{:S(2)}) async-start(bf16[8,252,128]{2,1,0:T(8,128)(2,1)} %reshape_squeeze.3), calls=%async_computation.1 | async-start | bytes 1048576 | tf_op jit(solution)/shard_map/all_to_all | solution.py:95
  108.5 3.8 %collective-permute-start.7 = (f32[8,192]{1,0:T(8,128)S(1)}, f32[8,192]{1,0:T(8,128)S(1)}, u32[]{:S(2)}, u32[]{:S(2)}) collective-permute-start(f32[8,192]{1,0:T(8,128)S(1)} %stack.65), channel_id=1, source_target_pairs={{0,1},{1,0},{2,3},{3,2},{4,5},{5,4},{6,7},{7,6},{8,9},{9,8},{10,11... | collective-permute-start | bytes 18440 | tf_op jit(solution)/shard_map/ppermute | solution.py:171
where the time goes:
time: 113 us
  waiting for transfers between devices  45.2 us (40%)
  blocking collectives  21.6 us (19%)
  starting transfers between devices  17.9 us (16%)
  matrix products  16.5 us (15%)
  local copies, waits for them, and re-layouts  5.29 us (5%)
  other arithmetic  4.85 us (4%)
  between operations  1.53 us (1%)
    all_to_all x1, blocking collectives, exchanged(): lax.all_to_all(flat, 'expert', split_axis=0, concat_axis=0, tiled=True)  21.6 us
    dot_general x9, matrix products, dot(): return lax.dot_general(a, b, dims, preferred_element_type=F32)  12.3 us
    ppermute x1, waiting for transfers between devices, on_device(): moved = lax.ppermute(arrived, 'expert', partner)  11.9 us
    ppermute x2, waiting for transfers between devices, collect(): got = lax.ppermute(block, ('dp', 'tensor'), route)  10.3 us
    ppermute x4, waiting for transfers between devices, spread(): blocks.append(lax.ppermute(chunk, ('dp', 'tensor'), self.pairs(step)))  9.1 us
    ppermute x1, waiting for transfers between devices, on_device(): units_moved = lax.ppermute(units_own, 'expert', partner)  7.6 us
    ppermute x4, starting transfers between devices, spread(): blocks.append(lax.ppermute(chunk, ('dp', 'tensor'), self.pairs(step)))  6.51 us
    all_to_all x1, waiting for transfers between devices, exchanged(): lax.all_to_all(flat, 'expert', split_axis=0, concat_axis=0, tiled=True)  5.84 us
  transfers between devices with their start and end apart: 14, of which 6 were waited for; matrix products, arithmetic and copies ran while one was open for 13% of the time, Pallas kernels for 0%

commit v1 on v0

--- a/solution.py
+++ b/solution.py
@@ -52,25 +52,26 @@
             blocks.append(lax.ppermute(chunk, ("dp", "tensor"), self.pairs(step)))
         return self.canonical(blocks)
 
-    def collect(self, blocks):
-        parts = []
+    def send_back(self, blocks):
+        got = []
         for step in range(self.n_d):
             if self.group == 1:
                 block = blocks[step]
             else:
                 block = pick(blocks, (self.order + step) % self.n_d, self.n_d)
             route = [(b, a) for a, b in self.pairs(step)]
-            got = lax.ppermute(block, ("dp", "tensor"), route)
-            got = got.astype(F32)
-            source = (self.d - step) % self.n_d
-            parts.append(
-                jnp.stack([jnp.where(source // self.n_t == c, got, 0.0) for c in range(self.group)])
-                if self.group > 1
-                else got[None]
-            )
-        total = parts[0]
-        for part in parts[1:]:
-            total = total + part
+            got.append(lax.ppermute(block, ("dp", "tensor"), route))
+        return got
+
+    def add_up(self, got):
+        total = None
+        for step, block in enumerate(got):
+            part = block.astype(F32)[None]
+            if self.group > 1:
+                place = ((self.d - step) % self.n_d) // self.n_t
+                mask = jnp.arange(self.group) == place
+                part = jnp.where(mask[:, None, None], part, 0.0)
+            total = part if total is None else total + part
         return total.astype(BF)
 
     def summed(self, value):
@@ -89,11 +90,13 @@
         return lax.all_gather(value, "dp", axis=0)
 
 
-def exchanged(rows, experts):
-    cols = rows.shape[1]
-    flat = rows.reshape(experts, CAP * cols // LANES, LANES)
+def flat_rows(rows, experts):
+    return rows.reshape(experts, CAP * rows.shape[1] // LANES, LANES)
+
+
+def exchanged(flat):
     got = lax.all_to_all(flat, "expert", split_axis=0, concat_axis=0, tiled=True)
-    return got.reshape(experts * CAP, cols)
+    return got.reshape(flat.shape[0] * CAP, flat.shape[1] * LANES // CAP)
 
 
 def on_device(tokens, routes, gates, cotangent, placement, swap_flag, w_gate, w_up, w_down):
@@ -106,6 +109,7 @@
     chunk, units = wg.shape
     tok_count, top_count = routes.shape
     slots_all = experts * CAP
+    rows_all = lay.n_d * slots_all
     half_width = tokens.shape[1]
 
     slot_ids = lax.broadcasted_iota(jnp.int32, (1, slots_all), 1)
@@ -129,37 +133,43 @@
         [dot(select, tokens, contract).astype(BF), dot(weighted, cotangent, contract).astype(BF)],
         axis=1,
     )
-    arrived = exchanged(outgoing, experts)
-
-    def chunks(rows):
-        both = rows.reshape(slots_all, 2, lay.group, chunk)
+    outgoing = flat_rows(outgoing, experts)
+    arrived = exchanged(outgoing)
+    traded = jnp.where(
+        (swap_flag == 1)[:, None, None], jnp.roll(outgoing, experts // 2, axis=0), outgoing
+    )
+    held_rows = exchanged(traded)
+
+    def spread(rows):
         if lay.group == 1:
-            return rows[None]
-        return jnp.moveaxis(both, 2, 0).reshape(lay.group, slots_all, 2 * chunk)
-
-    mine = lay.spread(chunks(arrived)).reshape(lay.n_d * slots_all, 2 * chunk)
-    x_rows, d_rows = mine[:, :chunk], mine[:, chunk:]
+            pieces = rows[None]
+        else:
+            pieces = jnp.moveaxis(rows.reshape(slots_all, lay.group, chunk), 1, 0)
+        return lay.spread(pieces).reshape(rows_all, chunk)
+
+    def send_back(terms):
+        return lay.send_back(terms.reshape(lay.n_d, slots_all, chunk))
+
+    def add_up(got):
+        return jnp.moveaxis(lay.add_up(got), 0, 1).reshape(slots_all, half_width)
+
+    x_rows = spread(arrived[:, :half_width])
+    d_rows = spread(arrived[:, half_width:])
     pre_gate = lay.summed(jnp.dot(x_rows, wg, preferred_element_type=F32))
     pre_up = lay.summed(jnp.dot(x_rows, wu, preferred_element_type=F32))
-    d_hidden = lay.summed(jnp.dot(d_rows, wd, preferred_element_type=F32))
     sig = jax.nn.sigmoid(pre_gate)
     hidden = (pre_gate * sig * pre_up).astype(BF)
+    pre_gate, pre_up, hidden = lax.optimization_barrier((pre_gate, pre_up, hidden))
+    sig = jax.nn.sigmoid(pre_gate)
+    out_terms = dot(hidden, wd, inner).astype(BF)
+    out_got = send_back(out_terms)
+    d_hidden = lay.summed(jnp.dot(d_rows, wd, preferred_element_type=F32))
     d_pre_gate = (d_hidden * pre_up * sig * (1.0 + pre_gate * (1.0 - sig))).astype(BF)
     d_pre_up = (d_hidden * pre_gate * sig).astype(BF)
-    out_terms = dot(hidden, wd, inner).astype(BF)
     in_terms = (dot(d_pre_gate, wg, inner) + dot(d_pre_up, wu, inner)).astype(BF)
-    terms = jnp.concatenate([out_terms, in_terms], axis=1).reshape(lay.n_d, slots_all, 2 * chunk)
-    sums = lay.collect(terms)
-    if lay.group == 1:
-        home = sums[0]
-    else:
-        home = jnp.moveaxis(sums.reshape(lay.group, slots_all, 2, chunk), 0, 2).reshape(
-            slots_all, 2 * half_width
-        )
-    partner = [(i, (i + experts // 2) % experts) for i in range(experts)]
-    moved = lax.ppermute(arrived, "expert", partner)
-    held_rows = jnp.where(my_flag, moved, arrived)
-    back = exchanged(home, experts)
+    in_got = send_back(in_terms)
+    home = jnp.concatenate([add_up(out_got), add_up(in_got)], axis=1)
+    back = exchanged(flat_rows(home, experts))
     out_rows, in_rows = back[:, :half_width], back[:, half_width:]
     scores = dot(cotangent, out_rows, inner)
     scores = jnp.where(live, scores, 0.0)
@@ -168,23 +178,22 @@
     )
     gate_grad = gate_part
     for step in range(1, lay.n_t):
-        gate_grad = gate_grad + lax.ppermute(
+        other = lax.ppermute(
             gate_part, "tensor", [(i, (i + step) % lay.n_t) for i in range(lay.n_t)]
         )
+        gate_grad = gate_grad + other
     gate_grad = gate_grad.T
     layer_out = jnp.dot(weighted, out_rows, preferred_element_type=F32).astype(BF)
     input_grad = jnp.dot(select, in_rows, preferred_element_type=F32).astype(BF)
 
-    held_rows = lay.spread(chunks(held_rows)).reshape(lay.n_d * slots_all, 2 * chunk)
     units_all = jnp.concatenate([d_pre_gate, d_pre_up, hidden], axis=1)
-    units_own = pick(
-        units_all.reshape(lay.n_d, slots_all, 3 * units), lay.d, lay.n_d
-    )
+    units_own = pick(units_all.reshape(lay.n_d, slots_all, 3 * units), lay.d, lay.n_d)
+    partner = [(i, (i + experts // 2) % experts) for i in range(experts)]
     units_moved = lax.ppermute(units_own, "expert", partner)
-    units_held = lay.gathered(jnp.where(my_flag, units_moved, units_own)).reshape(
-        lay.n_d * slots_all, 3 * units
-    )
-    hx, hd = held_rows[:, :chunk], held_rows[:, chunk:]
+    units_held = jnp.where(my_flag, units_moved, units_own)
+    units_held = lay.gathered(units_held).reshape(rows_all, 3 * units)
+    hx = spread(held_rows[:, :half_width])
+    hd = spread(held_rows[:, half_width:])
     grads = (
         dot(hx, units_held[:, :units], contract).astype(BF)[None],
         dot(hx, units_held[:, units : 2 * units], contract).astype(BF)[None],
@@ -205,6 +214,7 @@
         P("expert", "dp", "tensor"),
         P("expert", "dp", "tensor"),
     )
+
 
     return jax.shard_map(
         on_device,

time: 113 us -> 110 us (0.973)
  blocking collectives: 21.6 us -> 0 us
  starting transfers between devices: 17.9 us -> 38.5 us
  waiting for transfers between devices: 45.2 us -> 35.5 us
  other arithmetic: 4.85 us -> 9.05 us
  local copies, waits for them, and re-layouts: 5.29 us -> 8.12 us
    all_to_all x1 -> x0, blocking collectives: 21.6 us -> none  [exchanged(): lax.all_to_all(flat, 'expert', split_axis=0, concat_axis=0, tiled=True)]
    ppermute x3 -> x4, waiting for transfers between devices: 22.3 us -> 1.11 us  [send_back(): got.append(lax.ppermute(block, ('dp', 'tensor'), route))]
    all_to_all x1 -> x3, waiting for transfers between devices: 5.84 us -> 23.7 us  [exchanged(): lax.all_to_all(flat, 'expert', split_axis=0, concat_axis=0, tiled=True)]
    all_to_all x1 -> x3, starting transfers between devices: 3.86 us -> 14.7 us  [exchanged(): lax.all_to_all(flat, 'expert', split_axis=0, concat_axis=0, tiled=True)]
    ppermute x4 -> x8, starting transfers between devices: 6.51 us -> 14.8 us  [spread(): blocks.append(lax.ppermute(chunk, ('dp', 'tensor'), self.pairs(step)))]
    ppermute x4 -> x8, waiting for transfers between devices: 9.1 us -> 3.41 us  [spread(): blocks.append(lax.ppermute(chunk, ('dp', 'tensor'), self.pairs(step)))]
    reshape x2 -> x5, local copies, waits for them, and re-layouts: 1.25 us -> 4.67 us  [the longest x2 2.93 us: flat_rows(): return rows.reshape(experts, CAP * rows.shape[1] // LANES, LANES)]
    another operation x2 -> x4, other arithmetic: 0.19 us -> 2.35 us  [canonical(): return jnp.stack(blocks)]
  transfers between devices with their start and end apart: 14 -> 21, of which waited for: 6 -> 7; matrix products, arithmetic and copies ran while one was open for 13% -> 19% of each run, Pallas kernels for 0% -> 0%
where the time goes in v1:
time: 110 us; the launch traced here: 109 us
  starting transfers between devices  38.5 us (35%)
  waiting for transfers between devices  35.5 us (32%)
  matrix products  16.4 us (15%)
  other arithmetic  9.05 us (8%)
  local copies, waits for them, and re-layouts  8.12 us (7%)
  between operations  1.66 us (2%)
    all_to_all x3, waiting for transfers between devices, exchanged(): lax.all_to_all(flat, 'expert', split_axis=0, concat_axis=0, tiled=True)  23.7 us
    ppermute x8, starting transfers between devices, spread(): blocks.append(lax.ppermute(chunk, ('dp', 'tensor'), self.pairs(step)))  14.8 us
    all_to_all x3, starting transfers between devices, exchanged(): lax.all_to_all(flat, 'expert', split_axis=0, concat_axis=0, tiled=True)  14.7 us
    dot_general x9, matrix products, dot(): return lax.dot_general(a, b, dims, preferred_element_type=F32)  12.3 us
    ppermute x1, waiting for transfers between devices, on_device(): units_moved = lax.ppermute(units_own, 'expert', partner)  6.28 us
    ppermute x4, starting transfers between devices, send_back(): got.append(lax.ppermute(block, ('dp', 'tensor'), route))  5.23 us
    ppermute x8, waiting for transfers between devices, spread(): blocks.append(lax.ppermute(chunk, ('dp', 'tensor'), self.pairs(step)))  3.41 us
    reshape x2, local copies, waits for them, and re-layouts, flat_rows(): return rows.reshape(experts, CAP * rows.shape[1] // LANES, LANES)  2.93 us
  transfers between devices with their start and end apart: 21, of which 7 were waited for; matrix products, arithmetic and copies ran while one was open for 19% of the time, Pallas kernels for 0%

profile of v1, /device:TPU:0, one launch (start us, length us, event | category | flops | bytes accessed | tf_op | source)
XLA Modules:
  0.0 109.2 jit_solution(8693004037888241933)
XLA Ops:
  0.7 1.0 fusion.58
  2.5 1.0 slice_convert_fusion.7
  3.7 1.3 %convolution_convert_fusion.7 = bf16[72,1792]{1,0:T(8,128)(2,1)S(1)} fusion(pred[192,72]{0,1:T(8,128)(4,1)S(1)} %fusion.15, bf16[192,1792]{1,0:T(8,128)(2,1)} %param.9), kind=kOutput, calls=%fused_computation.12 | convolution fusion | flops 49674240 | bytes 960000 | tf_op jit(solution)/shard_map/dot_general | solution.py:16
  5.1 1.4 %convolution_convert_fusion.6 = bf16[72,1792]{1,0:T(8,128)(2,1)S(1)} fusion(bf16[192,1792]{1,0:T(8,128)(2,1)} %param.12, pred[192,72]{0,1:T(8,128)(4,1)S(1)} %fusion.15, f32[192]{0:T(256)S(1)} %bitcast.147, f32[192]{0:T(256)S(1)} %bitcast.149, f32[192]{0:T(256)S(1)} %bitcast.137, f32[192]{0:T(256)S(1)} %bitcast.139, f32[192]{0:T(256)S(1)} %bitcast.141, ...), kind=kOutput, calls=%fused_computation.11 | convolution fusion | flops 50019840 | bytes 972576 | tf_op jit(solution)/shard_map/dot_general | solution.py:16
  6.6 1.5 %reshape.82 = bf16[8,252,128]{2,1,0:T(8,128)(2,1)} reshape(bf16[72,3584]{1,0:T(8,128)(2,1)S(1)} %pad_maximum_fusion) | data formatting | bytes 1032192 | tf_op jit(solution)/shard_map/reshape | solution.py:94
  8.0 7.4 %all-to-all-start = ((bf16[8,252,128]{2,1,0:T(8,128)(2,1)}), bf16[8,252,128]{2,1,0:T(8,128)(2,1)S(1)}, u32[]{:S(2)}, u32[]{:S(2)}) async-start(bf16[8,252,128]{2,1,0:T(8,128)(2,1)} %reshape.82), calls=%async_computation | async-start | bytes 1048576 | tf_op jit(solution)/shard_map/all_to_all | solution.py:98
  16.3 2.0 %maximum_select_fusion = bf16[8,252,128]{2,1,0:T(8,128)(2,1)} fusion(bf16[8,252,128]{2,1,0:T(8,128)(2,1)} %reshape.82, bf16[4,252,128]{2,1,0:T(8,128)(2,1)S(1)} %slice.132, bf16[4,252,128]{2,1,0:T(8,128)(2,1)S(1)} %slice.130, pred[8]{0:T(512)(128)(4,1)S(1)} %broadcast_compare_fusion), kind=kLoop, calls=%fused_computation.32 | loop fusion | flops 516096 | bytes 1548296 | tf_op jit(solution)/shard_map/jit(_where)/select_n | solution.py:138
  18.2 11.7 %all-to-all-done = bf16[8,252,128]{2,1,0:T(8,128)(2,1)S(1)} async-done(((bf16[8,252,128]{2,1,0:T(8,128)(2,1)}), bf16[8,252,128]{2,1,0:T(8,128)(2,1)S(1)}, u32[]{:S(2)}, u32[]{:S(2)}) %all-to-all-start) | async-done | bytes 516128 | tf_op jit(solution)/shard_map/all_to_all | solution.py:98
  29.9 3.6 %all-to-all-start.2 = ((bf16[8,252,128]{2,1,0:T(8,128)(2,1)}), bf16[8,252,128]{2,1,0:T(8,128)(2,1)S(1)}, u32[]{:S(2)}, u32[]{:S(2)}) async-start(bf16[8,252,128]{2,1,0:T(8,128)(2,1)} %maximum_select_fusion), calls=%async_computation.2 | async-start | bytes 1048576 | tf_op jit(solution)/shard_map/all_to_all | solution.py:98
  36.2 3.6 %collective-permute-start.6 = (bf16[72,1792]{1,0:T(8,128)(2,1)}, bf16[72,1792]{1,0:T(8,128)(2,1)}, u32[]{:S(2)}, u32[]{:S(2)}) collective-permute-start(bf16[72,1792]{1,0:T(8,128)(2,1)} %get-tuple-element.33), channel_id=1, source_target_pairs={{0,0},{2,1},{1,2},{3,3},{4,4},{6,5},{5,6},{7,7},{8,8},{10,9},{9,10... | collective-permute-start | bytes 774152 | tf_op jit(solution)/shard_map/ppermute | solution.py:52
  40.4 3.4 %collective-permute-start.1 = (bf16[72,1792]{1,0:T(8,128)(2,1)S(1)}, bf16[72,1792]{1,0:T(8,128)(2,1)}, u32[]{:S(2)}, u32[]{:S(2)}) collective-permute-start(bf16[72,1792]{1,0:T(8,128)(2,1)S(1)} %get-tuple-element.34), channel_id=1, source_target_pairs={{2,0},{0,1},{3,2},{1,3},{6,4},{4,5},{7,6},{5,7},{10,8},{8,9},{11,1... | collective-permute-start | bytes 774152 | tf_op jit(solution)/shard_map/ppermute | solution.py:52
  43.8 4.4 %all-to-all-done.2 = bf16[8,252,128]{2,1,0:T(8,128)(2,1)S(1)} async-done(((bf16[8,252,128]{2,1,0:T(8,128)(2,1)}), bf16[8,252,128]{2,1,0:T(8,128)(2,1)S(1)}, u32[]{:S(2)}, u32[]{:S(2)}) %all-to-all-start.2) | async-done | bytes 516128 | tf_op jit(solution)/shard_map/all_to_all | solution.py:98
  49.6 2.8 %collective-permute-start.17 = (bf16[72,1792]{1,0:T(8,128)(2,1)S(1)}, bf16[72,1792]{1,0:T(8,128)(2,1)S(1)}, u32[]{:S(2)}, u32[]{:S(2)}) collective-permute-start(bf16[72,1792]{1,0:T(8,128)(2,1)S(1)} %get-tuple-element.25), channel_id=1, source_target_pairs={{2,0},{0,1},{3,2},{1,3},{6,4},{4,5},{7,6},{5,7},{10,8},{8,9},{11,1... | collective-permute-start | bytes 774152 | tf_op jit(solution)/shard_map/ppermute | solution.py:52
  53.0 1.1 %pad_maximum_fusion.2 = bf16[2,72,1792]{2,1,0:T(8,128)(2,1)S(1)} fusion(bf16[1,72,1792]{2,1,0:T(8,128)(2,1)} %bitcast.23, bf16[1,72,1792]{2,1,0:T(8,128)(2,1)} %bitcast.22), kind=kLoop, calls=%fused_computation.34 | loop fusion | flops 258048 | bytes 1032192 | tf_op jit(solution)/shard_map/stack | solution.py:43
  54.6 3.0 %collective-permute-start.13 = (bf16[72,1792]{1,0:T(8,128)(2,1)S(1)}, bf16[72,1792]{1,0:T(8,128)(2,1)S(1)}, u32[]{:S(2)}, u32[]{:S(2)}) collective-permute-start(bf16[72,1792]{1,0:T(8,128)(2,1)S(1)} %get-tuple-element.26), channel_id=1, source_target_pairs={{2,0},{0,1},{3,2},{1,3},{6,4},{4,5},{7,6},{5,7},{10,8},{8,9},{11,1... | collective-permute-start | bytes 774152 | tf_op jit(solution)/shard_map/ppermute | solution.py:52
  57.6 1.1 %pad_maximum_fusion.1 = bf16[2,72,1792]{2,1,0:T(8,128)(2,1)S(1)} fusion(bf16[1,72,1792]{2,1,0:T(8,128)(2,1)} %bitcast.17, bf16[1,72,1792]{2,1,0:T(8,128)(2,1)S(1)} %bitcast.99), kind=kLoop, calls=%fused_computation.33 | loop fusion | flops 258048 | bytes 1032192 | tf_op jit(solution)/shard_map/stack | solution.py:43
  60.5 3.4 %collective-permute-done.13 = bf16[72,1792]{1,0:T(8,128)(2,1)S(1)} collective-permute-done((bf16[72,1792]{1,0:T(8,128)(2,1)S(1)}, bf16[72,1792]{1,0:T(8,128)(2,1)S(1)}, u32[]{:S(2)}, u32[]{:S(2)}) %collective-permute-start.13) | collective-permute-done | bytes 258080 | tf_op jit(solution)/shard_map/ppermute | solution.py:52
  65.8 1.6 %collective-permute-start.14 = (bf16[72,1536]{1,0:T(8,128)(2,1)S(1)}, bf16[72,1536]{1,0:T(8,128)(2,1)S(1)}, u32[]{:S(2)}, u32[]{:S(2)}) collective-permute-start(bf16[72,1536]{1,0:T(8,128)(2,1)S(1)} %dynamic-slice_bitcast_fusion), channel_id=1, source_target_pairs={{0,16},{4,20},{8,24},{12,28},{16,0},{20,4},{24,8},{28,12},{1,17},{... | collective-permute-start | bytes 663560 | tf_op jit(solution)/shard_map/ppermute | solution.py:192
  68.1 3.8 %collective-permute-start.5 = (bf16[72,1792]{1,0:T(8,128)(2,1)S(1)}, bf16[72,1792]{1,0:T(8,128)(2,1)S(1)}, u32[]{:S(2)}, u32[]{:S(2)}) collective-permute-start(bf16[72,1792]{1,0:T(8,128)(2,1)S(1)} %get-tuple-element.30), channel_id=1, source_target_pairs={{0,2},{1,0},{2,3},{3,1},{4,6},{5,4},{6,7},{7,5},{8,10},{9,8},{10,1... | collective-permute-start | bytes 774152 | tf_op jit(solution)/shard_map/ppermute | solution.py:63
  73.5 6.3 %collective-permute-done.14 = bf16[72,1536]{1,0:T(8,128)(2,1)S(1)} collective-permute-done((bf16[72,1536]{1,0:T(8,128)(2,1)S(1)}, bf16[72,1536]{1,0:T(8,128)(2,1)S(1)}, u32[]{:S(2)}, u32[]{:S(2)}) %collective-permute-start.14) | collective-permute-done | bytes 221216 | tf_op jit(solution)/shard_map/ppermute | solution.py:192
  80.6 1.1 %collective-permute-done.10 = bf16[72,1792]{1,0:T(8,128)(2,1)S(1)} collective-permute-done((bf16[72,1792]{1,0:T(8,128)(2,1)S(1)}, bf16[72,1792]{1,0:T(8,128)(2,1)S(1)}, u32[]{:S(2)}, u32[]{:S(2)}) %collective-permute-start.10) | collective-permute-done | bytes 258080 | tf_op jit(solution)/shard_map/ppermute | solution.py:63
  81.8 1.5 %reshape.86 = bf16[8,252,128]{2,1,0:T(8,128)(2,1)} reshape(bf16[72,3584]{1,0:T(8,128)(2,1)S(1)} %pad_maximum_fusion.3) | data formatting | bytes 1032192 | tf_op jit(solution)/shard_map/reshape | solution.py:94
  83.2 3.7 %all-to-all-start.1 = ((bf16[8,252,128]{2,1,0:T(8,128)(2,1)}), bf16[8,252,128]{2,1,0:T(8,128)(2,1)S(1)}, u32[]{:S(2)}, u32[]{:S(2)}) async-start(bf16[8,252,128]{2,1,0:T(8,128)(2,1)} %reshape.86), calls=%async_computation.1 | async-start | bytes 1048576 | tf_op jit(solution)/shard_map/all_to_all | solution.py:98
  86.9 1.1 select_bitcast_fusion.1
  88.1 1.9 %fusion.1 = bf16[1,1792,512]{2,1,0:T(8,128)(2,1)} fusion(bf16[144,1792]{1,0:T(8,128)(2,1)S(1)} %bitcast.87, bf16[144,1536]{1,0:T(8,128)(2,1)S(1)} %bitcast.93), kind=kOutput, calls=%fused_computation.4 | convolution fusion | flops 265158656 | bytes 2498560 | tf_op jit(solution)/shard_map/dot_general | solution.py:16
  90.0 1.9 %fusion = bf16[1,1792,512]{2,1,0:T(8,128)(2,1)} fusion(bf16[144,1792]{1,0:T(8,128)(2,1)S(1)} %bitcast.88, bf16[144,1536]{1,0:T(8,128)(2,1)S(1)} %bitcast.94), kind=kOutput, calls=%fused_computation.3 | convolution fusion | flops 265158656 | bytes 2498560 | tf_op jit(solution)/shard_map/dot_general | solution.py:16
  91.9 1.9 %fusion.2 = bf16[1,1792,512]{2,1,0:T(8,128)(2,1)} fusion(bf16[144,1792]{1,0:T(8,128)(2,1)S(1)} %bitcast.91, bf16[144,1536]{1,0:T(8,128)(2,1)S(1)} %bitcast.95), kind=kOutput, calls=%fused_computation.5 | convolution fusion | flops 265158656 | bytes 2498560 | tf_op jit(solution)/shard_map/dot_general | solution.py:16
  93.8 7.6 %all-to-all-done.1 = bf16[8,252,128]{2,1,0:T(8,128)(2,1)S(1)} async-done(((bf16[8,252,128]{2,1,0:T(8,128)(2,1)}), bf16[8,252,128]{2,1,0:T(8,128)(2,1)S(1)}, u32[]{:S(2)}, u32[]{:S(2)}) %all-to-all-start.1) | async-done | bytes 516128 | tf_op jit(solution)/shard_map/all_to_all | solution.py:98
  102.0 1.6 %fusion.40 = (f32[192]{0:T(256)S(1)}, f32[192]{0:T(256)S(1)}, f32[192]{0:T(256)S(1)}, f32[192]{0:T(256)S(1)}, f32[192]{0:T(256)S(1)}, /*index=5*/f32[192]{0:T(256)S(1)}, f32[192]{0:T(256)S(1)}, f32[192]{0:T(256)S(1)}) fusion(s32[192]{0:T(256)S(1)} %bitcast.129, s32[72]{0:T(128)S(1)} %eq.135, s32[192]{0:T(256)S(1)} %bitcast.133, s32[192]{0:T(256)S(1)} %bitcast.109, ...), kind=kOutput, calls=%fused_computation.98 | convolution fusion | flops 49889280 | bytes 979456 | tf_op jit(solution)/shard_map/dot_general | solution.py:16
  103.5 1.4 %convolution_convert_fusion.4 = bf16[192,1792]{1,0:T(8,128)(2,1)} fusion(bf16[72,3584]{1,0:T(8,128)(2,1)S(1)} %reshape.87, pred[192,72]{0,1:T(8,128)(4,1)S(1)} %fusion.15, f32[192]{0:T(256)S(1)} %bitcast.148, f32[192]{0:T(256)S(1)} %bitcast.150, f32[192]{0:T(256)S(1)} %bitcast.138, f32[192]{0:T(256)S(1)} %bitcast.140, f32[192]{0:T(256)S(1)} %bitcast.142, ...), kind=kOutput, calls=%fused_computation.8 | convolution fusion | flops 50234880 | bytes 981504 | tf_op jit(solution)/shard_map/dot_general | solution.py:186
  104.9 1.5 %collective-permute-start.11 = (f32[8,192]{1,0:T(8,128)S(1)}, f32[8,192]{1,0:T(8,128)S(1)}, u32[]{:S(2)}, u32[]{:S(2)}) collective-permute-start(f32[8,192]{1,0:T(8,128)S(1)} %stack.86), channel_id=1, source_target_pairs={{0,1},{1,0},{2,3},{3,2},{4,5},{5,4},{6,7},{7,6},{8,9},{9,8},{10,11... | collective-permute-start | bytes 18440 | tf_op jit(solution)/shard_map/ppermute | solution.py:181
  106.4 1.2 %convolution_convert_fusion.3 = bf16[192,1792]{1,0:T(8,128)(2,1)} fusion(pred[192,72]{0,1:T(8,128)(4,1)S(1)} %fusion.15, bf16[72,3584]{1,0:T(8,128)(2,1)S(1)} %reshape.87), kind=kOutput, calls=%fused_computation.7 | convolution fusion | flops 49889280 | bytes 964608 | tf_op jit(solution)/shard_map/dot_general | solution.py:187
  (70 shorter events, 15.8 us)
Async XLA Ops:
  0.6 53.5 %copy-start = (bf16[1,1792,512]{2,1,0:T(8,128)(2,1)S(1)}, bf16[1,1792,512]{2,1,0:T(8,128)(2,1)}, u32[]{:S(2)}) copy-start(bf16[1,1792,512]{2,1,0:T(8,128)(2,1)} %param.17) | copy-start | bytes 5505028
  8.0 8.2 %copy-start.3 = (s32[8]{0:T(128)S(1)}, s32[8]{0:T(128)}, u32[]{:S(2)}) copy-start(s32[8]{0:T(128)} %param.14) | copy-start | bytes 100
  8.0 21.9 %all-to-all-start = ((bf16[8,252,128]{2,1,0:T(8,128)(2,1)}), bf16[8,252,128]{2,1,0:T(8,128)(2,1)S(1)}, u32[]{:S(2)}, u32[]{:S(2)}) async-start(bf16[8,252,128]{2,1,0:T(8,128)(2,1)} %reshape.82), calls=%async_computation | async-start | bytes 1048576 | tf_op jit(solution)/shard_map/all_to_all | solution.py:98
  29.9 18.3 %all-to-all-start.2 = ((bf16[8,252,128]{2,1,0:T(8,128)(2,1)}), bf16[8,252,128]{2,1,0:T(8,128)(2,1)S(1)}, u32[]{:S(2)}, u32[]{:S(2)}) async-start(bf16[8,252,128]{2,1,0:T(8,128)(2,1)} %maximum_select_fusion), calls=%async_computation.2 | async-start | bytes 1048576 | tf_op jit(solution)/shard_map/all_to_all | solution.py:98
  36.2 13.4 %collective-permute-start.6 = (bf16[72,1792]{1,0:T(8,128)(2,1)}, bf16[72,1792]{1,0:T(8,128)(2,1)}, u32[]{:S(2)}, u32[]{:S(2)}) collective-permute-start(bf16[72,1792]{1,0:T(8,128)(2,1)} %get-tuple-element.33), channel_id=1, source_target_pairs={{0,0},{2,1},{1,2},{3,3},{4,4},{6,5},{5,6},{7,7},{8,8},{10,9},{9,10... | collective-permute-start | bytes 774152 | tf_op jit(solution)/shard_map/ppermute | solution.py:52
  39.8 12.6 %collective-permute-start.7 = (bf16[72,1792]{1,0:T(8,128)(2,1)}, bf16[72,1792]{1,0:T(8,128)(2,1)}, u32[]{:S(2)}, u32[]{:S(2)}) collective-permute-start(bf16[72,1792]{1,0:T(8,128)(2,1)} %get-tuple-element.33), channel_id=1, source_target_pairs={{2,0},{0,1},{3,2},{1,3},{6,4},{4,5},{7,6},{5,7},{10,8},{8,9},{11,1... | collective-permute-start | bytes 774152 | tf_op jit(solution)/shard_map/ppermute | solution.py:52
  39.8 14.8 %collective-permute-start = (bf16[72,1792]{1,0:T(8,128)(2,1)S(1)}, bf16[72,1792]{1,0:T(8,128)(2,1)S(1)}, u32[]{:S(2)}, u32[]{:S(2)}) collective-permute-start(bf16[72,1792]{1,0:T(8,128)(2,1)S(1)} %get-tuple-element.34), channel_id=1, source_target_pairs={{0,0},{2,1},{1,2},{3,3},{4,4},{6,5},{5,6},{7,7},{8,8},{10,9},{9,10... | collective-permute-start | bytes 774152 | tf_op jit(solution)/shard_map/ppermute | solution.py:52
  40.4 17.2 %collective-permute-start.1 = (bf16[72,1792]{1,0:T(8,128)(2,1)S(1)}, bf16[72,1792]{1,0:T(8,128)(2,1)}, u32[]{:S(2)}, u32[]{:S(2)}) collective-permute-start(bf16[72,1792]{1,0:T(8,128)(2,1)S(1)} %get-tuple-element.34), channel_id=1, source_target_pairs={{2,0},{0,1},{3,2},{1,3},{6,4},{4,5},{7,6},{5,7},{10,8},{8,9},{11,1... | collective-permute-start | bytes 774152 | tf_op jit(solution)/shard_map/ppermute | solution.py:52
  48.9 10.8 %collective-permute-start.16 = (bf16[72,1792]{1,0:T(8,128)(2,1)S(1)}, bf16[72,1792]{1,0:T(8,128)(2,1)S(1)}, u32[]{:S(2)}, u32[]{:S(2)}) collective-permute-start(bf16[72,1792]{1,0:T(8,128)(2,1)S(1)} %get-tuple-element.25), channel_id=1, source_target_pairs={{0,0},{2,1},{1,2},{3,3},{4,4},{6,5},{5,6},{7,7},{8,8},{10,9},{9,10... | collective-permute-start | bytes 774152 | tf_op jit(solution)/shard_map/ppermute | solution.py:52
  49.6 10.7 %collective-permute-start.17 = (bf16[72,1792]{1,0:T(8,128)(2,1)S(1)}, bf16[72,1792]{1,0:T(8,128)(2,1)S(1)}, u32[]{:S(2)}, u32[]{:S(2)}) collective-permute-start(bf16[72,1792]{1,0:T(8,128)(2,1)S(1)} %get-tuple-element.25), channel_id=1, source_target_pairs={{2,0},{0,1},{3,2},{1,3},{6,4},{4,5},{7,6},{5,7},{10,8},{8,9},{11,1... | collective-permute-start | bytes 774152 | tf_op jit(solution)/shard_map/ppermute | solution.py:52
  52.4 8.1 %collective-permute-start.12 = (bf16[72,1792]{1,0:T(8,128)(2,1)S(1)}, bf16[72,1792]{1,0:T(8,128)(2,1)S(1)}, u32[]{:S(2)}, u32[]{:S(2)}) collective-permute-start(bf16[72,1792]{1,0:T(8,128)(2,1)S(1)} %get-tuple-element.26), channel_id=1, source_target_pairs={{0,0},{2,1},{1,2},{3,3},{4,4},{6,5},{5,6},{7,7},{8,8},{10,9},{9,10... | collective-permute-start | bytes 774152 | tf_op jit(solution)/shard_map/ppermute | solution.py:52
  54.2 4.6 %copy-start.2 = (bf16[1,1792,512]{2,1,0:T(8,128)(2,1)S(1)}, bf16[1,1792,512]{2,1,0:T(8,128)(2,1)}, u32[]{:S(2)}) copy-start(bf16[1,1792,512]{2,1,0:T(8,128)(2,1)} %param.15) | copy-start | bytes 5505028
  54.6 9.2 %collective-permute-start.13 = (bf16[72,1792]{1,0:T(8,128)(2,1)S(1)}, bf16[72,1792]{1,0:T(8,128)(2,1)S(1)}, u32[]{:S(2)}, u32[]{:S(2)}) collective-permute-start(bf16[72,1792]{1,0:T(8,128)(2,1)S(1)} %get-tuple-element.26), channel_id=1, source_target_pairs={{2,0},{0,1},{3,2},{1,3},{6,4},{4,5},{7,6},{5,7},{10,8},{8,9},{11,1... | collective-permute-start | bytes 774152 | tf_op jit(solution)/shard_map/ppermute | solution.py:52
  57.6 7.2 %collective-permute-start.8 = (f32[144,512]{1,0:T(8,128)S(1)}, f32[144,512]{1,0:T(8,128)S(1)}, u32[]{:S(2)}, u32[]{:S(2)}) collective-permute-start(f32[144,512]{1,0:T(8,128)S(1)} %fusion.4), channel_id=1, source_target_pairs={{0,2},{2,0},{1,3},{3,1},{4,6},{6,4},{5,7},{7,5},{8,10},{10,8},{9,1... | collective-permute-start | bytes 884744 | tf_op jit(solution)/shard_map/ppermute | solution.py:81
  57.6 1.6 %copy-start.1 = (bf16[1,1792,512]{2,1,0:T(8,128)(2,1)S(1)}, bf16[1,1792,512]{2,1,0:T(8,128)(2,1)}, u32[]{:S(2)}) copy-start(bf16[1,1792,512]{2,1,0:T(8,128)(2,1)} %param.16) | copy-start | bytes 5505028
  59.7 4.2 %collective-permute-start.2 = (f32[144,512]{1,0:T(8,128)S(1)}, f32[144,512]{1,0:T(8,128)S(1)}, u32[]{:S(2)}, u32[]{:S(2)}) collective-permute-start(f32[144,512]{1,0:T(8,128)S(1)} %fusion.12), channel_id=1, source_target_pairs={{0,2},{2,0},{1,3},{3,1},{4,6},{6,4},{5,7},{7,5},{8,10},{10,8},{9,1... | collective-permute-start | bytes 884744 | tf_op jit(solution)/shard_map/ppermute | solution.py:81
  60.3 3.6 %collective-permute-start.3 = (f32[144,512]{1,0:T(8,128)S(1)}, f32[144,512]{1,0:T(8,128)S(1)}, u32[]{:S(2)}, u32[]{:S(2)}) collective-permute-start(f32[144,512]{1,0:T(8,128)S(1)} %fusion.8), channel_id=1, source_target_pairs={{0,2},{2,0},{1,3},{3,1},{4,6},{6,4},{5,7},{7,5},{8,10},{10,8},{9,1... | collective-permute-start | bytes 884744 | tf_op jit(solution)/shard_map/ppermute | solution.py:81
  65.8 13.9 %collective-permute-start.14 = (bf16[72,1536]{1,0:T(8,128)(2,1)S(1)}, bf16[72,1536]{1,0:T(8,128)(2,1)S(1)}, u32[]{:S(2)}, u32[]{:S(2)}) collective-permute-start(bf16[72,1536]{1,0:T(8,128)(2,1)S(1)} %dynamic-slice_bitcast_fusion), channel_id=1, source_target_pairs={{0,16},{4,20},{8,24},{12,28},{16,0},{20,4},{24,8},{28,12},{1,17},{... | collective-permute-start | bytes 663560 | tf_op jit(solution)/shard_map/ppermute | solution.py:192
  67.4 13.0 %collective-permute-start.4 = (bf16[72,1792]{1,0:T(8,128)(2,1)S(1)}, bf16[72,1792]{1,0:T(8,128)(2,1)S(1)}, u32[]{:S(2)}, u32[]{:S(2)}) collective-permute-start(bf16[72,1792]{1,0:T(8,128)(2,1)S(1)} %get-tuple-element.29), channel_id=1, source_target_pairs={{0,0},{1,2},{2,1},{3,3},{4,4},{5,6},{6,5},{7,7},{8,8},{9,10},{10,9... | collective-permute-start | bytes 774152 | tf_op jit(solution)/shard_map/ppermute | solution.py:63
  68.1 12.4 %collective-permute-start.5 = (bf16[72,1792]{1,0:T(8,128)(2,1)S(1)}, bf16[72,1792]{1,0:T(8,128)(2,1)S(1)}, u32[]{:S(2)}, u32[]{:S(2)}) collective-permute-start(bf16[72,1792]{1,0:T(8,128)(2,1)S(1)} %get-tuple-element.30), channel_id=1, source_target_pairs={{0,2},{1,0},{2,3},{3,1},{4,6},{5,4},{6,7},{7,5},{8,10},{9,8},{10,1... | collective-permute-start | bytes 774152 | tf_op jit(solution)/shard_map/ppermute | solution.py:63
  72.8 8.9 %collective-permute-start.10 = (bf16[72,1792]{1,0:T(8,128)(2,1)S(1)}, bf16[72,1792]{1,0:T(8,128)(2,1)S(1)}, u32[]{:S(2)}, u32[]{:S(2)}) collective-permute-start(bf16[72,1792]{1,0:T(8,128)(2,1)S(1)} %get-tuple-element.32), channel_id=1, source_target_pairs={{0,2},{1,0},{2,3},{3,1},{4,6},{5,4},{6,7},{7,5},{8,10},{9,8},{10,1... | collective-permute-start | bytes 774152 | tf_op jit(solution)/shard_map/ppermute | solution.py:63
  72.8 8.9 %collective-permute-start.9 = (bf16[72,1792]{1,0:T(8,128)(2,1)S(1)}, bf16[72,1792]{1,0:T(8,128)(2,1)S(1)}, u32[]{:S(2)}, u32[]{:S(2)}) collective-permute-start(bf16[72,1792]{1,0:T(8,128)(2,1)S(1)} %get-tuple-element.31), channel_id=1, source_target_pairs={{0,0},{1,2},{2,1},{3,3},{4,4},{5,6},{6,5},{7,7},{8,8},{9,10},{10,9... | collective-permute-start | bytes 774152 | tf_op jit(solution)/shard_map/ppermute | solution.py:63
  80.5 6.5 %collective-permute-start.15 = (bf16[72,1536]{1,0:T(8,128)(2,1)}, bf16[72,1536]{1,0:T(8,128)(2,1)}, u32[]{:S(2)}, u32[]{:S(2)}) collective-permute-start(bf16[72,1536]{1,0:T(8,128)(2,1)} %broadcast_select_fusion), channel_id=1, source_target_pairs={{0,2},{2,0},{1,3},{3,1},{4,6},{6,4},{5,7},{7,5},{8,10},{10,8},{9,1... | collective-permute-start | bytes 663560 | tf_op jit(solution)/shard_map/ppermute | solution.py:87
  83.2 18.1 %all-to-all-start.1 = ((bf16[8,252,128]{2,1,0:T(8,128)(2,1)}), bf16[8,252,128]{2,1,0:T(8,128)(2,1)S(1)}, u32[]{:S(2)}, u32[]{:S(2)}) async-start(bf16[8,252,128]{2,1,0:T(8,128)(2,1)} %reshape.86), calls=%async_computation.1 | async-start | bytes 1048576 | tf_op jit(solution)/shard_map/all_to_all | solution.py:98
  104.9 3.7 %collective-permute-start.11 = (f32[8,192]{1,0:T(8,128)S(1)}, f32[8,192]{1,0:T(8,128)S(1)}, u32[]{:S(2)}, u32[]{:S(2)}) collective-permute-start(f32[8,192]{1,0:T(8,128)S(1)} %stack.86), channel_id=1, source_target_pairs={{0,1},{1,0},{2,3},{3,2},{4,5},{5,4},{6,7},{7,6},{8,9},{9,8},{10,11... | collective-permute-start | bytes 18440 | tf_op jit(solution)/shard_map/ppermute | solution.py:181

commit v2 on v1

v2 whole, which is shorter than its diff:
```python
import jax
import jax.numpy as jnp
from jax import lax
from jax.experimental import pallas as pl
from jax.experimental.pallas import tpu as pltpu
from jax.sharding import PartitionSpec as P

CAP = 9
BF = jnp.bfloat16
F32 = jnp.float32
LANES = 128

ROWS_AT_ONCE = 320
contract = (((0,), (0,)), ((), ()))
inner = (((1,), (1,)), ((), ()))


def dot(a, b, dims):
    return lax.dot_general(a, b, dims, preferred_element_type=F32)


def pick(stack, index, count):
    return stack[0] if count == 1 else lax.dynamic_index_in_dim(stack, index, 0, keepdims=False)


class Layout:
    def __init__(self):
        self.n_d = lax.axis_size("dp")
        self.n_t = lax.axis_size("tensor")
        self.group = self.n_d // self.n_t
        self.d = lax.axis_index("dp")
        self.t = lax.axis_index("tensor")
        self.order = (self.d % self.group) * self.n_t + self.t

    def pairs(self, step):
        route = []
        for d in range(self.n_d):
            for t in range(self.n_t):
                half = d // self.group
                data = ((d % self.group) * self.n_t + t + step) % self.n_d
                route.append((data * self.n_t + half, d * self.n_t + t))
        return route

    def canonical(self, blocks):
        if self.group == 1:
            return blocks
        whole = jnp.stack(blocks)
        whole = jnp.take(whole, (jnp.arange(self.n_d) - self.order) % self.n_d, axis=0)
        return [whole[i] for i in range(self.n_d)]

    def spread(self, rows):
        blocks = []
        for step in range(self.n_d):
            target = (self.d - step) % self.n_d
            chunk = pick(rows, target // self.n_t, self.group)
            blocks.append(lax.ppermute(chunk, ("dp", "tensor"), self.pairs(step)))
        return self.canonical(blocks)

    def send_back(self, blocks):
        got = []
        for step in range(self.n_d):
            if self.group == 1:
                block = blocks[step]
            else:
                block = pick(jnp.stack(blocks), (self.order + step) % self.n_d, self.n_d)
            route = [(b, a) for a, b in self.pairs(step)]
            got.append(lax.ppermute(block, ("dp", "tensor"), route))
        return got

    def add_up(self, got):
        total = None
        for step, block in enumerate(got):
            part = block.astype(F32)[None]
            if self.group > 1:
                place = ((self.d - step) % self.n_d) // self.n_t
                mask = jnp.arange(self.group) == place
                part = jnp.where(mask[:, None, None], part, 0.0)
            total = part if total is None else total + part
        return total.astype(BF)

    def others(self, value):
        got = []
        for step in range(1, self.n_d):
            route = [(i, (i + step) % self.n_d) for i in range(self.n_d)]
            got.append(lax.ppermute(value, "dp", route))
        return got

    def gathered(self, value):
        if self.n_d == 2:
            other = lax.ppermute(value, "dp", [(0, 1), (1, 0)])
            first = self.d == 0
            return jnp.concatenate([jnp.where(first, value, other), jnp.where(first, other, value)])
        return lax.all_gather(value, "dp", axis=0, tiled=True)


def exchanged(rows, experts):
    cols = rows.shape[1]
    flat = rows.reshape(experts, CAP * cols // LANES, LANES)
    got = lax.all_to_all(flat, "expert", split_axis=0, concat_axis=0, tiled=True)
    return got.reshape(experts * CAP, cols)


def call(kernel, outs, args, room, smem=0, flops=0):
    vmem = pl.BlockSpec(memory_space=pltpu.VMEM)
    moved = sum(a.size * a.dtype.itemsize for a in args) + sum(
        o.size * o.dtype.itemsize for o in outs
    )
    return pl.pallas_call(
        kernel,
        out_shape=outs,
        in_specs=[pl.BlockSpec(memory_space=pltpu.SMEM)] * smem + [vmem] * (len(args) - smem),
        out_specs=[vmem] * len(outs),
        compiler_params=pltpu.CompilerParams(vmem_limit_bytes=room),
        cost_estimate=pl.CostEstimate(flops=flops, bytes_accessed=moved, transcendentals=0),
    )(*args)


def room_for(*arrays):
    return (6 << 20) + 3 * sum(a.size * a.dtype.itemsize for a in arrays) // 2


def shape(dims, dtype):
    return jax.ShapeDtypeStruct(dims, dtype)


def wanted_column(placement, slots):
    row = lax.broadcasted_iota(jnp.int32, (slots, 1), 0)
    wanted = jnp.zeros((slots, 1), jnp.int32)
    base = jnp.zeros((slots, 1), jnp.int32)
    for e in range(slots // CAP):
        inside = row >= e * CAP
        wanted = jnp.where(inside, placement[e], wanted)
        base = jnp.where(inside, e * CAP, base)
    return wanted, row - base


def head_kernel(placement, routes, gates, tokens, cot, rows, select, weighted):
    slots, tok_count = select.shape
    top_count = routes.shape[0]
    half = tokens.shape[1]
    wanted, slot = wanted_column(placement, slots)
    hit = jnp.zeros((slots, tok_count), F32)
    weight = jnp.zeros((slots, tok_count), F32)
    for k in range(top_count):
        match = routes[k : k + 1, :] == wanted
        hit = jnp.where(match, 1.0, hit)
        weight = jnp.where(match, gates[k : k + 1, :].astype(F32), weight)
    row_id = lax.broadcasted_iota(jnp.int32, (tok_count, tok_count), 0)
    col_id = lax.broadcasted_iota(jnp.int32, (tok_count, tok_count), 1)
    before = jnp.where(row_id < col_id, 1.0, 0.0).astype(BF)
    earlier = jnp.dot(hit.astype(BF), before, preferred_element_type=F32)
    live = (hit > 0.0) & (earlier == slot.astype(F32))
    chosen = jnp.where(live, 1.0, 0.0).astype(BF)
    scaled = jnp.where(live, weight, 0.0).astype(BF)
    select[...] = chosen
    weighted[...] = scaled
    rows[:, :half] = jnp.dot(chosen, tokens[...], preferred_element_type=F32).astype(BF)
    rows[:, half:] = jnp.dot(scaled, cot[...], preferred_element_type=F32).astype(BF)


def first_kernel(xd, wg, wu, wd, terms):
    chunk, units = wg.shape
    x, d = xd[:, :chunk], xd[:, chunk:]
    terms[:, :units] = jnp.dot(x, wg[...], preferred_element_type=F32)
    terms[:, units : 2 * units] = jnp.dot(x, wu[...], preferred_element_type=F32)
    terms[:, 2 * units :] = jnp.dot(d, wd[...], preferred_element_type=F32)


def middle_kernel(count, *refs):
    parts, (wg, wu, wd) = refs[:count], refs[count : count + 3]
    units_out, results = refs[count + 3], refs[count + 4 :]
    chunk, units = wg.shape
    blocks, rows = units_out.shape[:2]
    at_once = blocks if blocks * rows <= ROWS_AT_ONCE else 1
    for first in range(0, blocks, at_once):
        span = pl.ds(first * rows, at_once * rows)

        def total(which):
            cols = pl.ds(which * units, units)
            value = parts[0][span, cols]
            for part in parts[1:]:
                value = value + part[span, cols]
            return value

        gate, up, d_hidden = total(0), total(1), total(2)
        sig = jax.nn.sigmoid(gate)
        hidden = (gate * sig * up).astype(BF)
        d_gate = (d_hidden * up * sig * (1.0 + gate * (1.0 - sig))).astype(BF)
        d_up = (d_hidden * gate * sig).astype(BF)
        out = dot(hidden, wd[...], inner)
        back = dot(d_gate, wg[...], inner) + dot(d_up, wu[...], inner)
        for j in range(at_once):
            part = slice(j * rows, (j + 1) * rows)
            results[first + j][:, :chunk] = out[part].astype(BF)
            results[first + j][:, chunk:] = back[part].astype(BF)
            units_out[first + j, :, :units] = d_gate.astype(F32)[part].astype(BF)
            units_out[first + j, :, units : 2 * units] = d_up.astype(F32)[part].astype(BF)
            units_out[first + j, :, 2 * units :] = hidden.astype(F32)[part].astype(BF)


def gate_kernel(placement, routes, select, cot, back, gate_part):
    slots = select.shape[0]
    half = cot.shape[1]
    wanted, _ = wanted_column(placement, slots)
    scores = dot(back[:, :half], cot[...], inner)
    scores = jnp.where(select[...].astype(F32) > 0.0, scores, 0.0)
    for k in range(routes.shape[0]):
        match = routes[k : k + 1, :] == wanted
        gate_part[k : k + 1, :] = jnp.sum(
            jnp.where(match, scores, 0.0), axis=0, keepdims=True
        )


def combine_kernel(select, weighted, back, layer_out, input_grad):
    half = layer_out.shape[1]
    layer_out[...] = dot(weighted[...], back[:, :half], contract).astype(BF)
    input_grad[...] = dot(select[...], back[:, half:], contract).astype(BF)


def grads_kernel(x, d, units_ref, g_gate, g_up, g_down):
    units = g_gate.shape[1]
    both = dot(x[...], units_ref[:, : 2 * units], contract).astype(BF)
    g_gate[...] = both[:, :units]
    g_up[...] = both[:, units:]
    g_down[...] = dot(d[...], units_ref[:, 2 * units :], contract).astype(BF)


def weight_grads(held, units_held, chunk, units):
    rows = held.shape[0]
    block = 256 if chunk % 256 == 0 else LANES
    steps = chunk // block
    out = shape((chunk, units), BF)
    spec = pl.BlockSpec((block, units), lambda i: (i, 0))
    return pl.pallas_call(
        grads_kernel,
        grid=(steps,),
        out_shape=[out] * 3,
        in_specs=[
            pl.BlockSpec((rows, block), lambda i: (0, i)),
            pl.BlockSpec((rows, block), lambda i: (0, i + steps)),
            pl.BlockSpec((rows, 3 * units), lambda i: (0, 0)),
        ],
        out_specs=[spec] * 3,
        compiler_params=pltpu.CompilerParams(
            vmem_limit_bytes=(6 << 20) + 3 * rows * 2 * (3 * units + 2 * block)
        ),
        cost_estimate=pl.CostEstimate(
            flops=6 * rows * chunk * units, bytes_accessed=6 * chunk * units, transcendentals=0
        ),
        name="weight_grads",
    )(held, held, units_held)


def on_device(tokens, routes, gates, cotangent, placement, swap_flag, w_gate, w_up, w_down):
    experts = lax.axis_size("expert")
    myself = lax.axis_index("expert")
    lay = Layout()
    places = jnp.arange(experts, dtype=jnp.int32)
    my_flag = jnp.sum(jnp.where(places == myself, swap_flag, 0)) == 1
    wg, wu, wd = w_gate[0], w_up[0], w_down[0]
    chunk, units = wg.shape
    tok_count, top_count = routes.shape
    slots_all = experts * CAP
    rows_all = lay.n_d * slots_all
    half_width = tokens.shape[1]
    routes_t, gates_t = routes.T, gates.T

    outs = [
        shape((slots_all, 2 * half_width), BF),
        shape((slots_all, tok_count), BF),
        shape((slots_all, tok_count), BF),
    ]
    outgoing, select, weighted = call(
        head_kernel,
        outs,
        (placement, routes_t, gates_t, tokens, cotangent),
        room_for(tokens, cotangent, *outs),
        smem=1,
    )
    arrived = exchanged(outgoing, experts)

    def spread(rows):
        if lay.group == 1:
            pieces = rows[None]
        else:
            both = rows.reshape(slots_all, 2, lay.group, chunk)
            pieces = jnp.moveaxis(both, 2, 0).reshape(lay.group, slots_all, 2 * chunk)
        return jnp.concatenate(lay.spread(pieces), axis=0)

    xd = spread(arrived)
    partial_sums = shape((rows_all, 3 * units), F32)
    (own_terms,) = call(
        first_kernel,
        [partial_sums],
        (xd, wg, wu, wd),
        room_for(xd, wg, wu, wd, partial_sums),
        flops=6 * rows_all * chunk * units,
    )
    parts = [own_terms, *lay.others(own_terms)]
    outs = [shape((lay.n_d, slots_all, 3 * units), BF)]
    outs += [shape((slots_all, 2 * chunk), BF)] * lay.n_d
    units_all, *results = call(
        lambda *refs: middle_kernel(lay.n_d, *refs),
        outs,
        (*parts, wg, wu, wd),
        room_for(*parts, wg, wu, wd, *outs),
        flops=6 * rows_all * chunk * units,
    )
    sums = lay.add_up(lay.send_back(results))
    if lay.group == 1:
        home = sums[0]
    else:
        home = jnp.moveaxis(sums.reshape(lay.group, slots_all, 2, chunk), 0, 2)
        home = home.reshape(slots_all, 2 * half_width)
    back = exchanged(home, experts)

    gate_shape = shape((top_count, tok_count), F32)
    (gate_part,) = call(
        gate_kernel,
        [gate_shape],
        (placement, routes_t, select, cotangent, back),
        room_for(cotangent, back),
        smem=1,
    )
    gate_grad = gate_part
    for step in range(1, lay.n_t):
        other = lax.ppermute(
            gate_part, "tensor", [(i, (i + step) % lay.n_t) for i in range(lay.n_t)]
        )
        gate_grad = gate_grad + other
    gate_grad = gate_grad.T
    outs = [shape(tokens.shape, BF)] * 2
    layer_out, input_grad = call(
        combine_kernel, outs, (select, weighted, back), room_for(back, *outs)
    )

    partner = [(i, (i + experts // 2) % experts) for i in range(experts)]
    moved = lax.ppermute(arrived, "expert", partner)
    held = spread(jnp.where(my_flag, moved, arrived))
    units_own = pick(units_all, lay.d, lay.n_d)
    units_moved = lax.ppermute(units_own, "expert", partner)
    units_held = jnp.where(my_flag, units_moved, units_own)
    units_held = lay.gathered(units_held)
    grads = weight_grads(held, units_held, chunk, units)
    return (layer_out, input_grad, gate_grad, grads[0][None], grads[1][None], grads[2][None])


def solution(mesh):
    placed = (
        P(("expert", "dp"), "tensor"),
        P(("expert", "dp"), None),
        P(("expert", "dp"), None),
        P(("expert", "dp"), "tensor"),
        P(),
        P(),
        P("expert", "dp", "tensor"),
        P("expert", "dp", "tensor"),
        P("expert", "dp", "tensor"),
    )


    return jax.shard_map(
        on_device,
        mesh=mesh,
        in_specs=placed,
        out_specs=(
            P(("expert", "dp"), "tensor"),
            P(("expert", "dp"), "tensor"),
            P(("expert", "dp"), None),
            P("expert", "dp", "tensor"),
            P("expert", "dp", "tensor"),
            P("expert", "dp", "tensor"),
        ),
        check_vma=False,
    )
```

time: 110 us -> 115 us (1.045)
  blocking collectives: 0 us -> 21.7 us
  starting transfers between devices: 38.5 us -> 20.3 us
  matrix products: 16.4 us -> 0 us
  Pallas kernels: 0 us -> 12.4 us
  waiting for transfers between devices: 35.5 us -> 42.3 us
  other arithmetic: 9.05 us -> 3.9 us
  local copies, waits for them, and re-layouts: 8.12 us -> 12.1 us
    all_to_all x0 -> x1, blocking collectives: none -> 21.7 us  [exchanged(): lax.all_to_all(flat, 'expert', split_axis=0, concat_axis=0, tiled=True)]
    ppermute x3 -> x2, waiting for transfers between devices: 0.01 us -> 17 us  [the longest x1 17 us: on_device(): moved = lax.ppermute(arrived, 'expert', partner)]
    dot_general x15 -> x0, matrix products: 16.4 us -> none  [the longest x9 12.3 us: dot(): return lax.dot_general(a, b, dims, preferred_element_type=F32)]
    all_to_all x3 -> x1, waiting for transfers between devices: 23.7 us -> 7.66 us  [exchanged(): lax.all_to_all(flat, 'expert', split_axis=0, concat_axis=0, tiled=True)]
    ppermute x8 -> x4, waiting for transfers between devices: 3.41 us -> 17.7 us  [spread(): blocks.append(lax.ppermute(chunk, ('dp', 'tensor'), self.pairs(step)))]
    pallas_call x0 -> x6, Pallas kernels: none -> 12.4 us  [the longest x5 7.52 us: call(): pl.pallas_call(kernel, out_shape=outs, in_specs=[pl.BlockSpec(memory_spac...]
    all_to_all x3 -> x1, starting transfers between devices: 14.7 us -> 3.49 us  [exchanged(): lax.all_to_all(flat, 'expert', split_axis=0, concat_axis=0, tiled=True)]
    unnamed x8 -> x32, local copies, waits for them, and re-layouts: 0.06 us -> 8.76 us
  transfers between devices with their start and end apart: 21 -> 12, of which waited for: 7 -> 4; matrix products, arithmetic and copies ran while one was open for 19% -> 4% of each run, Pallas kernels for 0% -> 8%
where the time goes in v2:
time: 115 us; the launch traced here: 114 us
  waiting for transfers between devices  42.3 us (37%)
  blocking collectives  21.7 us (19%)
  starting transfers between devices  20.3 us (18%)
  Pallas kernels  12.4 us (11%)
  local copies, waits for them, and re-layouts  12.1 us (11%)
  other arithmetic  3.9 us (3%)
  between operations  1.55 us (1%)
    all_to_all x1, blocking collectives, exchanged(): lax.all_to_all(flat, 'expert', split_axis=0, concat_axis=0, tiled=True)  21.7 us
    ppermute x4, waiting for transfers between devices, spread(): blocks.append(lax.ppermute(chunk, ('dp', 'tensor'), self.pairs(step)))  17.7 us
    ppermute x1, waiting for transfers between devices, on_device(): moved = lax.ppermute(arrived, 'expert', partner)  17 us
    unnamed x32, local copies, waits for them, and re-layouts  8.76 us
    all_to_all x1, waiting for transfers between devices, exchanged(): lax.all_to_all(flat, 'expert', split_axis=0, concat_axis=0, tiled=True)  7.66 us
    pallas_call x5, Pallas kernels, call(): pl.pallas_call(kernel, out_shape=outs, in_specs=[pl.BlockSpec(memory_spac...  7.52 us
    ppermute x4, starting transfers between devices, spread(): blocks.append(lax.ppermute(chunk, ('dp', 'tensor'), self.pairs(step)))  7.5 us
    pallas_call x1, Pallas kernels, weight_grads(): pl.pallas_call(grads_kernel, grid=(steps,), out_shape=[out] * 3, in_specs...  4.91 us
  transfers between devices with their start and end apart: 12, of which 4 were waited for; matrix products, arithmetic and copies ran while one was open for 4% of the time, Pallas kernels for 8%

profile of v2, /device:TPU:0, one launch (start us, length us, event | category | flops | bytes accessed | tf_op | source)
XLA Modules:
  0.0 114.3 jit_solution(4364038245533152647)
XLA Ops:
  0.6 1.1 copy-done.5
  1.7 1.1 copy-done.7
  2.8 0.7 copy-done.8
  3.5 0.7 copy-done.10
  4.9 1.0 shard_map.136
  6.6 21.7 %all_to_all.10 = bf16[8,252,128]{2,1,0:T(8,128)(2,1)S(1)} all-to-all(bf16[8,252,128]{2,1,0:T(8,128)(2,1)S(1)} %reshape.22), channel_id=1, replica_groups=mesh['expert'=8,'dp'=2,'tensor'=2] {'expert'}, dimensions={0} | all-to-all | bytes 1032192 | tf_op jit(solution)/shard_map/all_to_all | solution.py:99
  28.9 0.8 collective-permute-start
  29.8 2.8 %collective-permute-start.1 = (bf16[72,3584]{1,0:T(8,128)(2,1)S(1)}, bf16[72,3584]{1,0:T(8,128)(2,1)S(1)}, u32[]{:S(2)}, u32[]{:S(2)}) collective-permute-start(bf16[72,3584]{1,0:T(8,128)(2,1)S(1)} %squeeze_broadcast_in_dim_reshape.4), channel_id=1, source_target_pairs={{2,0},{0,1},{3,2},{1,3},{6,4},{4,5},{7,6},{5,7},{10,8},{8,9},{11,1... | collective-permute-start | bytes 1548296 | tf_op jit(solution)/shard_map/ppermute | solution.py:56
  32.5 11.5 %collective-permute-done.1 = bf16[72,3584]{1,0:T(8,128)(2,1)S(1)} collective-permute-done((bf16[72,3584]{1,0:T(8,128)(2,1)S(1)}, bf16[72,3584]{1,0:T(8,128)(2,1)S(1)}, u32[]{:S(2)}, u32[]{:S(2)}) %collective-permute-start.1) | collective-permute-done | bytes 516128 | tf_op jit(solution)/shard_map/ppermute | solution.py:56
  44.1 1.5 %copy-done.3 = bf16[1,1792,512]{2,1,0:T(8,128)(2,1)S(1)} copy-done((bf16[1,1792,512]{2,1,0:T(8,128)(2,1)S(1)}, bf16[1,1792,512]{2,1,0:T(8,128)(2,1)}, u32[]{:S(2)}) %copy-start.3) | copy-done | bytes 1835032
  45.6 1.0 shard_map.137.refs_0_
  46.6 0.9 collective-permute-start.2
  47.5 1.1 collective-permute-start.6
  49.9 1.5 %copy-done.2 = bf16[1,1792,512]{2,1,0:T(8,128)(2,1)S(1)} copy-done((bf16[1,1792,512]{2,1,0:T(8,128)(2,1)S(1)}, bf16[1,1792,512]{2,1,0:T(8,128)(2,1)}, u32[]{:S(2)}) %copy-start.2) | copy-done | bytes 1835032
  51.4 1.5 %copy-done.4 = bf16[1,1792,512]{2,1,0:T(8,128)(2,1)S(1)} copy-done((bf16[1,1792,512]{2,1,0:T(8,128)(2,1)S(1)}, bf16[1,1792,512]{2,1,0:T(8,128)(2,1)}, u32[]{:S(2)}) %copy-start.4) | copy-done | bytes 1835032
  52.9 3.1 %shard_map.138 = (bf16[2,72,1536]{2,1,0:T(8,128)(2,1)S(1)}, bf16[72,3584]{1,0:T(8,128)(2,1)S(1)}, bf16[72,3584]{1,0:T(8,128)(2,1)S(1)}) custom-call(f32[144,1536]{1,0:T(8,128)S(1)} %shard_map.137.refs_0_, f32[144,1536]{1,0:T(8,128)} %collective-permute-done.2.refs_1_, bf16[1792,512]{1,0:T(8,128)(2,1)S(1)} %bitcast.15, bf16[1792,512]{1,0:T(8,128)(2,1)S(1)} %bitcast.17, ...), custom_call_target="tpu_custom_call" | custom-call | flops 792723456 | bytes 8749056 | tf_op jit(solution)/shard_map/pallas_call | solution.py:108
  56.1 1.9 %collective-permute-start.9 = (bf16[72,1536]{1,0:T(8,128)(2,1)S(1)}, bf16[72,1536]{1,0:T(8,128)(2,1)S(1)}, u32[]{:S(2)}, u32[]{:S(2)}) collective-permute-start(bf16[72,1536]{1,0:T(8,128)(2,1)S(1)} %dynamic-slice_bitcast_fusion), channel_id=1, source_target_pairs={{0,16},{4,20},{8,24},{12,28},{16,0},{20,4},{24,8},{28,12},{1,17},{... | collective-permute-start | bytes 663560 | tf_op jit(solution)/shard_map/ppermute | solution.py:341
  58.0 0.7 collective-permute-start.3
  58.7 3.0 %collective-permute-start.4 = (bf16[72,3584]{1,0:T(8,128)(2,1)S(1)}, bf16[72,3584]{1,0:T(8,128)(2,1)S(1)}, u32[]{:S(2)}, u32[]{:S(2)}) collective-permute-start(bf16[72,3584]{1,0:T(8,128)(2,1)S(1)} %get-tuple-element.21), channel_id=1, source_target_pairs={{0,2},{1,0},{2,3},{3,1},{4,6},{5,4},{6,7},{7,5},{8,10},{9,8},{10,1... | collective-permute-start | bytes 1548296 | tf_op jit(solution)/shard_map/ppermute | solution.py:67
  61.7 17.0 %collective-permute-done.6 = bf16[72,3584]{1,0:T(8,128)(2,1)} collective-permute-done((bf16[72,3584]{1,0:T(8,128)(2,1)S(1)}, bf16[72,3584]{1,0:T(8,128)(2,1)}, u32[]{:S(2)}, u32[]{:S(2)}) %collective-permute-start.6) | collective-permute-done | bytes 516128 | tf_op jit(solution)/shard_map/ppermute | solution.py:338
  78.7 1.1 broadcast_select_fusion
  79.8 1.5 %collective-permute-start.7 = (bf16[72,3584]{1,0:T(8,128)(2,1)S(1)}, bf16[72,3584]{1,0:T(8,128)(2,1)}, u32[]{:S(2)}, u32[]{:S(2)}) collective-permute-start(bf16[72,3584]{1,0:T(8,128)(2,1)S(1)} %broadcast_select_fusion), channel_id=1, source_target_pairs={{0,0},{2,1},{1,2},{3,3},{4,4},{6,5},{5,6},{7,7},{8,8},{10,9},{9,10... | collective-permute-start | bytes 1548296 | tf_op jit(solution)/shard_map/ppermute | solution.py:56
  81.3 2.5 %collective-permute-start.8 = (bf16[72,3584]{1,0:T(8,128)(2,1)S(1)}, bf16[72,3584]{1,0:T(8,128)(2,1)}, u32[]{:S(2)}, u32[]{:S(2)}) collective-permute-start(bf16[72,3584]{1,0:T(8,128)(2,1)S(1)} %broadcast_select_fusion), channel_id=1, source_target_pairs={{2,0},{0,1},{3,2},{1,3},{6,4},{4,5},{7,6},{5,7},{10,8},{8,9},{11,1... | collective-permute-start | bytes 1548296 | tf_op jit(solution)/shard_map/ppermute | solution.py:56
  84.1 1.5 %reshape_squeeze.3 = bf16[8,252,128]{2,1,0:T(8,128)(2,1)} reshape(bf16[72,3584]{1,0:T(8,128)(2,1)S(1)} %add_convert_fusion) | data formatting | bytes 1032192 | tf_op jit(solution)/shard_map/reshape;squeeze | solution.py:98
  85.6 3.5 %all-to-all-start.1 = ((bf16[8,252,128]{2,1,0:T(8,128)(2,1)}), bf16[8,252,128]{2,1,0:T(8,128)(2,1)S(1)}, u32[]{:S(2)}, u32[]{:S(2)}) async-start(bf16[8,252,128]{2,1,0:T(8,128)(2,1)} %reshape_squeeze.3), calls=%async_computation.1 | async-start | bytes 1048576 | tf_op jit(solution)/shard_map/all_to_all | solution.py:99
  89.1 6.2 %collective-permute-done.8 = bf16[72,3584]{1,0:T(8,128)(2,1)} collective-permute-done((bf16[72,3584]{1,0:T(8,128)(2,1)S(1)}, bf16[72,3584]{1,0:T(8,128)(2,1)}, u32[]{:S(2)}, u32[]{:S(2)}) %collective-permute-start.8) | collective-permute-done | bytes 516128 | tf_op jit(solution)/shard_map/ppermute | solution.py:56
  95.2 1.3 %pad_maximum_fusion.1.x.d = bf16[144,3584]{1,0:T(8,128)(2,1)S(1)} fusion(bf16[72,3584]{1,0:T(8,128)(2,1)} %collective-permute-done.8, bf16[72,3584]{1,0:T(8,128)(2,1)} %collective-permute-done.7), kind=kLoop, calls=%fused_computation.1 | loop fusion | flops 2064384 | bytes 2064384 | tf_op jit(solution)/shard_map/concatenate | solution.py:288
  96.6 7.7 %all-to-all-done.1 = bf16[8,252,128]{2,1,0:T(8,128)(2,1)S(1)} async-done(((bf16[8,252,128]{2,1,0:T(8,128)(2,1)}), bf16[8,252,128]{2,1,0:T(8,128)(2,1)S(1)}, u32[]{:S(2)}, u32[]{:S(2)}) %all-to-all-start.1) | async-done | bytes 516128 | tf_op jit(solution)/shard_map/all_to_all | solution.py:99
  104.9 1.0 shard_map.140
  105.9 1.4 %collective-permute-start.5 = (f32[8,192]{1,0:T(8,128)S(1)}, f32[8,192]{1,0:T(8,128)S(1)}, u32[]{:S(2)}, u32[]{:S(2)}) collective-permute-start(f32[8,192]{1,0:T(8,128)S(1)} %shard_map.140), channel_id=1, source_target_pairs={{0,1},{1,0},{2,3},{3,2},{4,5},{5,4},{6,7},{7,6},{8,9},{9,8},{10,11... | collective-permute-start | bytes 18440 | tf_op jit(solution)/shard_map/ppermute | solution.py:327
  107.3 4.9 %weight_grads.1 = (bf16[1792,512]{1,0:T(8,128)(2,1)}, bf16[1792,512]{1,0:T(8,128)(2,1)}, bf16[1792,512]{1,0:T(8,128)(2,1)}) custom-call(bf16[144,3584]{1,0:T(8,128)(2,1)S(1)} %pad_maximum_fusion.1.x.d, bf16[144,3584]{1,0:T(8,128)(2,1)S(1)} %pad_maximum_fusion.1.x.d, bf16[144,1536]{1,0:T(8,128)(2,1)S(1)} %pad_maximum_fusion.2.units_ref), custom_call_target="tpu_custom_call" | custom-call | flops 792723456 | bytes 5505024 | tf_op jit(solution)/shard_map/weight_grads/pallas_call | solution.py:234
  112.2 1.5 %shard_map.139 = (bf16[192,1792]{1,0:T(8,128)(2,1)}, bf16[192,1792]{1,0:T(8,128)(2,1)}) custom-call(bf16[72,192]{1,0:T(8,128)(2,1)S(1)} %get-tuple-element.17.select, bf16[72,192]{1,0:T(8,128)(2,1)S(1)} %get-tuple-element.18.weighted, bf16[72,3584]{1,0:T(8,128)(2,1)S(1)} %reshape.23.back), custom_call_target="tpu_custom_call" | custom-call | bytes 1947648 | tf_op jit(solution)/shard_map/pallas_call | solution.py:108
  (45 shorter events, 4.3 us)
Async XLA Ops:
  0.6 1.1 copy-start.5
  1.7 1.1 copy-start.7
  2.8 0.7 copy-start.8
  3.5 0.7 copy-start.10
  4.2 0.7 copy-start.11
  6.6 37.6 %copy-start = (bf16[1,1792,512]{2,1,0:T(8,128)(2,1)S(1)}, bf16[1,1792,512]{2,1,0:T(8,128)(2,1)}, u32[]{:S(2)}) copy-start(bf16[1,1792,512]{2,1,0:T(8,128)(2,1)} %param.15) | copy-start | bytes 5505028
  28.9 15.2 %copy-start.13 = (bf16[72,3584]{1,0:T(8,128)(2,1)}, bf16[72,3584]{1,0:T(8,128)(2,1)S(1)}, u32[]{:S(2)}) copy-start(bf16[72,3584]{1,0:T(8,128)(2,1)S(1)} %squeeze_broadcast_in_dim_reshape.4) | copy-start | bytes 1548292
  28.9 15.2 %copy-start.1 = (bf16[1,1792,512]{2,1,0:T(8,128)(2,1)S(1)}, bf16[1,1792,512]{2,1,0:T(8,128)(2,1)}, u32[]{:S(2)}) copy-start(bf16[1,1792,512]{2,1,0:T(8,128)(2,1)} %param.16) | copy-start | bytes 5505028
  28.9 3.6 %collective-permute-start = (bf16[72,3584]{1,0:T(8,128)(2,1)S(1)}, bf16[72,3584]{1,0:T(8,128)(2,1)S(1)}, u32[]{:S(2)}, u32[]{:S(2)}) collective-permute-start(bf16[72,3584]{1,0:T(8,128)(2,1)S(1)} %squeeze_broadcast_in_dim_reshape.4), channel_id=1, source_target_pairs={{0,0},{2,1},{1,2},{3,3},{4,4},{6,5},{5,6},{7,7},{8,8},{10,9},{9,10... | collective-permute-start | bytes 1548296 | tf_op jit(solution)/shard_map/ppermute | solution.py:56
  29.8 14.3 %collective-permute-start.1 = (bf16[72,3584]{1,0:T(8,128)(2,1)S(1)}, bf16[72,3584]{1,0:T(8,128)(2,1)S(1)}, u32[]{:S(2)}, u32[]{:S(2)}) collective-permute-start(bf16[72,3584]{1,0:T(8,128)(2,1)S(1)} %squeeze_broadcast_in_dim_reshape.4), channel_id=1, source_target_pairs={{2,0},{0,1},{3,2},{1,3},{6,4},{4,5},{7,6},{5,7},{10,8},{8,9},{11,1... | collective-permute-start | bytes 1548296 | tf_op jit(solution)/shard_map/ppermute | solution.py:56
  44.1 1.5 %copy-start.3 = (bf16[1,1792,512]{2,1,0:T(8,128)(2,1)S(1)}, bf16[1,1792,512]{2,1,0:T(8,128)(2,1)}, u32[]{:S(2)}) copy-start(bf16[1,1792,512]{2,1,0:T(8,128)(2,1)} %param.17) | copy-start | bytes 5505028
  45.6 1.9 %copy-start.14 = (bf16[72,3584]{1,0:T(8,128)(2,1)S(1)}, bf16[72,3584]{1,0:T(8,128)(2,1)}, u32[]{:S(2)}) copy-start(bf16[72,3584]{1,0:T(8,128)(2,1)} %copy-done.13) | copy-start | bytes 1548292
  45.6 3.0 %copy-start.15 = (s32[8]{0:T(128)S(1)}, s32[8]{0:T(128)}, u32[]{:S(2)}) copy-start(s32[8]{0:T(128)} %param.14) | copy-start | bytes 100
  46.6 3.3 %collective-permute-start.2 = (f32[144,1536]{1,0:T(8,128)S(1)}, f32[144,1536]{1,0:T(8,128)}, u32[]{:S(2)}, u32[]{:S(2)}) collective-permute-start(f32[144,1536]{1,0:T(8,128)S(1)} %shard_map.137.refs_0_), channel_id=1, source_target_pairs={{0,2},{2,0},{1,3},{3,1},{4,6},{6,4},{5,7},{7,5},{8,10},{10,8},{9,1... | collective-permute-start | bytes 2654216 | tf_op jit(solution)/shard_map/ppermute | solution.py:85
  47.5 31.1 %collective-permute-start.6 = (bf16[72,3584]{1,0:T(8,128)(2,1)S(1)}, bf16[72,3584]{1,0:T(8,128)(2,1)}, u32[]{:S(2)}, u32[]{:S(2)}) collective-permute-start(bf16[72,3584]{1,0:T(8,128)(2,1)S(1)} %copy-done.14), channel_id=1, source_target_pairs={{0,16},{4,20},{8,24},{12,28},{16,0},{20,4},{24,8},{28,12},{1,17},{... | collective-permute-start | bytes 1548296 | tf_op jit(solution)/shard_map/ppermute | solution.py:338
  49.9 1.5 %copy-start.2 = (bf16[1,1792,512]{2,1,0:T(8,128)(2,1)S(1)}, bf16[1,1792,512]{2,1,0:T(8,128)(2,1)}, u32[]{:S(2)}) copy-start(bf16[1,1792,512]{2,1,0:T(8,128)(2,1)} %param.16) | copy-start | bytes 5505028
  51.4 1.5 %copy-start.4 = (bf16[1,1792,512]{2,1,0:T(8,128)(2,1)S(1)}, bf16[1,1792,512]{2,1,0:T(8,128)(2,1)}, u32[]{:S(2)}) copy-start(bf16[1,1792,512]{2,1,0:T(8,128)(2,1)} %param.17) | copy-start | bytes 5505028
  56.1 27.7 %collective-permute-start.9 = (bf16[72,1536]{1,0:T(8,128)(2,1)S(1)}, bf16[72,1536]{1,0:T(8,128)(2,1)S(1)}, u32[]{:S(2)}, u32[]{:S(2)}) collective-permute-start(bf16[72,1536]{1,0:T(8,128)(2,1)S(1)} %dynamic-slice_bitcast_fusion), channel_id=1, source_target_pairs={{0,16},{4,20},{8,24},{12,28},{16,0},{20,4},{24,8},{28,12},{1,17},{... | collective-permute-start | bytes 663560 | tf_op jit(solution)/shard_map/ppermute | solution.py:341
  58.0 26.0 %collective-permute-start.3 = (bf16[72,3584]{1,0:T(8,128)(2,1)S(1)}, bf16[72,3584]{1,0:T(8,128)(2,1)S(1)}, u32[]{:S(2)}, u32[]{:S(2)}) collective-permute-start(bf16[72,3584]{1,0:T(8,128)(2,1)S(1)} %get-tuple-element.20), channel_id=1, source_target_pairs={{0,0},{1,2},{2,1},{3,3},{4,4},{5,6},{6,5},{7,7},{8,8},{9,10},{10,9... | collective-permute-start | bytes 1548296 | tf_op jit(solution)/shard_map/ppermute | solution.py:67
  58.7 25.3 %collective-permute-start.4 = (bf16[72,3584]{1,0:T(8,128)(2,1)S(1)}, bf16[72,3584]{1,0:T(8,128)(2,1)S(1)}, u32[]{:S(2)}, u32[]{:S(2)}) collective-permute-start(bf16[72,3584]{1,0:T(8,128)(2,1)S(1)} %get-tuple-element.21), channel_id=1, source_target_pairs={{0,2},{1,0},{2,3},{3,1},{4,6},{5,4},{6,7},{7,5},{8,10},{9,8},{10,1... | collective-permute-start | bytes 1548296 | tf_op jit(solution)/shard_map/ppermute | solution.py:67
  79.8 9.3 %collective-permute-start.7 = (bf16[72,3584]{1,0:T(8,128)(2,1)S(1)}, bf16[72,3584]{1,0:T(8,128)(2,1)}, u32[]{:S(2)}, u32[]{:S(2)}) collective-permute-start(bf16[72,3584]{1,0:T(8,128)(2,1)S(1)} %broadcast_select_fusion), channel_id=1, source_target_pairs={{0,0},{2,1},{1,2},{3,3},{4,4},{6,5},{5,6},{7,7},{8,8},{10,9},{9,10... | collective-permute-start | bytes 1548296 | tf_op jit(solution)/shard_map/ppermute | solution.py:56
  81.3 14.0 %collective-permute-start.8 = (bf16[72,3584]{1,0:T(8,128)(2,1)S(1)}, bf16[72,3584]{1,0:T(8,128)(2,1)}, u32[]{:S(2)}, u32[]{:S(2)}) collective-permute-start(bf16[72,3584]{1,0:T(8,128)(2,1)S(1)} %broadcast_select_fusion), channel_id=1, source_target_pairs={{2,0},{0,1},{3,2},{1,3},{6,4},{4,5},{7,6},{5,7},{10,8},{8,9},{11,1... | collective-permute-start | bytes 1548296 | tf_op jit(solution)/shard_map/ppermute | solution.py:56
  83.8 12.8 %collective-permute-start.10 = (bf16[72,1536]{1,0:T(8,128)(2,1)S(1)}, bf16[72,1536]{1,0:T(8,128)(2,1)S(1)}, u32[]{:S(2)}, u32[]{:S(2)}) collective-permute-start(bf16[72,1536]{1,0:T(8,128)(2,1)S(1)} %broadcast_select_fusion.1), channel_id=1, source_target_pairs={{0,2},{2,0},{1,3},{3,1},{4,6},{6,4},{5,7},{7,5},{8,10},{10,8},{9,1... | collective-permute-start | bytes 663560 | tf_op jit(solution)/shard_map/ppermute | solution.py:90
  85.6 18.7 %all-to-all-start.1 = ((bf16[8,252,128]{2,1,0:T(8,128)(2,1)}), bf16[8,252,128]{2,1,0:T(8,128)(2,1)S(1)}, u32[]{:S(2)}, u32[]{:S(2)}) async-start(bf16[8,252,128]{2,1,0:T(8,128)(2,1)} %reshape_squeeze.3), calls=%async_computation.1 | async-start | bytes 1048576 | tf_op jit(solution)/shard_map/all_to_all | solution.py:99
  96.5 8.4 %copy-start.6 = (bf16[192,1792]{1,0:T(8,128)(2,1)S(1)}, bf16[192,1792]{1,0:T(8,128)(2,1)}, u32[]{:S(2)}) copy-start(bf16[192,1792]{1,0:T(8,128)(2,1)} %cot.3) | copy-start | bytes 2064388
  96.5 8.4 %copy-start.9 = (s32[192,8]{0,1:T(8,128)S(1)}, s32[192,8]{0,1:T(8,128)}, u32[]{:S(2)}) copy-start(s32[192,8]{0,1:T(8,128)} %param.10) | copy-start | bytes 18436
  96.5 8.4 %copy-start.12 = (s32[8]{0:T(128)S(1)}, s32[8]{0:T(128)}, u32[]{:S(2)}) copy-start(s32[8]{0:T(128)} %placement.3) | copy-start | bytes 100
  105.9 7.8 %collective-permute-start.5 = (f32[8,192]{1,0:T(8,128)S(1)}, f32[8,192]{1,0:T(8,128)S(1)}, u32[]{:S(2)}, u32[]{:S(2)}) collective-permute-start(f32[8,192]{1,0:T(8,128)S(1)} %shard_map.140), channel_id=1, source_target_pairs={{0,1},{1,0},{2,3},{3,2},{4,5},{5,4},{6,7},{7,6},{8,9},{9,8},{10,11... | collective-permute-start | bytes 18440 | tf_op jit(solution)/shard_map/ppermute | solution.py:327

commit v3 on v2

--- a/solution.py
+++ b/solution.py
@@ -10,7 +10,6 @@
 F32 = jnp.float32
 LANES = 128
 
-ROWS_AT_ONCE = 320
 contract = (((0,), (0,)), ((), ()))
 inner = (((1,), (1,)), ((), ()))
 
@@ -56,27 +55,12 @@
             blocks.append(lax.ppermute(chunk, ("dp", "tensor"), self.pairs(step)))
         return self.canonical(blocks)
 
-    def send_back(self, blocks):
+    def flipped(self, values):
         got = []
-        for step in range(self.n_d):
-            if self.group == 1:
-                block = blocks[step]
-            else:
-                block = pick(jnp.stack(blocks), (self.order + step) % self.n_d, self.n_d)
-            route = [(b, a) for a, b in self.pairs(step)]
-            got.append(lax.ppermute(block, ("dp", "tensor"), route))
+        for step in range(1, self.n_t):
+            route = [(i, (i + step) % self.n_t) for i in range(self.n_t)]
+            got.append(lax.ppermute(values[step - 1], "tensor", route))
         return got
-
-    def add_up(self, got):
-        total = None
-        for step, block in enumerate(got):
-            part = block.astype(F32)[None]
-            if self.group > 1:
-                place = ((self.d - step) % self.n_d) // self.n_t
-                mask = jnp.arange(self.group) == place
-                part = jnp.where(mask[:, None, None], part, 0.0)
-            total = part if total is None else total + part
-        return total.astype(BF)
 
     def others(self, value):
         got = []
@@ -86,9 +70,9 @@
         return got
 
     def gathered(self, value):
-        if self.n_d == 2:
+        if self.n_d == 2 and self.group == 1:
             other = lax.ppermute(value, "dp", [(0, 1), (1, 0)])
-            first = self.d == 0
+            first = self.d == self.order
             return jnp.concatenate([jnp.where(first, value, other), jnp.where(first, other, value)])
         return lax.all_gather(value, "dp", axis=0, tiled=True)
 
@@ -100,17 +84,20 @@
     return got.reshape(experts * CAP, cols)
 
 
-def call(kernel, outs, args, room, smem=0, flops=0):
-    vmem = pl.BlockSpec(memory_space=pltpu.VMEM)
+def call(kernel, outs, args, room, smem=0, hbm=0, scratch=(), flops=0):
+    space = pl.ANY if scratch else pltpu.VMEM
     moved = sum(a.size * a.dtype.itemsize for a in args) + sum(
         o.size * o.dtype.itemsize for o in outs
     )
     return pl.pallas_call(
         kernel,
         out_shape=outs,
-        in_specs=[pl.BlockSpec(memory_space=pltpu.SMEM)] * smem + [vmem] * (len(args) - smem),
-        out_specs=[vmem] * len(outs),
-        compiler_params=pltpu.CompilerParams(vmem_limit_bytes=room),
+        in_specs=[pl.BlockSpec(memory_space=pltpu.SMEM)] * smem
+        + [pl.BlockSpec(memory_space=pltpu.HBM)] * hbm
+        + [pl.BlockSpec(memory_space=space)] * (len(args) - smem - hbm),
+        out_specs=[pl.BlockSpec(memory_space=pltpu.VMEM)] * len(outs),
+        scratch_shapes=scratch,
+        compiler_params=pltpu.CompilerParams(vmem_limit_bytes=None if scratch else room),
         cost_estimate=pl.CostEstimate(flops=flops, bytes_accessed=moved, transcendentals=0),
     )(*args)
 
@@ -134,7 +121,19 @@
     return wanted, row - base
 
 
-def head_kernel(placement, routes, gates, tokens, cot, rows, select, weighted):
+def fetch(pairs, sems):
+    copies = [pltpu.make_async_copy(x, y, sems.at[i]) for i, (x, y) in enumerate(pairs)]
+    for copy in copies:
+        copy.start()
+    return copies
+
+
+def head_kernel(*refs):
+    given, (rows, select, weighted), kept = refs[:5], refs[5:8], refs[8:13]
+    copies = fetch(zip(given, kept), refs[13])
+    placement, routes, gates, tokens, cot = kept
+    for copy in copies[:3]:
+        copy.wait()
     slots, tok_count = select.shape
     top_count = routes.shape[0]
     half = tokens.shape[1]
@@ -154,48 +153,64 @@
     scaled = jnp.where(live, weight, 0.0).astype(BF)
     select[...] = chosen
     weighted[...] = scaled
+    copies[3].wait()
     rows[:, :half] = jnp.dot(chosen, tokens[...], preferred_element_type=F32).astype(BF)
+    copies[4].wait()
     rows[:, half:] = jnp.dot(scaled, cot[...], preferred_element_type=F32).astype(BF)
 
 
-def first_kernel(xd, wg, wu, wd, terms):
-    chunk, units = wg.shape
-    x, d = xd[:, :chunk], xd[:, chunk:]
-    terms[:, :units] = jnp.dot(x, wg[...], preferred_element_type=F32)
-    terms[:, units : 2 * units] = jnp.dot(x, wu[...], preferred_element_type=F32)
-    terms[:, 2 * units :] = jnp.dot(d, wd[...], preferred_element_type=F32)
-
-
-def middle_kernel(count, *refs):
-    parts, (wg, wu, wd) = refs[:count], refs[count : count + 3]
-    units_out, results = refs[count + 3], refs[count + 4 :]
-    chunk, units = wg.shape
-    blocks, rows = units_out.shape[:2]
-    at_once = blocks if blocks * rows <= ROWS_AT_ONCE else 1
-    for first in range(0, blocks, at_once):
-        span = pl.ds(first * rows, at_once * rows)
-
-        def total(which):
-            cols = pl.ds(which * units, units)
-            value = parts[0][span, cols]
-            for part in parts[1:]:
-                value = value + part[span, cols]
-            return value
-
-        gate, up, d_hidden = total(0), total(1), total(2)
-        sig = jax.nn.sigmoid(gate)
-        hidden = (gate * sig * up).astype(BF)
-        d_gate = (d_hidden * up * sig * (1.0 + gate * (1.0 - sig))).astype(BF)
-        d_up = (d_hidden * gate * sig).astype(BF)
-        out = dot(hidden, wd[...], inner)
-        back = dot(d_gate, wg[...], inner) + dot(d_up, wu[...], inner)
-        for j in range(at_once):
-            part = slice(j * rows, (j + 1) * rows)
-            results[first + j][:, :chunk] = out[part].astype(BF)
-            results[first + j][:, chunk:] = back[part].astype(BF)
-            units_out[first + j, :, :units] = d_gate.astype(F32)[part].astype(BF)
-            units_out[first + j, :, units : 2 * units] = d_up.astype(F32)[part].astype(BF)
-            units_out[first + j, :, 2 * units :] = hidden.astype(F32)[part].astype(BF)
+def expert_kernel(n_d, n_t, *refs):
+    shards, rows_in = refs[: 3 * n_d], refs[3 * n_d : 3 * n_d + n_t]
+    refs = refs[3 * n_d + n_t :]
+    units_out, terms, (w, x, w_sems, x_sems) = refs[0], refs[1 : 1 + n_t], refs[1 + n_t :]
+    d, t = lax.axis_index("dp"), lax.axis_index("tensor")
+    chunk, units = w.shape[2:]
+    half = x.shape[2] // 2
+    group = n_d // n_t
+    x_copies = fetch(
+        [(rows_in[s], x.at[lax.rem(t - s + n_t, n_t)]) for s in range(n_t)], x_sems
+    )
+    w_copies = fetch(
+        [
+            (shards[which * n_d + s], w.at[which, lax.rem(d - s + n_d, n_d)])
+            for which in range(3)
+            for s in range(n_d)
+        ],
+        w_sems,
+    )
+    for copy in x_copies:
+        copy.wait()
+
+    def product(which, offset):
+        for copy in w_copies[which * n_d : (which + 1) * n_d]:
+            copy.wait()
+        value = None
+        for s in range(n_d):
+            cols = pl.ds(offset + (s % group) * chunk, chunk)
+            part = jnp.dot(x[s // group, :, cols], w[which, s], preferred_element_type=F32)
+            value = part if value is None else value + part
+        return value
+
+    gate, up = product(0, 0), product(1, 0)
+    sig = jax.nn.sigmoid(gate)
+    hidden = (gate * sig * up).astype(BF)
+    d_hidden = product(2, half)
+    d_gate = (d_hidden * up * sig * (1.0 + gate * (1.0 - sig))).astype(BF)
+    d_up = (d_hidden * gate * sig).astype(BF)
+    units_out[:, :units] = d_gate
+    units_out[:, units : 2 * units] = d_up
+    units_out[:, 2 * units :] = hidden
+    for s in range(n_d):
+        out = dot(hidden, w[2, s], inner).astype(BF)
+        back = (dot(d_gate, w[0, s], inner) + dot(d_up, w[1, s], inner)).astype(BF)
+        col = (s % group) * chunk
+        step = lax.rem(s // group - t + n_t, n_t)
+        for k in range(n_t):
+
+            @pl.when(step == k)
+            def _():
+                terms[k][:, col : col + chunk] = out
+                terms[k][:, half + col : half + col + chunk] = back
 
 
 def gate_kernel(placement, routes, select, cot, back, gate_part):
@@ -227,7 +242,7 @@
 
 def weight_grads(held, units_held, chunk, units):
     rows = held.shape[0]
-    block = 256 if chunk % 256 == 0 else LANES
+    block = next(b for b in (896, 512, 256, LANES) if chunk % b == 0)
     steps = chunk // block
     out = shape((chunk, units), BF)
     spec = pl.BlockSpec((block, units), lambda i: (i, 0))
@@ -261,7 +276,6 @@
     chunk, units = wg.shape
     tok_count, top_count = routes.shape
     slots_all = experts * CAP
-    rows_all = lay.n_d * slots_all
     half_width = tokens.shape[1]
     routes_t, gates_t = routes.T, gates.T
 
@@ -270,49 +284,47 @@
         shape((slots_all, tok_count), BF),
         shape((slots_all, tok_count), BF),
     ]
+    given = (placement, routes_t, gates_t, tokens, cotangent)
     outgoing, select, weighted = call(
         head_kernel,
         outs,
-        (placement, routes_t, gates_t, tokens, cotangent),
+        given,
         room_for(tokens, cotangent, *outs),
-        smem=1,
+        hbm=len(given),
+        scratch=[
+            pltpu.SMEM(placement.shape, jnp.int32),
+            *(pltpu.VMEM(x.shape, x.dtype) for x in given[1:]),
+            pltpu.SemaphoreType.DMA((len(given),)),
+        ],
     )
     arrived = exchanged(outgoing, experts)
 
-    def spread(rows):
-        if lay.group == 1:
-            pieces = rows[None]
-        else:
-            both = rows.reshape(slots_all, 2, lay.group, chunk)
-            pieces = jnp.moveaxis(both, 2, 0).reshape(lay.group, slots_all, 2 * chunk)
-        return jnp.concatenate(lay.spread(pieces), axis=0)
-
-    xd = spread(arrived)
-    partial_sums = shape((rows_all, 3 * units), F32)
-    (own_terms,) = call(
-        first_kernel,
-        [partial_sums],
-        (xd, wg, wu, wd),
-        room_for(xd, wg, wu, wd, partial_sums),
-        flops=6 * rows_all * chunk * units,
-    )
-    parts = [own_terms, *lay.others(own_terms)]
-    outs = [shape((lay.n_d, slots_all, 3 * units), BF)]
-    outs += [shape((slots_all, 2 * chunk), BF)] * lay.n_d
-    units_all, *results = call(
-        lambda *refs: middle_kernel(lay.n_d, *refs),
+    others = lay.flipped([arrived] * (lay.n_t - 1))
+    shards = []
+    for own in (wg, wu, wd):
+        shards += [own, *lay.others(own)]
+    weights_room = shape((3, lay.n_d, chunk, units), BF)
+    rows_room = shape((lay.n_t, slots_all, 2 * half_width), BF)
+    outs = [shape((slots_all, 3 * units), BF)]
+    outs += [shape((slots_all, 2 * half_width), BF)] * lay.n_t
+    units_own, *terms = call(
+        lambda *refs: expert_kernel(lay.n_d, lay.n_t, *refs),
         outs,
-        (*parts, wg, wu, wd),
-        room_for(*parts, wg, wu, wd, *outs),
-        flops=6 * rows_all * chunk * units,
-    )
-    sums = lay.add_up(lay.send_back(results))
-    if lay.group == 1:
-        home = sums[0]
-    else:
-        home = jnp.moveaxis(sums.reshape(lay.group, slots_all, 2, chunk), 0, 2)
-        home = home.reshape(slots_all, 2 * half_width)
-    back = exchanged(home, experts)
+        (*shards, arrived, *others),
+        room_for(weights_room, rows_room, *outs),
+        hbm=len(shards),
+        scratch=[
+            pltpu.VMEM(weights_room.shape, BF),
+            pltpu.VMEM(rows_room.shape, BF),
+            pltpu.SemaphoreType.DMA((3 * lay.n_d,)),
+            pltpu.SemaphoreType.DMA((lay.n_t,)),
+        ],
+        flops=12 * slots_all * lay.n_d * chunk * units,
+    )
+    home = terms[0].astype(F32)
+    for got in lay.flipped(terms[1:]):
+        home = home + got.astype(F32)
+    back = exchanged(home.astype(BF), experts)
 
     gate_shape = shape((top_count, tok_count), F32)
     (gate_part,) = call(
@@ -336,8 +348,13 @@
 
     partner = [(i, (i + experts // 2) % experts) for i in range(experts)]
     moved = lax.ppermute(arrived, "expert", partner)
-    held = spread(jnp.where(my_flag, moved, arrived))
-    units_own = pick(units_all, lay.d, lay.n_d)
+    held = jnp.where(my_flag, moved, arrived)
+    if lay.group == 1:
+        pieces = held[None]
+    else:
+        pieces = jnp.moveaxis(held.reshape(slots_all, 2, lay.group, chunk), 2, 0)
+        pieces = pieces.reshape(lay.group, slots_all, 2 * chunk)
+    held = jnp.concatenate(lay.spread(pieces), axis=0)
     units_moved = lax.ppermute(units_own, "expert", partner)
     units_held = jnp.where(my_flag, units_moved, units_own)
     units_held = lay.gathered(units_held)

time: 115 us -> 95.6 us (0.83)
  waiting for transfers between devices: 42.3 us -> 29.4 us
  Pallas kernels: 12.4 us -> 19.9 us
  local copies, waits for them, and re-layouts: 12.1 us -> 5.74 us
  starting transfers between devices: 20.3 us -> 14.2 us
    ppermute x1, waiting for transfers between devices: 17 us -> 0.01 us  [on_device(): moved = lax.ppermute(arrived, 'expert', partner)]
    ppermute x4 -> x2, waiting for transfers between devices: 17.7 us -> 2.76 us  [spread(): blocks.append(lax.ppermute(chunk, ('dp', 'tensor'), self.pairs(step)))]
    ppermute x2, waiting for transfers between devices: 0.01 us -> 14.6 us  [flipped(): got.append(lax.ppermute(values[step - 1], 'tensor', route))]
    pallas_call x5 -> x4, Pallas kernels: 7.52 us -> 16.6 us  [call(): pl.pallas_call(kernel, out_shape=outs, in_specs=[pl.BlockSpec(memory_spac...]
    unnamed x32 -> x20, local copies, waits for them, and re-layouts: 8.76 us -> 1.41 us
    ppermute x1, waiting for transfers between devices: 0.01 us -> 5.37 us  [on_device(): units_moved = lax.ppermute(units_own, 'expert', partner)]
    ppermute x4 -> x2, starting transfers between devices: 7.5 us -> 2.46 us  [spread(): blocks.append(lax.ppermute(chunk, ('dp', 'tensor'), self.pairs(step)))]
    reshape x1 -> x2, local copies, waits for them, and re-layouts: 0.66 us -> 3.16 us  [exchanged(): flat = rows.reshape(experts, CAP * cols // LANES, LANES)]
  transfers between devices with their start and end apart: 12 -> 12, of which waited for: 4 -> 5; matrix products, arithmetic and copies ran while one was open for 4% -> 6% of each run, Pallas kernels for 8% -> 20%
where the time goes in v3:
time: 95.6 us; the launch traced here: 95.2 us
  waiting for transfers between devices  29.4 us (31%)
  blocking collectives  21.8 us (23%)
  Pallas kernels  19.9 us (21%)
  starting transfers between devices  14.2 us (15%)
  local copies, waits for them, and re-layouts  5.74 us (6%)
  other arithmetic  2.81 us (3%)
  between operations  1.51 us (2%)
    all_to_all x1, blocking collectives, exchanged(): lax.all_to_all(flat, 'expert', split_axis=0, concat_axis=0, tiled=True)  21.8 us
    pallas_call x4, Pallas kernels, call(): pl.pallas_call(kernel, out_shape=outs, in_specs=[pl.BlockSpec(memory_spac...  16.6 us
    ppermute x2, waiting for transfers between devices, flipped(): got.append(lax.ppermute(values[step - 1], 'tensor', route))  14.6 us
    all_to_all x1, waiting for transfers between devices, exchanged(): lax.all_to_all(flat, 'expert', split_axis=0, concat_axis=0, tiled=True)  6.65 us
    ppermute x1, waiting for transfers between devices, on_device(): units_moved = lax.ppermute(units_own, 'expert', partner)  5.37 us
    all_to_all x1, starting transfers between devices, exchanged(): lax.all_to_all(flat, 'expert', split_axis=0, concat_axis=0, tiled=True)  3.49 us
    pallas_call x1, Pallas kernels, weight_grads(): pl.pallas_call(grads_kernel, grid=(steps,), out_shape=[out] * 3, in_specs...  3.29 us
    reshape x2, local copies, waits for them, and re-layouts, exchanged(): flat = rows.reshape(experts, CAP * cols // LANES, LANES)  3.16 us
  transfers between devices with their start and end apart: 12, of which 5 were waited for; matrix products, arithmetic and copies ran while one was open for 6% of the time, Pallas kernels for 20%

profile of v3, /device:TPU:0, one launch (start us, length us, event | category | flops | bytes accessed | tf_op | source)
XLA Modules:
  0.0 95.2 jit_solution(1047776337678524543)
XLA Ops:
  0.6 0.6 collective-permute-start
  1.2 0.1 collective-permute-start.1
  1.3 0.4 collective-permute-start.2
  1.7 2.5 %shard_map.136 = (bf16[72,3584]{1,0:T(8,128)(2,1)}, bf16[72,192]{1,0:T(8,128)(2,1)}, bf16[72,192]{1,0:T(8,128)(2,1)}) custom-call(s32[8]{0:T(128)} %placement.1, s32[8,192]{1,0:T(8,128)} %bitcast.10, bf16[8,192]{1,0:T(8,128)(2,1)} %bitcast.18, bf16[192,1792]{1,0:T(8,128)(2,1)} %refs_3_.1, bf16[192,1792]{1,0:T(8,128)(2,1)} %cot.1), custom_call_target="tpu_custom_call" | custom-call | bytes 1956896 | tf_op jit(solution)/shard_map/pallas_call | solution.py:92
  4.2 1.7 %reshape.24 = bf16[8,252,128]{2,1,0:T(8,128)(2,1)S(1)} reshape(bf16[72,3584]{1,0:T(8,128)(2,1)} %get-tuple-element.19) | data formatting | bytes 1032192 | tf_op jit(solution)/shard_map/reshape | solution.py:82
  5.9 21.8 %all_to_all.10 = bf16[8,252,128]{2,1,0:T(8,128)(2,1)S(1)} all-to-all(bf16[8,252,128]{2,1,0:T(8,128)(2,1)S(1)} %reshape.24), channel_id=1, replica_groups=mesh['expert'=8,'dp'=2,'tensor'=2] {'expert'}, dimensions={0} | all-to-all | bytes 1032192 | tf_op jit(solution)/shard_map/all_to_all | solution.py:83
  27.6 0.6 reshape.25.refs_6_
  28.2 1.6 %collective-permute-start.3 = (bf16[72,3584]{1,0:T(8,128)(2,1)S(1)}, bf16[72,3584]{1,0:T(8,128)(2,1)S(1)}, u32[]{:S(2)}, u32[]{:S(2)}) collective-permute-start(bf16[72,3584]{1,0:T(8,128)(2,1)S(1)} %reshape.25.refs_6_), channel_id=1, source_target_pairs={{0,1},{1,0},{2,3},{3,2},{4,5},{5,4},{6,7},{7,6},{8,9},{9,8},{10,11... | collective-permute-start | bytes 1548296 | tf_op jit(solution)/shard_map/ppermute | solution.py:62
  29.8 0.9 collective-permute-start.6
  30.7 0.6 fusion
  32.0 9.3 %collective-permute-done.3.refs_7_ = bf16[72,3584]{1,0:T(8,128)(2,1)S(1)} collective-permute-done((bf16[72,3584]{1,0:T(8,128)(2,1)S(1)}, bf16[72,3584]{1,0:T(8,128)(2,1)S(1)}, u32[]{:S(2)}, u32[]{:S(2)}) %collective-permute-start.3) | collective-permute-done | bytes 516128 | tf_op jit(solution)/shard_map/ppermute | solution.py:62
  41.3 0.8 copy-done.7
  42.0 0.6 copy-done.6
  42.6 11.7 %shard_map.137 = (bf16[72,1536]{1,0:T(8,128)(2,1)}, bf16[72,3584]{1,0:T(8,128)(2,1)}, bf16[72,3584]{1,0:T(8,128)(2,1)}) custom-call(bf16[1792,512]{1,0:T(8,128)(2,1)} %bitcast.13, bf16[1792,512]{1,0:T(8,128)(2,1)} %copy-done.6, bf16[1792,512]{1,0:T(8,128)(2,1)} %bitcast.15, bf16[1792,512]{1,0:T(8,128)(2,1)} %collective-permute-done.1.refs_3_, ...), custom_call_target="tpu_custom_call" | custom-call | flops 1585446912 | bytes 13295616 | tf_op jit(solution)/shard_map/pallas_call | solution.py:92
  54.3 1.5 %collective-permute-start.9 = (bf16[72,1536]{1,0:T(8,128)(2,1)}, bf16[72,1536]{1,0:T(8,128)(2,1)S(1)}, u32[]{:S(2)}, u32[]{:S(2)}) collective-permute-start(bf16[72,1536]{1,0:T(8,128)(2,1)} %get-tuple-element.24), channel_id=1, source_target_pairs={{0,16},{4,20},{8,24},{12,28},{16,0},{20,4},{24,8},{28,12},{1,17},{... | collective-permute-start | bytes 663560 | tf_op jit(solution)/shard_map/ppermute | solution.py:358
  55.9 1.5 %collective-permute-start.4 = (bf16[72,3584]{1,0:T(8,128)(2,1)}, bf16[72,3584]{1,0:T(8,128)(2,1)S(1)}, u32[]{:S(2)}, u32[]{:S(2)}) collective-permute-start(bf16[72,3584]{1,0:T(8,128)(2,1)} %get-tuple-element.21), channel_id=1, source_target_pairs={{0,1},{1,0},{2,3},{3,2},{4,5},{5,4},{6,7},{7,6},{8,9},{9,8},{10,11... | collective-permute-start | bytes 1548296 | tf_op jit(solution)/shard_map/ppermute | solution.py:62
  57.5 1.5 %collective-permute-start.7 = (bf16[72,3584]{1,0:T(8,128)(2,1)S(1)}, bf16[72,3584]{1,0:T(8,128)(2,1)}, u32[]{:S(2)}, u32[]{:S(2)}) collective-permute-start(bf16[72,3584]{1,0:T(8,128)(2,1)S(1)} %broadcast_select_fusion), channel_id=1, source_target_pairs={{0,0},{2,1},{1,2},{3,3},{4,4},{6,5},{5,6},{7,7},{8,8},{10,9},{9,10... | collective-permute-start | bytes 1548296 | tf_op jit(solution)/shard_map/ppermute | solution.py:55
  58.9 1.0 %collective-permute-start.8 = (bf16[72,3584]{1,0:T(8,128)(2,1)S(1)}, bf16[72,3584]{1,0:T(8,128)(2,1)}, u32[]{:S(2)}, u32[]{:S(2)}) collective-permute-start(bf16[72,3584]{1,0:T(8,128)(2,1)S(1)} %broadcast_select_fusion), channel_id=1, source_target_pairs={{2,0},{0,1},{3,2},{1,3},{6,4},{4,5},{7,6},{5,7},{10,8},{8,9},{11,1... | collective-permute-start | bytes 1548296 | tf_op jit(solution)/shard_map/ppermute | solution.py:55
  59.9 5.4 %collective-permute-done.9 = bf16[72,1536]{1,0:T(8,128)(2,1)S(1)} collective-permute-done((bf16[72,1536]{1,0:T(8,128)(2,1)}, bf16[72,1536]{1,0:T(8,128)(2,1)S(1)}, u32[]{:S(2)}, u32[]{:S(2)}) %collective-permute-start.9) | collective-permute-done | bytes 221216 | tf_op jit(solution)/shard_map/ppermute | solution.py:358
  65.4 5.3 %collective-permute-done.4 = bf16[72,3584]{1,0:T(8,128)(2,1)S(1)} collective-permute-done((bf16[72,3584]{1,0:T(8,128)(2,1)}, bf16[72,3584]{1,0:T(8,128)(2,1)S(1)}, u32[]{:S(2)}, u32[]{:S(2)}) %collective-permute-start.4) | collective-permute-done | bytes 516128 | tf_op jit(solution)/shard_map/ppermute | solution.py:62
  70.7 0.1 add_convert_fusion
  70.8 1.5 %reshape.26 = bf16[8,252,128]{2,1,0:T(8,128)(2,1)} reshape(bf16[72,3584]{1,0:T(8,128)(2,1)S(1)} %add_convert_fusion) | data formatting | bytes 1032192 | tf_op jit(solution)/shard_map/reshape | solution.py:82
  72.3 3.5 %all-to-all-start.1 = ((bf16[8,252,128]{2,1,0:T(8,128)(2,1)}), bf16[8,252,128]{2,1,0:T(8,128)(2,1)S(1)}, u32[]{:S(2)}, u32[]{:S(2)}) async-start(bf16[8,252,128]{2,1,0:T(8,128)(2,1)} %reshape.26), calls=%async_computation.1 | async-start | bytes 1048576 | tf_op jit(solution)/shard_map/all_to_all | solution.py:83
  75.8 2.8 %collective-permute-done.8 = bf16[72,3584]{1,0:T(8,128)(2,1)} collective-permute-done((bf16[72,3584]{1,0:T(8,128)(2,1)S(1)}, bf16[72,3584]{1,0:T(8,128)(2,1)}, u32[]{:S(2)}, u32[]{:S(2)}) %collective-permute-start.8) | collective-permute-done | bytes 516128 | tf_op jit(solution)/shard_map/ppermute | solution.py:55
  78.6 1.3 %pad_maximum_fusion.x.d = bf16[144,3584]{1,0:T(8,128)(2,1)S(1)} fusion(bf16[72,3584]{1,0:T(8,128)(2,1)} %collective-permute-done.8, bf16[72,3584]{1,0:T(8,128)(2,1)} %collective-permute-done.7), kind=kLoop, calls=%fused_computation | loop fusion | flops 2064384 | bytes 2064384 | tf_op jit(solution)/shard_map/concatenate | solution.py:357
  80.0 6.7 %all-to-all-done.1 = bf16[8,252,128]{2,1,0:T(8,128)(2,1)S(1)} async-done(((bf16[8,252,128]{2,1,0:T(8,128)(2,1)}), bf16[8,252,128]{2,1,0:T(8,128)(2,1)S(1)}, u32[]{:S(2)}, u32[]{:S(2)}) %all-to-all-start.1) | async-done | bytes 516128 | tf_op jit(solution)/shard_map/all_to_all | solution.py:83
  86.6 0.6 reshape.27.back
  87.3 1.0 %shard_map.139 = f32[8,192]{1,0:T(8,128)S(1)} custom-call(s32[8]{0:T(128)S(1)} %copy-done.4, s32[8,192]{1,0:T(8,128)S(1)} %bitcast.11, bf16[72,192]{1,0:T(8,128)(2,1)S(1)} %copy-done.1, bf16[192,1792]{1,0:T(8,128)(2,1)S(1)} %copy-done, bf16[72,3584]{1,0:T(8,128)(2,1)S(1)} %reshape.27.back), custom_call_target="tpu_custom_call" | custom-call | bytes 1244192 | tf_op jit(solution)/shard_map/pallas_call | solution.py:92
  88.2 1.6 %collective-permute-start.5 = (f32[8,192]{1,0:T(8,128)S(1)}, f32[8,192]{1,0:T(8,128)S(1)}, u32[]{:S(2)}, u32[]{:S(2)}) collective-permute-start(f32[8,192]{1,0:T(8,128)S(1)} %shard_map.139), channel_id=1, source_target_pairs={{0,1},{1,0},{2,3},{3,2},{4,5},{5,4},{6,7},{7,6},{8,9},{9,8},{10,11... | collective-permute-start | bytes 18440 | tf_op jit(solution)/shard_map/ppermute | solution.py:339
  89.8 3.3 %weight_grads.1 = (bf16[1792,512]{1,0:T(8,128)(2,1)}, bf16[1792,512]{1,0:T(8,128)(2,1)}, bf16[1792,512]{1,0:T(8,128)(2,1)}) custom-call(bf16[144,3584]{1,0:T(8,128)(2,1)S(1)} %pad_maximum_fusion.x.d, bf16[144,3584]{1,0:T(8,128)(2,1)S(1)} %pad_maximum_fusion.x.d, bf16[144,1536]{1,0:T(8,128)(2,1)S(1)} %pad_maximum_fusion.1.units_ref), custom_call_target="tpu_custom_call" | custom-call | flops 792723456 | bytes 5505024 | tf_op jit(solution)/shard_map/weight_grads/pallas_call | solution.py:249
  93.1 1.5 %shard_map.138 = (bf16[192,1792]{1,0:T(8,128)(2,1)}, bf16[192,1792]{1,0:T(8,128)(2,1)}) custom-call(bf16[72,192]{1,0:T(8,128)(2,1)S(1)} %copy-done.1, bf16[72,192]{1,0:T(8,128)(2,1)S(1)} %copy-done.2, bf16[72,3584]{1,0:T(8,128)(2,1)S(1)} %reshape.27.back), custom_call_target="tpu_custom_call" | custom-call | bytes 1947648 | tf_op jit(solution)/shard_map/pallas_call | solution.py:92
  94.6 0.6 add_bitcast_fusion
  (30 shorter events, 0.3 us)
Async XLA Ops:
  0.6 40.6 %collective-permute-start = (bf16[1792,512]{1,0:T(8,128)(2,1)}, bf16[1792,512]{1,0:T(8,128)(2,1)S(1)}, u32[]{:S(2)}, u32[]{:S(2)}) collective-permute-start(bf16[1792,512]{1,0:T(8,128)(2,1)} %bitcast.12), channel_id=1, source_target_pairs={{0,2},{2,0},{1,3},{3,1},{4,6},{6,4},{5,7},{7,5},{8,10},{10,8},{9,1... | collective-permute-start | bytes 5505032 | tf_op jit(solution)/shard_map/ppermute | solution.py:69
  1.2 40.1 %collective-permute-start.1 = (bf16[1792,512]{1,0:T(8,128)(2,1)}, bf16[1792,512]{1,0:T(8,128)(2,1)}, u32[]{:S(2)}, u32[]{:S(2)}) collective-permute-start(bf16[1792,512]{1,0:T(8,128)(2,1)} %bitcast.14), channel_id=1, source_target_pairs={{0,2},{2,0},{1,3},{3,1},{4,6},{6,4},{5,7},{7,5},{8,10},{10,8},{9,1... | collective-permute-start | bytes 5505032 | tf_op jit(solution)/shard_map/ppermute | solution.py:69
  1.3 40.0 %collective-permute-start.2 = (bf16[1792,512]{1,0:T(8,128)(2,1)}, bf16[1792,512]{1,0:T(8,128)(2,1)}, u32[]{:S(2)}, u32[]{:S(2)}) collective-permute-start(bf16[1792,512]{1,0:T(8,128)(2,1)} %bitcast.16), channel_id=1, source_target_pairs={{0,2},{2,0},{1,3},{3,1},{4,6},{6,4},{5,7},{7,5},{8,10},{10,8},{9,1... | collective-permute-start | bytes 5505032 | tf_op jit(solution)/shard_map/ppermute | solution.py:69
  4.2 26.5 %copy-start.9 = (s32[8]{0:T(128)S(1)}, s32[8]{0:T(128)}, u32[]{:S(2)}) copy-start(s32[8]{0:T(128)} %param.14) | copy-start | bytes 100
  28.2 13.1 %copy-start.5 = (bf16[72,3584]{1,0:T(8,128)(2,1)}, bf16[72,3584]{1,0:T(8,128)(2,1)S(1)}, u32[]{:S(2)}) copy-start(bf16[72,3584]{1,0:T(8,128)(2,1)S(1)} %reshape.25.refs_6_) | copy-start | bytes 1548292
  28.2 13.0 %collective-permute-start.3 = (bf16[72,3584]{1,0:T(8,128)(2,1)S(1)}, bf16[72,3584]{1,0:T(8,128)(2,1)S(1)}, u32[]{:S(2)}, u32[]{:S(2)}) collective-permute-start(bf16[72,3584]{1,0:T(8,128)(2,1)S(1)} %reshape.25.refs_6_), channel_id=1, source_target_pairs={{0,1},{1,0},{2,3},{3,2},{4,5},{5,4},{6,7},{7,6},{8,9},{9,8},{10,11... | collective-permute-start | bytes 1548296 | tf_op jit(solution)/shard_map/ppermute | solution.py:62
  29.8 27.6 %collective-permute-start.6 = (bf16[72,3584]{1,0:T(8,128)(2,1)S(1)}, bf16[72,3584]{1,0:T(8,128)(2,1)S(1)}, u32[]{:S(2)}, u32[]{:S(2)}) collective-permute-start(bf16[72,3584]{1,0:T(8,128)(2,1)S(1)} %reshape.25.refs_6_), channel_id=1, source_target_pairs={{0,16},{4,20},{8,24},{12,28},{16,0},{20,4},{24,8},{28,12},{1,17},{... | collective-permute-start | bytes 1548296 | tf_op jit(solution)/shard_map/ppermute | solution.py:350
  41.2 0.8 copy-start.7
  41.3 1.4 %copy-start.6 = (bf16[1792,512]{1,0:T(8,128)(2,1)}, bf16[1792,512]{1,0:T(8,128)(2,1)S(1)}, u32[]{:S(2)}) copy-start(bf16[1792,512]{1,0:T(8,128)(2,1)S(1)} %collective-permute-done.refs_1_) | copy-start | bytes 5505028
  54.3 16.4 %copy-start.8 = (bf16[72,3584]{1,0:T(8,128)(2,1)S(1)}, bf16[72,3584]{1,0:T(8,128)(2,1)}, u32[]{:S(2)}) copy-start(bf16[72,3584]{1,0:T(8,128)(2,1)} %get-tuple-element.20) | copy-start | bytes 1548292
  54.3 10.9 %collective-permute-start.9 = (bf16[72,1536]{1,0:T(8,128)(2,1)}, bf16[72,1536]{1,0:T(8,128)(2,1)S(1)}, u32[]{:S(2)}, u32[]{:S(2)}) collective-permute-start(bf16[72,1536]{1,0:T(8,128)(2,1)} %get-tuple-element.24), channel_id=1, source_target_pairs={{0,16},{4,20},{8,24},{12,28},{16,0},{20,4},{24,8},{28,12},{1,17},{... | collective-permute-start | bytes 663560 | tf_op jit(solution)/shard_map/ppermute | solution.py:358
  55.9 14.8 %collective-permute-start.4 = (bf16[72,3584]{1,0:T(8,128)(2,1)}, bf16[72,3584]{1,0:T(8,128)(2,1)S(1)}, u32[]{:S(2)}, u32[]{:S(2)}) collective-permute-start(bf16[72,3584]{1,0:T(8,128)(2,1)} %get-tuple-element.21), channel_id=1, source_target_pairs={{0,1},{1,0},{2,3},{3,2},{4,5},{5,4},{6,7},{7,6},{8,9},{9,8},{10,11... | collective-permute-start | bytes 1548296 | tf_op jit(solution)/shard_map/ppermute | solution.py:62
  57.5 18.3 %collective-permute-start.7 = (bf16[72,3584]{1,0:T(8,128)(2,1)S(1)}, bf16[72,3584]{1,0:T(8,128)(2,1)}, u32[]{:S(2)}, u32[]{:S(2)}) collective-permute-start(bf16[72,3584]{1,0:T(8,128)(2,1)S(1)} %broadcast_select_fusion), channel_id=1, source_target_pairs={{0,0},{2,1},{1,2},{3,3},{4,4},{6,5},{5,6},{7,7},{8,8},{10,9},{9,10... | collective-permute-start | bytes 1548296 | tf_op jit(solution)/shard_map/ppermute | solution.py:55
  58.9 19.7 %collective-permute-start.8 = (bf16[72,3584]{1,0:T(8,128)(2,1)S(1)}, bf16[72,3584]{1,0:T(8,128)(2,1)}, u32[]{:S(2)}, u32[]{:S(2)}) collective-permute-start(bf16[72,3584]{1,0:T(8,128)(2,1)S(1)} %broadcast_select_fusion), channel_id=1, source_target_pairs={{2,0},{0,1},{3,2},{1,3},{6,4},{4,5},{7,6},{5,7},{10,8},{8,9},{11,1... | collective-permute-start | bytes 1548296 | tf_op jit(solution)/shard_map/ppermute | solution.py:55
  65.3 14.6 %collective-permute-start.10 = (bf16[72,1536]{1,0:T(8,128)(2,1)S(1)}, bf16[72,1536]{1,0:T(8,128)(2,1)S(1)}, u32[]{:S(2)}, u32[]{:S(2)}) collective-permute-start(bf16[72,1536]{1,0:T(8,128)(2,1)S(1)} %broadcast_select_fusion.1), channel_id=1, source_target_pairs={{0,2},{2,0},{1,3},{3,1},{4,6},{6,4},{5,7},{7,5},{8,10},{10,8},{9,1... | collective-permute-start | bytes 663560 | tf_op jit(solution)/shard_map/ppermute | solution.py:74
  72.3 14.3 %all-to-all-start.1 = ((bf16[8,252,128]{2,1,0:T(8,128)(2,1)}), bf16[8,252,128]{2,1,0:T(8,128)(2,1)S(1)}, u32[]{:S(2)}, u32[]{:S(2)}) async-start(bf16[8,252,128]{2,1,0:T(8,128)(2,1)} %reshape.26), calls=%async_computation.1 | async-start | bytes 1048576 | tf_op jit(solution)/shard_map/all_to_all | solution.py:83
  79.8 7.4 %copy-start = (bf16[192,1792]{1,0:T(8,128)(2,1)S(1)}, bf16[192,1792]{1,0:T(8,128)(2,1)}, u32[]{:S(2)}) copy-start(bf16[192,1792]{1,0:T(8,128)(2,1)} %cot.1) | copy-start | bytes 2064388
  79.8 7.4 %copy-start.1 = (bf16[72,192]{1,0:T(8,128)(2,1)S(1)}, bf16[72,192]{1,0:T(8,128)(2,1)}, u32[]{:S(2)}) copy-start(bf16[72,192]{1,0:T(8,128)(2,1)} %get-tuple-element.17.select) | copy-start | bytes 82948
  79.8 7.4 %copy-start.3 = (s32[192,8]{0,1:T(8,128)S(1)}, s32[192,8]{0,1:T(8,128)}, u32[]{:S(2)}) copy-start(s32[192,8]{0,1:T(8,128)} %param.10) | copy-start | bytes 18436
  79.9 7.4 %copy-start.4 = (s32[8]{0:T(128)S(1)}, s32[8]{0:T(128)}, u32[]{:S(2)}) copy-start(s32[8]{0:T(128)} %placement.1) | copy-start | bytes 100
  87.2 5.9 %copy-start.2 = (bf16[72,192]{1,0:T(8,128)(2,1)S(1)}, bf16[72,192]{1,0:T(8,128)(2,1)}, u32[]{:S(2)}) copy-start(bf16[72,192]{1,0:T(8,128)(2,1)} %get-tuple-element.18.weighted) | copy-start | bytes 82948
  88.2 6.4 %collective-permute-start.5 = (f32[8,192]{1,0:T(8,128)S(1)}, f32[8,192]{1,0:T(8,128)S(1)}, u32[]{:S(2)}, u32[]{:S(2)}) collective-permute-start(f32[8,192]{1,0:T(8,128)S(1)} %shard_map.139), channel_id=1, source_target_pairs={{0,1},{1,0},{2,3},{3,2},{4,5},{5,4},{6,7},{7,6},{8,9},{9,8},{10,11... | collective-permute-start | bytes 18440 | tf_op jit(solution)/shard_map/ppermute | solution.py:339

commit v4 on v3

--- a/solution.py
+++ b/solution.py
@@ -84,8 +84,7 @@
     return got.reshape(experts * CAP, cols)
 
 
-def call(kernel, outs, args, room, smem=0, hbm=0, scratch=(), flops=0):
-    space = pl.ANY if scratch else pltpu.VMEM
+def call(kernel, outs, args, room, smem=0, far=0, scratch=(), flops=0):
     moved = sum(a.size * a.dtype.itemsize for a in args) + sum(
         o.size * o.dtype.itemsize for o in outs
     )
@@ -93,11 +92,11 @@
         kernel,
         out_shape=outs,
         in_specs=[pl.BlockSpec(memory_space=pltpu.SMEM)] * smem
-        + [pl.BlockSpec(memory_space=pltpu.HBM)] * hbm
-        + [pl.BlockSpec(memory_space=space)] * (len(args) - smem - hbm),
+        + [pl.BlockSpec(memory_space=pl.ANY)] * far
+        + [pl.BlockSpec(memory_space=pltpu.VMEM)] * (len(args) - smem - far),
         out_specs=[pl.BlockSpec(memory_space=pltpu.VMEM)] * len(outs),
         scratch_shapes=scratch,
-        compiler_params=pltpu.CompilerParams(vmem_limit_bytes=None if scratch else room),
+        compiler_params=pltpu.CompilerParams(vmem_limit_bytes=room),
         cost_estimate=pl.CostEstimate(flops=flops, bytes_accessed=moved, transcendentals=0),
     )(*args)
 
@@ -159,58 +158,104 @@
     rows[:, half:] = jnp.dot(scaled, cot[...], preferred_element_type=F32).astype(BF)
 
 
-def expert_kernel(n_d, n_t, *refs):
-    shards, rows_in = refs[: 3 * n_d], refs[3 * n_d : 3 * n_d + n_t]
-    refs = refs[3 * n_d + n_t :]
-    units_out, terms, (w, x, w_sems, x_sems) = refs[0], refs[1 : 1 + n_t], refs[1 + n_t :]
-    d, t = lax.axis_index("dp"), lax.axis_index("tensor")
-    chunk, units = w.shape[2:]
-    half = x.shape[2] // 2
-    group = n_d // n_t
-    x_copies = fetch(
-        [(rows_in[s], x.at[lax.rem(t - s + n_t, n_t)]) for s in range(n_t)], x_sems
-    )
-    w_copies = fetch(
-        [
-            (shards[which * n_d + s], w.at[which, lax.rem(d - s + n_d, n_d)])
-            for which in range(3)
-            for s in range(n_d)
-        ],
-        w_sems,
-    )
-    for copy in x_copies:
-        copy.wait()
-
-    def product(which, offset):
-        for copy in w_copies[which * n_d : (which + 1) * n_d]:
-            copy.wait()
+class Rows:
+    def __init__(self, n_d, n_t, own, others, kept):
+        self.n_d, self.n_t, self.kept = n_d, n_t, kept
+        self.group = n_d // n_t
+        self.d, self.t = lax.axis_index("dp"), lax.axis_index("tensor")
+        self.half = kept.shape[2]
+        self.chunk = self.half // self.group
+        kept[self.t] = own
+        for s in range(1, n_t):
+            kept[lax.rem(self.t - s + n_t, n_t)] = others[s - 1][...]
+
+    def place(self, s):
+        where = lax.rem(self.d - s + self.n_d, self.n_d)
+        if self.group == 1:
+            return where, slice(None)
+        col = pl.multiple_of(lax.rem(where, self.group) * self.chunk, LANES)
+        return where // self.group, pl.ds(col, self.chunk)
+
+    def times(self, weight):
         value = None
-        for s in range(n_d):
-            cols = pl.ds(offset + (s % group) * chunk, chunk)
-            part = jnp.dot(x[s // group, :, cols], w[which, s], preferred_element_type=F32)
+        for s in range(self.n_d):
+            side, cols = self.place(s)
+            part = jnp.dot(self.kept[side, :, cols], weight(s), preferred_element_type=F32)
             value = part if value is None else value + part
         return value
 
-    gate, up = product(0, 0), product(1, 0)
+    def store(self, s, term, results):
+        side, cols = self.place(s)
+        step = lax.rem(side - self.t + self.n_t, self.n_t)
+        for k in range(self.n_t):
+
+            @pl.when(step == k)
+            def _():
+                results[k][:, cols] = term.astype(BF)
+
+
+class Weights:
+    def __init__(self, n_d, shards, room, sems, order):
+        self.n_d, self.room, self.waited = n_d, room, set()
+        keys = [(which, s) for which in order for s in range(n_d)]
+        pairs = [(shards[which * n_d + s], room.at[which, s]) for which, s in keys]
+        self.copies = dict(zip(keys, fetch(pairs, sems)))
+
+    def of(self, which):
+        def shard(s):
+            if (which, s) not in self.waited:
+                self.copies[which, s].wait()
+                self.waited.add((which, s))
+            return self.room[which, s]
+
+        return shard
+
+
+def forward_kernel(n_d, n_t, *refs):
+    shards, own, others = refs[: 3 * n_d], refs[3 * n_d], refs[3 * n_d + 1 : 3 * n_d + n_t]
+    refs = refs[3 * n_d + n_t :]
+    (gate_out, up_out, hidden_out), terms, (kept, room, sems) = refs[:3], refs[3:-3], refs[-3:]
+    weights = Weights(n_d, shards, room, sems, (0, 1, 2))
+    rows = Rows(n_d, n_t, own[:, : kept.shape[2]], others, kept)
+    gate, up = rows.times(weights.of(0)), rows.times(weights.of(1))
+    hidden = (gate * jax.nn.sigmoid(gate) * up).astype(BF)
+    gate_out[...], up_out[...], hidden_out[...] = gate, up, hidden
+    down = weights.of(2)
+    for s in range(n_d):
+        rows.store(s, dot(hidden, down(s), inner), terms)
+
+
+def backward_kernel(n_d, n_t, *refs):
+    shards, own, others = refs[: 3 * n_d], refs[3 * n_d], refs[3 * n_d + 1 : 3 * n_d + n_t]
+    refs = refs[3 * n_d + n_t :]
+    (gate_in, up_in, hidden_in, units_out), terms = refs[:4], refs[4:-3]
+    kept, room, sems = refs[-3:]
+    weights = Weights(n_d, shards, room, sems, (2, 0, 1))
+    rows = Rows(n_d, n_t, own[:, kept.shape[2] :], others, kept)
+    d_hidden = rows.times(weights.of(2))
+    gate, up = gate_in[...], up_in[...]
     sig = jax.nn.sigmoid(gate)
-    hidden = (gate * sig * up).astype(BF)
-    d_hidden = product(2, half)
     d_gate = (d_hidden * up * sig * (1.0 + gate * (1.0 - sig))).astype(BF)
     d_up = (d_hidden * gate * sig).astype(BF)
+    units = gate.shape[1]
     units_out[:, :units] = d_gate
     units_out[:, units : 2 * units] = d_up
-    units_out[:, 2 * units :] = hidden
+    units_out[:, 2 * units :] = hidden_in[...]
+    by_gate = [dot(d_gate, weights.of(0)(s), inner) for s in range(n_d)]
     for s in range(n_d):
-        out = dot(hidden, w[2, s], inner).astype(BF)
-        back = (dot(d_gate, w[0, s], inner) + dot(d_up, w[1, s], inner)).astype(BF)
-        col = (s % group) * chunk
-        step = lax.rem(s // group - t + n_t, n_t)
-        for k in range(n_t):
-
-            @pl.when(step == k)
-            def _():
-                terms[k][:, col : col + chunk] = out
-                terms[k][:, half + col : half + col + chunk] = back
+        rows.store(s, by_gate[s] + dot(d_up, weights.of(1)(s), inner), terms)
+
+
+def home_kernel(*refs):
+    home = refs[-1]
+    count = (len(refs) - 1) // 2
+    half = home.shape[1] // 2
+    for side in range(2):
+        value = None
+        for ref in refs[side * count : (side + 1) * count]:
+            part = ref[...].astype(F32)
+            value = part if value is None else value + part
+        home[:, side * half : (side + 1) * half] = value.astype(BF)
 
 
 def gate_kernel(placement, routes, select, cot, back, gate_part):
@@ -289,8 +334,8 @@
         head_kernel,
         outs,
         given,
-        room_for(tokens, cotangent, *outs),
-        hbm=len(given),
+        None,
+        far=len(given),
         scratch=[
             pltpu.SMEM(placement.shape, jnp.int32),
             *(pltpu.VMEM(x.shape, x.dtype) for x in given[1:]),
@@ -299,32 +344,48 @@
     )
     arrived = exchanged(outgoing, experts)
 
-    others = lay.flipped([arrived] * (lay.n_t - 1))
+    own_weights = (wg, wu, wd)
     shards = []
-    for own in (wg, wu, wd):
+    for own in own_weights:
         shards += [own, *lay.others(own)]
-    weights_room = shape((3, lay.n_d, chunk, units), BF)
-    rows_room = shape((lay.n_t, slots_all, 2 * half_width), BF)
-    outs = [shape((slots_all, 3 * units), BF)]
-    outs += [shape((slots_all, 2 * half_width), BF)] * lay.n_t
-    units_own, *terms = call(
-        lambda *refs: expert_kernel(lay.n_d, lay.n_t, *refs),
-        outs,
-        (*shards, arrived, *others),
-        room_for(weights_room, rows_room, *outs),
-        hbm=len(shards),
-        scratch=[
-            pltpu.VMEM(weights_room.shape, BF),
-            pltpu.VMEM(rows_room.shape, BF),
-            pltpu.SemaphoreType.DMA((3 * lay.n_d,)),
-            pltpu.SemaphoreType.DMA((lay.n_t,)),
-        ],
-        flops=12 * slots_all * lay.n_d * chunk * units,
-    )
-    home = terms[0].astype(F32)
-    for got in lay.flipped(terms[1:]):
-        home = home + got.astype(F32)
-    back = exchanged(home.astype(BF), experts)
+    x_other = lay.flipped([arrived[:, :half_width]] * (lay.n_t - 1))
+    d_other = lay.flipped([arrived[:, half_width:]] * (lay.n_t - 1))
+    term = shape((slots_all, half_width), BF)
+    kept = [
+        pltpu.VMEM((lay.n_t, slots_all, half_width), BF),
+        pltpu.VMEM((3, lay.n_d, chunk, units), BF),
+        pltpu.SemaphoreType.DMA((3 * lay.n_d,)),
+    ]
+    outs = [shape((slots_all, units), F32)] * 2 + [shape((slots_all, units), BF)]
+    room = None
+    work = 6 * slots_all * lay.n_d * chunk * units
+    gate, up, hidden, *out_terms = call(
+        lambda *refs: forward_kernel(lay.n_d, lay.n_t, *refs),
+        outs + [term] * lay.n_t,
+        (*shards, arrived, *x_other),
+        room,
+        scratch=kept,
+        far=len(shards),
+        flops=work,
+    )
+    units_own, *in_terms = call(
+        lambda *refs: backward_kernel(lay.n_d, lay.n_t, *refs),
+        [shape((slots_all, 3 * units), BF)] + [term] * lay.n_t,
+        (*shards, arrived, *d_other, gate, up, hidden),
+        room,
+        scratch=kept,
+        far=len(shards),
+        flops=work,
+    )
+    out_got = [out_terms[0], *lay.flipped(out_terms[1:])]
+    in_got = [in_terms[0], *lay.flipped(in_terms[1:])]
+    (home,) = call(
+        home_kernel,
+        [shape((slots_all, 2 * half_width), BF)],
+        (*out_got, *in_got),
+        room_for(*out_got, *in_got),
+    )
+    back = exchanged(home, experts)
 
     gate_shape = shape((top_count, tok_count), F32)
     (gate_part,) = call(

time: 95.6 us -> 115 us (1.20)
  waiting for transfers between devices: 29.4 us -> 38.5 us
  Pallas kernels: 19.9 us -> 24.5 us
  starting transfers between devices: 14.2 us -> 17.2 us
  local copies, waits for them, and re-layouts: 5.74 us -> 8.16 us
    all_to_all x1, waiting for transfers between devices: 6.65 us -> 14.6 us  [exchanged(): lax.all_to_all(flat, 'expert', split_axis=0, concat_axis=0, tiled=True)]
    pallas_call x4 -> x6, Pallas kernels: 16.6 us -> 21.2 us  [call(): pl.pallas_call(kernel, out_shape=outs, in_specs=[pl.BlockSpec(memory_spac...]
    ppermute x2 -> x4, waiting for transfers between devices: 14.6 us -> 19 us  [flipped(): got.append(lax.ppermute(values[step - 1], 'tensor', route))]
    ppermute x2, waiting for transfers between devices: 2.76 us -> 0.01 us  [spread(): blocks.append(lax.ppermute(chunk, ('dp', 'tensor'), self.pairs(step)))]
    ppermute x2 -> x4, starting transfers between devices: 3.1 us -> 5.33 us  [flipped(): got.append(lax.ppermute(values[step - 1], 'tensor', route))]
    ppermute x1, starting transfers between devices: 1.6 us -> 2.79 us  [on_device(): lax.ppermute(gate_part, 'tensor', [(i, (i + step) % lay.n_t) for i in ran...]
  transfers between devices with their start and end apart: 12 -> 14, of which waited for: 5 -> 5; matrix products, arithmetic and copies ran while one was open for 6% -> 7% of each run, Pallas kernels for 20% -> 21%
where the time goes in v4:
time: 115 us; the launch traced here: 114 us
  waiting for transfers between devices  38.5 us (33%)
  Pallas kernels  24.5 us (21%)
  blocking collectives  21.8 us (19%)
  starting transfers between devices  17.2 us (15%)
  local copies, waits for them, and re-layouts  8.16 us (7%)
  other arithmetic  2.51 us (2%)
  between operations  1.55 us (1%)
    all_to_all x1, blocking collectives, exchanged(): lax.all_to_all(flat, 'expert', split_axis=0, concat_axis=0, tiled=True)  21.8 us
    pallas_call x6, Pallas kernels, call(): pl.pallas_call(kernel, out_shape=outs, in_specs=[pl.BlockSpec(memory_spac...  21.2 us
    ppermute x4, waiting for transfers between devices, flipped(): got.append(lax.ppermute(values[step - 1], 'tensor', route))  19 us
    all_to_all x1, waiting for transfers between devices, exchanged(): lax.all_to_all(flat, 'expert', split_axis=0, concat_axis=0, tiled=True)  14.6 us
    ppermute x4, starting transfers between devices, flipped(): got.append(lax.ppermute(values[step - 1], 'tensor', route))  5.33 us
    ppermute x1, waiting for transfers between devices, on_device(): units_moved = lax.ppermute(units_own, 'expert', partner)  4.84 us
    all_to_all x1, starting transfers between devices, exchanged(): lax.all_to_all(flat, 'expert', split_axis=0, concat_axis=0, tiled=True)  3.58 us
    pallas_call x1, Pallas kernels, weight_grads(): pl.pallas_call(grads_kernel, grid=(steps,), out_shape=[out] * 3, in_specs...  3.3 us
  transfers between devices with their start and end apart: 14, of which 5 were waited for; matrix products, arithmetic and copies ran while one was open for 7% of the time, Pallas kernels for 21%

profile of v4, /device:TPU:0, one launch (start us, length us, event | category | flops | bytes accessed | tf_op | source)
XLA Modules:
  0.0 114.1 jit_solution(7195852891597017164)
XLA Ops:
  0.6 0.6 collective-permute-start
  1.7 2.5 %shard_map.136 = (bf16[72,3584]{1,0:T(8,128)(2,1)}, bf16[72,192]{1,0:T(8,128)(2,1)}, bf16[72,192]{1,0:T(8,128)(2,1)}) custom-call(s32[8]{0:T(128)} %placement.1, s32[8,192]{1,0:T(8,128)} %bitcast.10, bf16[8,192]{1,0:T(8,128)(2,1)} %bitcast.21, bf16[192,1792]{1,0:T(8,128)(2,1)} %refs_3_.1, bf16[192,1792]{1,0:T(8,128)(2,1)} %cot.1), custom_call_target="tpu_custom_call" | custom-call | bytes 1956896 | tf_op jit(solution)/shard_map/pallas_call | solution.py:91
  4.2 1.7 %reshape.24 = bf16[8,252,128]{2,1,0:T(8,128)(2,1)S(1)} reshape(bf16[72,3584]{1,0:T(8,128)(2,1)} %get-tuple-element.24) | data formatting | bytes 1032192 | tf_op jit(solution)/shard_map/reshape | solution.py:82
  5.9 21.8 %all_to_all.10 = bf16[8,252,128]{2,1,0:T(8,128)(2,1)S(1)} all-to-all(bf16[8,252,128]{2,1,0:T(8,128)(2,1)S(1)} %reshape.24), channel_id=1, replica_groups=mesh['expert'=8,'dp'=2,'tensor'=2] {'expert'}, dimensions={0} | all-to-all | bytes 1032192 | tf_op jit(solution)/shard_map/all_to_all | solution.py:83
  27.6 1.4 %reshape.25.refs_6_ = bf16[72,3584]{1,0:T(8,128)(2,1)} reshape(bf16[8,252,128]{2,1,0:T(8,128)(2,1)S(1)} %all_to_all.10) | data formatting | bytes 1032192 | tf_op jit(solution)/shard_map/reshape | solution.py:84
  29.0 1.1 fusion.1
  30.1 1.6 %collective-permute-start.3 = (bf16[72,1792]{1,0:T(8,128)(2,1)S(1)}, bf16[72,1792]{1,0:T(8,128)(2,1)S(1)}, u32[]{:S(2)}, u32[]{:S(2)}) collective-permute-start(bf16[72,1792]{1,0:T(8,128)(2,1)S(1)} %get-tuple-element.39), channel_id=1, source_target_pairs={{0,1},{1,0},{2,3},{3,2},{4,5},{5,4},{6,7},{7,6},{8,9},{9,8},{10,11... | collective-permute-start | bytes 774152 | tf_op jit(solution)/shard_map/ppermute | solution.py:62
  31.7 0.9 collective-permute-start.8
  32.6 5.0 %collective-permute-done.3.refs_7_ = bf16[72,1792]{1,0:T(8,128)(2,1)S(1)} collective-permute-done((bf16[72,1792]{1,0:T(8,128)(2,1)S(1)}, bf16[72,1792]{1,0:T(8,128)(2,1)S(1)}, u32[]{:S(2)}, u32[]{:S(2)}) %collective-permute-start.3) | collective-permute-done | bytes 258080 | tf_op jit(solution)/shard_map/ppermute | solution.py:62
  37.6 1.5 %collective-permute-start.5 = (bf16[72,1792]{1,0:T(8,128)(2,1)S(1)}, bf16[72,1792]{1,0:T(8,128)(2,1)S(1)}, u32[]{:S(2)}, u32[]{:S(2)}) collective-permute-start(bf16[72,1792]{1,0:T(8,128)(2,1)S(1)} %get-tuple-element.38), channel_id=1, source_target_pairs={{0,1},{1,0},{2,3},{3,2},{4,5},{5,4},{6,7},{7,6},{8,9},{9,8},{10,11... | collective-permute-start | bytes 774152 | tf_op jit(solution)/shard_map/ppermute | solution.py:62
  39.1 0.6 fusion
  40.5 1.2 %copy-done.7 = bf16[1792,512]{1,0:T(8,128)(2,1)} copy-done((bf16[1792,512]{1,0:T(8,128)(2,1)}, bf16[1792,512]{1,0:T(8,128)(2,1)S(1)}, u32[]{:S(2)}) %copy-start.7) | copy-done | bytes 1835032
  41.6 7.5 %shard_map.137 = (f32[72,512]{1,0:T(8,128)}, f32[72,512]{1,0:T(8,128)}, bf16[72,512]{1,0:T(8,128)(2,1)}, bf16[72,1792]{1,0:T(8,128)(2,1)}, bf16[72,1792]{1,0:T(8,128)(2,1)}) custom-call(bf16[1792,512]{1,0:T(8,128)(2,1)} %bitcast.13, bf16[1792,512]{1,0:T(8,128)(2,1)} %copy-done.7, bf16[1792,512]{1,0:T(8,128)(2,1)} %bitcast.16, ...), custom_call_target="tpu_custom_call" | custom-call | flops 792723456 | bytes 12668928 | tf_op jit(solution)/shard_map/pallas_call | solution.py:91
  49.2 0.7 copy-done.8
  49.9 8.7 %shard_map.138 = (bf16[72,1536]{1,0:T(8,128)(2,1)}, bf16[72,1792]{1,0:T(8,128)(2,1)}, bf16[72,1792]{1,0:T(8,128)(2,1)}) custom-call(bf16[1792,512]{1,0:T(8,128)(2,1)} %bitcast.14, bf16[1792,512]{1,0:T(8,128)(2,1)} %copy-done.7, bf16[1792,512]{1,0:T(8,128)(2,1)} %bitcast.17, bf16[1792,512]{1,0:T(8,128)(2,1)} %collective-permute-done.1.refs_3_, ...), custom_call_target="tpu_custom_call" | custom-call | flops 792723456 | bytes 12890112 | tf_op jit(solution)/shard_map/pallas_call | solution.py:91
  58.5 1.5 %collective-permute-start.11 = (bf16[72,1536]{1,0:T(8,128)(2,1)}, bf16[72,1536]{1,0:T(8,128)(2,1)S(1)}, u32[]{:S(2)}, u32[]{:S(2)}) collective-permute-start(bf16[72,1536]{1,0:T(8,128)(2,1)} %get-tuple-element.34), channel_id=1, source_target_pairs={{0,16},{4,20},{8,24},{12,28},{16,0},{20,4},{24,8},{28,12},{1,17},{... | collective-permute-start | bytes 663560 | tf_op jit(solution)/shard_map/ppermute | solution.py:419
  60.1 0.5 collective-permute-start.10
  60.7 1.5 %collective-permute-start.9 = (bf16[72,3584]{1,0:T(8,128)(2,1)S(1)}, bf16[72,3584]{1,0:T(8,128)(2,1)}, u32[]{:S(2)}, u32[]{:S(2)}) collective-permute-start(bf16[72,3584]{1,0:T(8,128)(2,1)S(1)} %broadcast_select_fusion), channel_id=1, source_target_pairs={{0,0},{2,1},{1,2},{3,3},{4,4},{6,5},{5,6},{7,7},{8,8},{10,9},{9,10... | collective-permute-start | bytes 1548296 | tf_op jit(solution)/shard_map/ppermute | solution.py:55
  62.1 2.1 %collective-permute-start.6 = (bf16[72,1792]{1,0:T(8,128)(2,1)}, bf16[72,1792]{1,0:T(8,128)(2,1)S(1)}, u32[]{:S(2)}, u32[]{:S(2)}) collective-permute-start(bf16[72,1792]{1,0:T(8,128)(2,1)} %get-tuple-element.31), channel_id=1, source_target_pairs={{0,1},{1,0},{2,3},{3,2},{4,5},{5,4},{6,7},{7,6},{8,9},{9,8},{10,11... | collective-permute-start | bytes 774152 | tf_op jit(solution)/shard_map/ppermute | solution.py:62
  64.4 4.8 %collective-permute-done.11 = bf16[72,1536]{1,0:T(8,128)(2,1)S(1)} collective-permute-done((bf16[72,1536]{1,0:T(8,128)(2,1)}, bf16[72,1536]{1,0:T(8,128)(2,1)S(1)}, u32[]{:S(2)}, u32[]{:S(2)}) %collective-permute-start.11) | collective-permute-done | bytes 221216 | tf_op jit(solution)/shard_map/ppermute | solution.py:419
  69.3 11.2 %collective-permute-done.6.refs_3_ = bf16[72,1792]{1,0:T(8,128)(2,1)S(1)} collective-permute-done((bf16[72,1792]{1,0:T(8,128)(2,1)}, bf16[72,1792]{1,0:T(8,128)(2,1)S(1)}, u32[]{:S(2)}, u32[]{:S(2)}) %collective-permute-start.6) | collective-permute-done | bytes 258080 | tf_op jit(solution)/shard_map/ppermute | solution.py:62
  80.6 2.8 %collective-permute-done.4.refs_1_ = bf16[72,1792]{1,0:T(8,128)(2,1)S(1)} collective-permute-done((bf16[72,1792]{1,0:T(8,128)(2,1)S(1)}, bf16[72,1792]{1,0:T(8,128)(2,1)S(1)}, u32[]{:S(2)}, u32[]{:S(2)}) %collective-permute-start.4) | collective-permute-done | bytes 258080 | tf_op jit(solution)/shard_map/ppermute | solution.py:62
  83.5 1.5 %reshape.26 = bf16[8,252,128]{2,1,0:T(8,128)(2,1)} reshape(bf16[72,3584]{1,0:T(8,128)(2,1)S(1)} %shard_map.139) | data formatting | bytes 1032192 | tf_op jit(solution)/shard_map/reshape | solution.py:82
  84.9 3.6 %all-to-all-start.1 = ((bf16[8,252,128]{2,1,0:T(8,128)(2,1)}), bf16[8,252,128]{2,1,0:T(8,128)(2,1)S(1)}, u32[]{:S(2)}, u32[]{:S(2)}) async-start(bf16[8,252,128]{2,1,0:T(8,128)(2,1)} %reshape.26), calls=%async_computation.1 | async-start | bytes 1048576 | tf_op jit(solution)/shard_map/all_to_all | solution.py:83
  88.5 1.1 pad_maximum_fusion.x.d
  89.8 14.6 %all-to-all-done.1 = bf16[8,252,128]{2,1,0:T(8,128)(2,1)S(1)} async-done(((bf16[8,252,128]{2,1,0:T(8,128)(2,1)}), bf16[8,252,128]{2,1,0:T(8,128)(2,1)S(1)}, u32[]{:S(2)}, u32[]{:S(2)}) %all-to-all-start.1) | async-done | bytes 516128 | tf_op jit(solution)/shard_map/all_to_all | solution.py:83
  104.4 0.6 reshape.27.back
  105.0 1.0 shard_map.141
  106.0 2.8 %collective-permute-start.7 = (f32[8,192]{1,0:T(8,128)S(1)}, f32[8,192]{1,0:T(8,128)S(1)}, u32[]{:S(2)}, u32[]{:S(2)}) collective-permute-start(f32[8,192]{1,0:T(8,128)S(1)} %shard_map.141), channel_id=1, source_target_pairs={{0,1},{1,0},{2,3},{3,2},{4,5},{5,4},{6,7},{7,6},{8,9},{9,8},{10,11... | collective-permute-start | bytes 18440 | tf_op jit(solution)/shard_map/ppermute | solution.py:400
  108.8 3.3 %weight_grads.1 = (bf16[1792,512]{1,0:T(8,128)(2,1)}, bf16[1792,512]{1,0:T(8,128)(2,1)}, bf16[1792,512]{1,0:T(8,128)(2,1)}) custom-call(bf16[144,3584]{1,0:T(8,128)(2,1)S(1)} %pad_maximum_fusion.x.d, bf16[144,3584]{1,0:T(8,128)(2,1)S(1)} %pad_maximum_fusion.x.d, bf16[144,1536]{1,0:T(8,128)(2,1)S(1)} %pad_maximum_fusion.1.units_ref), custom_call_target="tpu_custom_call" | custom-call | flops 792723456 | bytes 5505024 | tf_op jit(solution)/shard_map/weight_grads/pallas_call | solution.py:294
  112.1 1.5 %shard_map.140 = (bf16[192,1792]{1,0:T(8,128)(2,1)}, bf16[192,1792]{1,0:T(8,128)(2,1)}) custom-call(bf16[72,192]{1,0:T(8,128)(2,1)S(1)} %copy-done.3, bf16[72,192]{1,0:T(8,128)(2,1)S(1)} %copy-done.4, bf16[72,3584]{1,0:T(8,128)(2,1)S(1)} %reshape.27.back), custom_call_target="tpu_custom_call" | custom-call | bytes 1947648 | tf_op jit(solution)/shard_map/pallas_call | solution.py:91
  113.5 0.6 add_bitcast_fusion
  (40 shorter events, 1.0 us)
Async XLA Ops:
  0.6 39.8 %collective-permute-start = (bf16[1792,512]{1,0:T(8,128)(2,1)}, bf16[1792,512]{1,0:T(8,128)(2,1)S(1)}, u32[]{:S(2)}, u32[]{:S(2)}) collective-permute-start(bf16[1792,512]{1,0:T(8,128)(2,1)} %bitcast.12), channel_id=1, source_target_pairs={{0,2},{2,0},{1,3},{3,1},{4,6},{6,4},{5,7},{7,5},{8,10},{10,8},{9,1... | collective-permute-start | bytes 5505032 | tf_op jit(solution)/shard_map/ppermute | solution.py:69
  1.2 39.2 %collective-permute-start.1 = (bf16[1792,512]{1,0:T(8,128)(2,1)}, bf16[1792,512]{1,0:T(8,128)(2,1)}, u32[]{:S(2)}, u32[]{:S(2)}) collective-permute-start(bf16[1792,512]{1,0:T(8,128)(2,1)} %bitcast.15), channel_id=1, source_target_pairs={{0,2},{2,0},{1,3},{3,1},{4,6},{6,4},{5,7},{7,5},{8,10},{10,8},{9,1... | collective-permute-start | bytes 5505032 | tf_op jit(solution)/shard_map/ppermute | solution.py:69
  1.3 39.2 %collective-permute-start.2 = (bf16[1792,512]{1,0:T(8,128)(2,1)}, bf16[1792,512]{1,0:T(8,128)(2,1)}, u32[]{:S(2)}, u32[]{:S(2)}) collective-permute-start(bf16[1792,512]{1,0:T(8,128)(2,1)} %bitcast.18), channel_id=1, source_target_pairs={{0,2},{2,0},{1,3},{3,1},{4,6},{6,4},{5,7},{7,5},{8,10},{10,8},{9,1... | collective-permute-start | bytes 5505032 | tf_op jit(solution)/shard_map/ppermute | solution.py:69
  4.2 35.0 %copy-start.11 = (s32[8]{0:T(128)S(1)}, s32[8]{0:T(128)}, u32[]{:S(2)}) copy-start(s32[8]{0:T(128)} %param.14) | copy-start | bytes 100
  30.1 7.5 %collective-permute-start.3 = (bf16[72,1792]{1,0:T(8,128)(2,1)S(1)}, bf16[72,1792]{1,0:T(8,128)(2,1)S(1)}, u32[]{:S(2)}, u32[]{:S(2)}) collective-permute-start(bf16[72,1792]{1,0:T(8,128)(2,1)S(1)} %get-tuple-element.39), channel_id=1, source_target_pairs={{0,1},{1,0},{2,3},{3,2},{4,5},{5,4},{6,7},{7,6},{8,9},{9,8},{10,11... | collective-permute-start | bytes 774152 | tf_op jit(solution)/shard_map/ppermute | solution.py:62
  31.7 28.4 %collective-permute-start.8 = (bf16[72,3584]{1,0:T(8,128)(2,1)}, bf16[72,3584]{1,0:T(8,128)(2,1)S(1)}, u32[]{:S(2)}, u32[]{:S(2)}) collective-permute-start(bf16[72,3584]{1,0:T(8,128)(2,1)} %reshape.25.refs_6_), channel_id=1, source_target_pairs={{0,16},{4,20},{8,24},{12,28},{16,0},{20,4},{24,8},{28,12},{1,17},{... | collective-permute-start | bytes 1548296 | tf_op jit(solution)/shard_map/ppermute | solution.py:411
  37.6 2.8 %copy-start.9 = (bf16[72,1792]{1,0:T(8,128)(2,1)}, bf16[72,1792]{1,0:T(8,128)(2,1)S(1)}, u32[]{:S(2)}) copy-start(bf16[72,1792]{1,0:T(8,128)(2,1)S(1)} %collective-permute-done.3.refs_7_) | copy-start | bytes 774148
  37.6 11.5 %collective-permute-start.5 = (bf16[72,1792]{1,0:T(8,128)(2,1)S(1)}, bf16[72,1792]{1,0:T(8,128)(2,1)S(1)}, u32[]{:S(2)}, u32[]{:S(2)}) collective-permute-start(bf16[72,1792]{1,0:T(8,128)(2,1)S(1)} %get-tuple-element.38), channel_id=1, source_target_pairs={{0,1},{1,0},{2,3},{3,2},{4,5},{5,4},{6,7},{7,6},{8,9},{9,8},{10,11... | collective-permute-start | bytes 774152 | tf_op jit(solution)/shard_map/ppermute | solution.py:62
  40.4 1.2 %copy-start.7 = (bf16[1792,512]{1,0:T(8,128)(2,1)}, bf16[1792,512]{1,0:T(8,128)(2,1)S(1)}, u32[]{:S(2)}) copy-start(bf16[1792,512]{1,0:T(8,128)(2,1)S(1)} %collective-permute-done.refs_1_) | copy-start | bytes 5505028
  49.2 0.7 copy-start.8
  49.9 14.4 %copy-start.10 = (bf16[72,1792]{1,0:T(8,128)(2,1)S(1)}, bf16[72,1792]{1,0:T(8,128)(2,1)}, u32[]{:S(2)}) copy-start(bf16[72,1792]{1,0:T(8,128)(2,1)} %get-tuple-element.26) | copy-start | bytes 774148
  58.5 24.8 %copy-start.1 = (bf16[72,1792]{1,0:T(8,128)(2,1)S(1)}, bf16[72,1792]{1,0:T(8,128)(2,1)}, u32[]{:S(2)}) copy-start(bf16[72,1792]{1,0:T(8,128)(2,1)} %get-tuple-element.25.refs_0_) | copy-start | bytes 774148
  58.5 24.8 %copy-start.2 = (bf16[72,1792]{1,0:T(8,128)(2,1)S(1)}, bf16[72,1792]{1,0:T(8,128)(2,1)}, u32[]{:S(2)}) copy-start(bf16[72,1792]{1,0:T(8,128)(2,1)} %get-tuple-element.30.refs_2_) | copy-start | bytes 774148
  58.5 10.7 %collective-permute-start.11 = (bf16[72,1536]{1,0:T(8,128)(2,1)}, bf16[72,1536]{1,0:T(8,128)(2,1)S(1)}, u32[]{:S(2)}, u32[]{:S(2)}) collective-permute-start(bf16[72,1536]{1,0:T(8,128)(2,1)} %get-tuple-element.34), channel_id=1, source_target_pairs={{0,16},{4,20},{8,24},{12,28},{16,0},{20,4},{24,8},{28,12},{1,17},{... | collective-permute-start | bytes 663560 | tf_op jit(solution)/shard_map/ppermute | solution.py:419
  60.1 28.4 %collective-permute-start.10 = (bf16[72,3584]{1,0:T(8,128)(2,1)S(1)}, bf16[72,3584]{1,0:T(8,128)(2,1)S(1)}, u32[]{:S(2)}, u32[]{:S(2)}) collective-permute-start(bf16[72,3584]{1,0:T(8,128)(2,1)S(1)} %broadcast_select_fusion), channel_id=1, source_target_pairs={{2,0},{0,1},{3,2},{1,3},{6,4},{4,5},{7,6},{5,7},{10,8},{8,9},{11,1... | collective-permute-start | bytes 1548296 | tf_op jit(solution)/shard_map/ppermute | solution.py:55
  60.7 27.8 %collective-permute-start.9 = (bf16[72,3584]{1,0:T(8,128)(2,1)S(1)}, bf16[72,3584]{1,0:T(8,128)(2,1)}, u32[]{:S(2)}, u32[]{:S(2)}) collective-permute-start(bf16[72,3584]{1,0:T(8,128)(2,1)S(1)} %broadcast_select_fusion), channel_id=1, source_target_pairs={{0,0},{2,1},{1,2},{3,3},{4,4},{6,5},{5,6},{7,7},{8,8},{10,9},{9,10... | collective-permute-start | bytes 1548296 | tf_op jit(solution)/shard_map/ppermute | solution.py:55
  62.1 18.4 %collective-permute-start.6 = (bf16[72,1792]{1,0:T(8,128)(2,1)}, bf16[72,1792]{1,0:T(8,128)(2,1)S(1)}, u32[]{:S(2)}, u32[]{:S(2)}) collective-permute-start(bf16[72,1792]{1,0:T(8,128)(2,1)} %get-tuple-element.31), channel_id=1, source_target_pairs={{0,1},{1,0},{2,3},{3,2},{4,5},{5,4},{6,7},{7,6},{8,9},{9,8},{10,11... | collective-permute-start | bytes 774152 | tf_op jit(solution)/shard_map/ppermute | solution.py:62
  64.3 19.1 %collective-permute-start.4 = (bf16[72,1792]{1,0:T(8,128)(2,1)S(1)}, bf16[72,1792]{1,0:T(8,128)(2,1)S(1)}, u32[]{:S(2)}, u32[]{:S(2)}) collective-permute-start(bf16[72,1792]{1,0:T(8,128)(2,1)S(1)} %copy-done.10), channel_id=1, source_target_pairs={{0,1},{1,0},{2,3},{3,2},{4,5},{5,4},{6,7},{7,6},{8,9},{9,8},{10,11... | collective-permute-start | bytes 774152 | tf_op jit(solution)/shard_map/ppermute | solution.py:62
  69.2 20.4 %collective-permute-start.12 = (bf16[72,1536]{1,0:T(8,128)(2,1)S(1)}, bf16[72,1536]{1,0:T(8,128)(2,1)S(1)}, u32[]{:S(2)}, u32[]{:S(2)}) collective-permute-start(bf16[72,1536]{1,0:T(8,128)(2,1)S(1)} %broadcast_select_fusion.1), channel_id=1, source_target_pairs={{0,2},{2,0},{1,3},{3,1},{4,6},{6,4},{5,7},{7,5},{8,10},{10,8},{9,1... | collective-permute-start | bytes 663560 | tf_op jit(solution)/shard_map/ppermute | solution.py:74
  84.9 19.4 %all-to-all-start.1 = ((bf16[8,252,128]{2,1,0:T(8,128)(2,1)}), bf16[8,252,128]{2,1,0:T(8,128)(2,1)S(1)}, u32[]{:S(2)}, u32[]{:S(2)}) async-start(bf16[8,252,128]{2,1,0:T(8,128)(2,1)} %reshape.26), calls=%async_computation.1 | async-start | bytes 1048576 | tf_op jit(solution)/shard_map/all_to_all | solution.py:83
  89.6 15.3 %copy-start = (bf16[192,1792]{1,0:T(8,128)(2,1)S(1)}, bf16[192,1792]{1,0:T(8,128)(2,1)}, u32[]{:S(2)}) copy-start(bf16[192,1792]{1,0:T(8,128)(2,1)} %cot.1) | copy-start | bytes 2064388
  89.6 15.3 %copy-start.3 = (bf16[72,192]{1,0:T(8,128)(2,1)S(1)}, bf16[72,192]{1,0:T(8,128)(2,1)}, u32[]{:S(2)}) copy-start(bf16[72,192]{1,0:T(8,128)(2,1)} %get-tuple-element.22.select) | copy-start | bytes 82948
  89.7 15.3 %copy-start.5 = (s32[192,8]{0,1:T(8,128)S(1)}, s32[192,8]{0,1:T(8,128)}, u32[]{:S(2)}) copy-start(s32[192,8]{0,1:T(8,128)} %param.10) | copy-start | bytes 18436
  89.7 15.3 %copy-start.6 = (s32[8]{0:T(128)S(1)}, s32[8]{0:T(128)}, u32[]{:S(2)}) copy-start(s32[8]{0:T(128)} %placement.1) | copy-start | bytes 100
  105.0 7.1 %copy-start.4 = (bf16[72,192]{1,0:T(8,128)(2,1)S(1)}, bf16[72,192]{1,0:T(8,128)(2,1)}, u32[]{:S(2)}) copy-start(bf16[72,192]{1,0:T(8,128)(2,1)} %get-tuple-element.23.weighted) | copy-start | bytes 82948
  106.0 7.6 %collective-permute-start.7 = (f32[8,192]{1,0:T(8,128)S(1)}, f32[8,192]{1,0:T(8,128)S(1)}, u32[]{:S(2)}, u32[]{:S(2)}) collective-permute-start(f32[8,192]{1,0:T(8,128)S(1)} %shard_map.141), channel_id=1, source_target_pairs={{0,1},{1,0},{2,3},{3,2},{4,5},{5,4},{6,7},{7,6},{8,9},{9,8},{10,11... | collective-permute-start | bytes 18440 | tf_op jit(solution)/shard_map/ppermute | solution.py:400

commit v5 on v4

--- a/solution.py
+++ b/solution.py
@@ -6,6 +6,7 @@
 from jax.sharding import PartitionSpec as P
 
 CAP = 9
+MAIN = 8
 BF = jnp.bfloat16
 F32 = jnp.float32
 LANES = 128
@@ -77,11 +78,43 @@
         return lax.all_gather(value, "dp", axis=0, tiled=True)
 
 
-def exchanged(rows, experts):
-    cols = rows.shape[1]
-    flat = rows.reshape(experts, CAP * cols // LANES, LANES)
-    got = lax.all_to_all(flat, "expert", split_axis=0, concat_axis=0, tiled=True)
-    return got.reshape(experts * CAP, cols)
+def fold_width(cols):
+    return -(-cols // (MAIN * LANES)) * LANES
+
+
+def folded_shape(experts, cols):
+    return shape((experts * MAIN, cols + fold_width(cols)), BF)
+
+
+def fold(main, last, out):
+    rows, cols = main.shape
+    width = fold_width(cols)
+    out[:, :cols] = main.astype(BF)
+    row = lax.broadcasted_iota(jnp.int32, (rows, last.shape[0]), 0)
+    col = lax.broadcasted_iota(jnp.int32, (rows, last.shape[0]), 1)
+    repeat = jnp.where(row // MAIN == col, 1.0, 0.0).astype(BF)
+    wide = jnp.dot(repeat, last.astype(BF), preferred_element_type=F32)
+    place = lax.broadcasted_iota(jnp.int32, (rows, width), 0) % MAIN
+    value = jnp.zeros((rows, width), F32)
+    for q in range(cols // width):
+        value = jnp.where(place == q, wide[:, q * width : (q + 1) * width], value)
+    out[:, cols:] = value.astype(BF)
+
+
+def unfold(tail, cols):
+    rows, width = tail.shape
+    experts = rows // MAIN
+    row = lax.broadcasted_iota(jnp.int32, (experts, rows), 0)
+    col = lax.broadcasted_iota(jnp.int32, (experts, rows), 1)
+    pieces = []
+    for q in range(cols // width):
+        take = jnp.where(col == row * MAIN + q, 1.0, 0.0).astype(BF)
+        pieces.append(jnp.dot(take, tail, preferred_element_type=F32))
+    return jnp.concatenate(pieces, axis=1)
+
+
+def exchanged(rows):
+    return lax.all_to_all(rows, "expert", split_axis=0, concat_axis=0, tiled=True)
 
 
 def call(kernel, outs, args, room, smem=0, far=0, scratch=(), flops=0):
@@ -111,13 +144,13 @@
 
 def wanted_column(placement, slots):
     row = lax.broadcasted_iota(jnp.int32, (slots, 1), 0)
+    experts = slots // CAP
+    main = row < experts * MAIN
+    position = jnp.where(main, row // MAIN, row - experts * MAIN)
     wanted = jnp.zeros((slots, 1), jnp.int32)
-    base = jnp.zeros((slots, 1), jnp.int32)
-    for e in range(slots // CAP):
-        inside = row >= e * CAP
-        wanted = jnp.where(inside, placement[e], wanted)
-        base = jnp.where(inside, e * CAP, base)
-    return wanted, row - base
+    for e in range(experts):
+        wanted = jnp.where(position == e, placement[e], wanted)
+    return wanted, jnp.where(main, row % MAIN, MAIN)
 
 
 def fetch(pairs, sems):
@@ -135,7 +168,6 @@
         copy.wait()
     slots, tok_count = select.shape
     top_count = routes.shape[0]
-    half = tokens.shape[1]
     wanted, slot = wanted_column(placement, slots)
     hit = jnp.zeros((slots, tok_count), F32)
     weight = jnp.zeros((slots, tok_count), F32)
@@ -153,9 +185,37 @@
     select[...] = chosen
     weighted[...] = scaled
     copies[3].wait()
-    rows[:, :half] = jnp.dot(chosen, tokens[...], preferred_element_type=F32).astype(BF)
+    x = jnp.dot(chosen, tokens[...], preferred_element_type=F32)
     copies[4].wait()
-    rows[:, half:] = jnp.dot(scaled, cot[...], preferred_element_type=F32).astype(BF)
+    d = jnp.dot(scaled, cot[...], preferred_element_type=F32)
+    both = jnp.concatenate([x, d], axis=1)
+    main = rows.shape[0]
+    fold(both[:main], both[main:], rows)
+
+
+def split_kernel(rows, x, d):
+    main, half = rows.shape[0], x.shape[1]
+    last = unfold(rows[:, 2 * half :], 2 * half).astype(BF)
+    for side, out in ((0, x), (1, d)):
+        out[:main] = rows[:, side * half : (side + 1) * half]
+        out[main:] = last[:, side * half : (side + 1) * half]
+
+
+def held_kernel(flag, moved, own, out):
+    main, cols = own.shape[0], out.shape[1]
+    mine = flag[lax.axis_index("expert")] != 1
+
+    def put(ref):
+        out[:main] = ref[:, :cols]
+        out[main:] = unfold(ref[:, cols:], cols).astype(BF)
+
+    @pl.when(mine)
+    def _():
+        put(own)
+
+    @pl.when(jnp.logical_not(mine))
+    def _():
+        put(moved)
 
 
 class Rows:
@@ -216,7 +276,7 @@
     refs = refs[3 * n_d + n_t :]
     (gate_out, up_out, hidden_out), terms, (kept, room, sems) = refs[:3], refs[3:-3], refs[-3:]
     weights = Weights(n_d, shards, room, sems, (0, 1, 2))
-    rows = Rows(n_d, n_t, own[:, : kept.shape[2]], others, kept)
+    rows = Rows(n_d, n_t, own[...], others, kept)
     gate, up = rows.times(weights.of(0)), rows.times(weights.of(1))
     hidden = (gate * jax.nn.sigmoid(gate) * up).astype(BF)
     gate_out[...], up_out[...], hidden_out[...] = gate, up, hidden
@@ -231,7 +291,7 @@
     (gate_in, up_in, hidden_in, units_out), terms = refs[:4], refs[4:-3]
     kept, room, sems = refs[-3:]
     weights = Weights(n_d, shards, room, sems, (2, 0, 1))
-    rows = Rows(n_d, n_t, own[:, kept.shape[2] :], others, kept)
+    rows = Rows(n_d, n_t, own[...], others, kept)
     d_hidden = rows.times(weights.of(2))
     gate, up = gate_in[...], up_in[...]
     sig = jax.nn.sigmoid(gate)
@@ -249,20 +309,24 @@
 def home_kernel(*refs):
     home = refs[-1]
     count = (len(refs) - 1) // 2
-    half = home.shape[1] // 2
+    sides = []
     for side in range(2):
         value = None
         for ref in refs[side * count : (side + 1) * count]:
             part = ref[...].astype(F32)
             value = part if value is None else value + part
-        home[:, side * half : (side + 1) * half] = value.astype(BF)
+        sides.append(value)
+    both = jnp.concatenate(sides, axis=1)
+    main = home.shape[0]
+    fold(both[:main], both[main:], home)
 
 
 def gate_kernel(placement, routes, select, cot, back, gate_part):
     slots = select.shape[0]
     half = cot.shape[1]
     wanted, _ = wanted_column(placement, slots)
-    scores = dot(back[:, :half], cot[...], inner)
+    last = unfold(back[:, 2 * half :], 2 * half)[:, :half].astype(BF)
+    scores = jnp.concatenate([dot(back[:, :half], cot[...], inner), dot(last, cot[...], inner)])
     scores = jnp.where(select[...].astype(F32) > 0.0, scores, 0.0)
     for k in range(routes.shape[0]):
         match = routes[k : k + 1, :] == wanted
@@ -272,43 +336,53 @@
 
 
 def combine_kernel(select, weighted, back, layer_out, input_grad):
-    half = layer_out.shape[1]
-    layer_out[...] = dot(weighted[...], back[:, :half], contract).astype(BF)
-    input_grad[...] = dot(select[...], back[:, half:], contract).astype(BF)
-
-
-def grads_kernel(x, d, units_ref, g_gate, g_up, g_down):
+    main, half = back.shape[0], layer_out.shape[1]
+    last = unfold(back[:, 2 * half :], 2 * half).astype(BF)
+    for side, weight, out in ((0, weighted, layer_out), (1, select, input_grad)):
+        cols = slice(side * half, (side + 1) * half)
+        value = dot(weight[:main], back[:, cols], contract)
+        out[...] = (value + dot(weight[main:], last[:, cols], contract)).astype(BF)
+
+
+def grads_kernel(count, *refs):
+    held, kept_units, (g_gate, g_up, g_down) = refs[: 2 * count], refs[2 * count], refs[-3:]
     units = g_gate.shape[1]
-    both = dot(x[...], units_ref[:, : 2 * units], contract).astype(BF)
+
+    def joined(blocks):
+        return jnp.concatenate([x[...].astype(F32) for x in blocks]).astype(BF)
+
+    both = dot(joined(held[:count]), kept_units[:, : 2 * units], contract).astype(BF)
     g_gate[...] = both[:, :units]
     g_up[...] = both[:, units:]
-    g_down[...] = dot(d[...], units_ref[:, 2 * units :], contract).astype(BF)
+    g_down[...] = dot(joined(held[count:]), kept_units[:, 2 * units :], contract).astype(BF)
 
 
 def weight_grads(held, units_held, chunk, units):
-    rows = held.shape[0]
+    count, rows = len(held), held[0].shape[0]
     block = next(b for b in (896, 512, 256, LANES) if chunk % b == 0)
     steps = chunk // block
     out = shape((chunk, units), BF)
     spec = pl.BlockSpec((block, units), lambda i: (i, 0))
+    x_spec = pl.BlockSpec((rows, block), lambda i: (0, i))
+    d_spec = pl.BlockSpec((rows, block), lambda i: (0, i + steps))
     return pl.pallas_call(
-        grads_kernel,
+        lambda *refs: grads_kernel(count, *refs),
         grid=(steps,),
         out_shape=[out] * 3,
-        in_specs=[
-            pl.BlockSpec((rows, block), lambda i: (0, i)),
-            pl.BlockSpec((rows, block), lambda i: (0, i + steps)),
-            pl.BlockSpec((rows, 3 * units), lambda i: (0, 0)),
-        ],
+        in_specs=[x_spec] * count
+        + [d_spec] * count
+        + [pl.BlockSpec((count * rows, 3 * units), lambda i: (0, 0))],
         out_specs=[spec] * 3,
         compiler_params=pltpu.CompilerParams(
-            vmem_limit_bytes=(6 << 20) + 3 * rows * 2 * (3 * units + 2 * block)
+            vmem_limit_bytes=(12 << 20) + 6 * count * rows * 2 * (3 * units + 2 * block)
         ),
         cost_estimate=pl.CostEstimate(
-            flops=6 * rows * chunk * units, bytes_accessed=6 * chunk * units, transcendentals=0
+            flops=6 * count * rows * chunk * units,
+            bytes_accessed=6 * chunk * units,
+            transcendentals=0,
         ),
         name="weight_grads",
-    )(held, held, units_held)
+    )(*held, *held, units_held)
 
 
 def on_device(tokens, routes, gates, cotangent, placement, swap_flag, w_gate, w_up, w_down):
@@ -325,7 +399,7 @@
     routes_t, gates_t = routes.T, gates.T
 
     outs = [
-        shape((slots_all, 2 * half_width), BF),
+        folded_shape(experts, 2 * half_width),
         shape((slots_all, tok_count), BF),
         shape((slots_all, tok_count), BF),
     ]
@@ -342,14 +416,16 @@
             pltpu.SemaphoreType.DMA((len(given),)),
         ],
     )
-    arrived = exchanged(outgoing, experts)
+    arrived = exchanged(outgoing)
+    sides = [shape((slots_all, half_width), BF)] * 2
+    x_own, d_own = call(split_kernel, sides, (arrived,), room_for(*sides, *sides))
 
     own_weights = (wg, wu, wd)
     shards = []
     for own in own_weights:
         shards += [own, *lay.others(own)]
-    x_other = lay.flipped([arrived[:, :half_width]] * (lay.n_t - 1))
-    d_other = lay.flipped([arrived[:, half_width:]] * (lay.n_t - 1))
+    x_other = lay.flipped([x_own] * (lay.n_t - 1))
+    d_other = lay.flipped([d_own] * (lay.n_t - 1))
     term = shape((slots_all, half_width), BF)
     kept = [
         pltpu.VMEM((lay.n_t, slots_all, half_width), BF),
@@ -357,12 +433,12 @@
         pltpu.SemaphoreType.DMA((3 * lay.n_d,)),
     ]
     outs = [shape((slots_all, units), F32)] * 2 + [shape((slots_all, units), BF)]
-    room = None
+    room = 52 << 20
     work = 6 * slots_all * lay.n_d * chunk * units
     gate, up, hidden, *out_terms = call(
         lambda *refs: forward_kernel(lay.n_d, lay.n_t, *refs),
         outs + [term] * lay.n_t,
-        (*shards, arrived, *x_other),
+        (*shards, x_own, *x_other),
         room,
         scratch=kept,
         far=len(shards),
@@ -371,7 +447,7 @@
     units_own, *in_terms = call(
         lambda *refs: backward_kernel(lay.n_d, lay.n_t, *refs),
         [shape((slots_all, 3 * units), BF)] + [term] * lay.n_t,
-        (*shards, arrived, *d_other, gate, up, hidden),
+        (*shards, d_own, *d_other, gate, up, hidden),
         room,
         scratch=kept,
         far=len(shards),
@@ -381,11 +457,11 @@
     in_got = [in_terms[0], *lay.flipped(in_terms[1:])]
     (home,) = call(
         home_kernel,
-        [shape((slots_all, 2 * half_width), BF)],
+        [folded_shape(experts, 2 * half_width)],
         (*out_got, *in_got),
-        room_for(*out_got, *in_got),
-    )
-    back = exchanged(home, experts)
+        room_for(*out_got, *in_got, *out_got, *in_got),
+    )
+    back = exchanged(home)
 
     gate_shape = shape((top_count, tok_count), F32)
     (gate_part,) = call(
@@ -409,13 +485,16 @@
 
     partner = [(i, (i + experts // 2) % experts) for i in range(experts)]
     moved = lax.ppermute(arrived, "expert", partner)
-    held = jnp.where(my_flag, moved, arrived)
+    both = shape((slots_all, 2 * half_width), BF)
+    (held,) = call(
+        held_kernel, [both], (swap_flag, moved, arrived), room_for(both, both, both), smem=1
+    )
     if lay.group == 1:
         pieces = held[None]
     else:
         pieces = jnp.moveaxis(held.reshape(slots_all, 2, lay.group, chunk), 2, 0)
         pieces = pieces.reshape(lay.group, slots_all, 2 * chunk)
-    held = jnp.concatenate(lay.spread(pieces), axis=0)
+    held = lay.spread(pieces)
     units_moved = lax.ppermute(units_own, "expert", partner)
     units_held = jnp.where(my_flag, units_moved, units_own)
     units_held = lay.gathered(units_held)

time: 115 us -> 104 us (0.904)
  the two profiles are of different devices: /device:TPU:0 before, /device:TPU:28 now
where the time goes in v5:
time: 104 us; the launch traced here: 103 us
  waiting for transfers between devices  39.9 us (38%)
  Pallas kernels  22.9 us (22%)
  blocking collectives  18.5 us (18%)
  starting transfers between devices  16.1 us (15%)
  other arithmetic  3.06 us (3%)
  between operations  1.45 us (1%)
  local copies, waits for them, and re-layouts  1.25 us (1%)
    pallas_call x8, Pallas kernels, call(): pl.pallas_call(kernel, out_shape=outs, in_specs=[pl.BlockSpec(memory_spac...  19.6 us
    all_to_all x1, blocking collectives, exchanged(): lax.all_to_all(rows, 'expert', split_axis=0, concat_axis=0, tiled=True)  18.5 us
    ppermute x1, waiting for transfers between devices, on_device(): units_moved = lax.ppermute(units_own, 'expert', partner)  16.5 us
    ppermute x4, waiting for transfers between devices, flipped(): got.append(lax.ppermute(values[step - 1], 'tensor', route))  7.07 us
    ppermute x1, waiting for transfers between devices, on_device(): moved = lax.ppermute(arrived, 'expert', partner)  7.05 us
    ppermute x2, waiting for transfers between devices, spread(): blocks.append(lax.ppermute(chunk, ('dp', 'tensor'), self.pairs(step)))  6.91 us
    all_to_all x1, starting transfers between devices, exchanged(): lax.all_to_all(rows, 'expert', split_axis=0, concat_axis=0, tiled=True)  5.1 us
    ppermute x4, starting transfers between devices, flipped(): got.append(lax.ppermute(values[step - 1], 'tensor', route))  4.12 us
  transfers between devices with their start and end apart: 14, of which 6 were waited for; matrix products, arithmetic and copies ran while one was open for 2% of the time, Pallas kernels for 16%

profile of v5, /device:TPU:28, one launch (start us, length us, event | category | flops | bytes accessed | tf_op | source)
XLA Modules:
  0.0 103.2 jit_solution(5813031313627876349)
XLA Ops:
  0.7 0.5 collective-permute-start.1
  1.2 0.1 collective-permute-start.2
  1.3 2.6 %shard_map.136 = (bf16[64,4096]{1,0:T(8,128)(2,1)}, bf16[72,192]{1,0:T(8,128)(2,1)}, bf16[72,192]{1,0:T(8,128)(2,1)}) custom-call(s32[8]{0:T(128)} %placement.1, s32[8,192]{1,0:T(8,128)} %bitcast.19, bf16[8,192]{1,0:T(8,128)(2,1)} %bitcast.31, bf16[192,1792]{1,0:T(8,128)(2,1)} %refs_3_.1, bf16[192,1792]{1,0:T(8,128)(2,1)} %cot.1), custom_call_target="tpu_custom_call" | custom-call | bytes 1965088 | tf_op jit(solution)/shard_map/pallas_call | solution.py:124
  3.9 18.5 %all_to_all.22 = bf16[8,8,4096]{2,1,0:T(8,128)(2,1)S(1)} all-to-all(bf16[8,8,4096]{2,1,0:T(8,128)(2,1)} %bitcast.30), channel_id=1, replica_groups=mesh['expert'=8,'dp'=2,'tensor'=2] {'expert'}, dimensions={0} | all-to-all | bytes 1048576 | tf_op jit(solution)/shard_map/all_to_all | solution.py:117
  22.4 0.2 shard_map.137
  22.6 0.6 collective-permute-start.3
  23.1 1.5 %collective-permute-start.5 = (bf16[72,1792]{1,0:T(8,128)(2,1)S(1)}, bf16[72,1792]{1,0:T(8,128)(2,1)S(1)}, u32[]{:S(2)}, u32[]{:S(2)}) collective-permute-start(bf16[72,1792]{1,0:T(8,128)(2,1)S(1)} %get-tuple-element.30.refs_6_), channel_id=1, source_target_pairs={{0,1},{1,0},{2,3},{3,2},{4,5},{5,4},{6,7},{7,6},{8,9},{9,8},{10,11... | collective-permute-start | bytes 774152 | tf_op jit(solution)/shard_map/ppermute | solution.py:63
  24.6 7.1 %collective-permute-done.3.refs_7_ = bf16[72,1792]{1,0:T(8,128)(2,1)S(1)} collective-permute-done((bf16[72,1792]{1,0:T(8,128)(2,1)S(1)}, bf16[72,1792]{1,0:T(8,128)(2,1)S(1)}, u32[]{:S(2)}, u32[]{:S(2)}) %collective-permute-start.3) | collective-permute-done | bytes 258080 | tf_op jit(solution)/shard_map/ppermute | solution.py:63
  31.7 1.2 %copy-done.6 = bf16[1792,512]{1,0:T(8,128)(2,1)} copy-done((bf16[1792,512]{1,0:T(8,128)(2,1)}, bf16[1792,512]{1,0:T(8,128)(2,1)S(1)}, u32[]{:S(2)}) %copy-start.6) | copy-done | bytes 1835032
  32.9 5.5 %shard_map.138 = (f32[72,512]{1,0:T(8,128)S(1)}, f32[72,512]{1,0:T(8,128)S(1)}, bf16[72,512]{1,0:T(8,128)(2,1)S(1)}, bf16[72,1792]{1,0:T(8,128)(2,1)S(1)}, bf16[72,1792]{1,0:T(8,128)(2,1)S(1)}) custom-call(bf16[1792,512]{1,0:T(8,128)(2,1)} %bitcast.22, bf16[1792,512]{1,0:T(8,128)(2,1)} %copy-done.6, bf16[1792,512]{1,0:T(8,128)(2,1)} %bitcast.25, ...), custom_call_target="tpu_custom_call" | custom-call | flops 792723456 | bytes 12410880 | tf_op jit(solution)/shard_map/pallas_call | solution.py:124
  38.5 6.5 %shard_map.139 = (bf16[72,1536]{1,0:T(8,128)(2,1)S(1)}, bf16[72,1792]{1,0:T(8,128)(2,1)S(1)}, bf16[72,1792]{1,0:T(8,128)(2,1)S(1)}) custom-call(bf16[1792,512]{1,0:T(8,128)(2,1)} %bitcast.23, bf16[1792,512]{1,0:T(8,128)(2,1)} %copy-done.6, bf16[1792,512]{1,0:T(8,128)(2,1)} %bitcast.26, bf16[1792,512]{1,0:T(8,128)(2,1)} %collective-permute-done.1.refs_3_, ...), custom_call_target="tpu_custom_call" | custom-call | flops 792723456 | bytes 12632064 | tf_op jit(solution)/shard_map/pallas_call | solution.py:124
  44.9 2.4 %collective-permute-start.11 = (bf16[72,1536]{1,0:T(8,128)(2,1)S(1)}, bf16[72,1536]{1,0:T(8,128)(2,1)S(1)}, u32[]{:S(2)}, u32[]{:S(2)}) collective-permute-start(bf16[72,1536]{1,0:T(8,128)(2,1)S(1)} %get-tuple-element.38), channel_id=1, source_target_pairs={{0,16},{4,20},{8,24},{12,28},{16,0},{20,4},{24,8},{28,12},{1,17},{... | collective-permute-start | bytes 663560 | tf_op jit(solution)/shard_map/ppermute | solution.py:498
  47.3 0.6 fusion
  48.6 0.7 collective-permute-start.8
  49.3 0.5 collective-permute-start.6
  49.8 1.5 %collective-permute-start.4 = (bf16[72,1792]{1,0:T(8,128)(2,1)S(1)}, bf16[72,1792]{1,0:T(8,128)(2,1)S(1)}, u32[]{:S(2)}, u32[]{:S(2)}) collective-permute-start(bf16[72,1792]{1,0:T(8,128)(2,1)S(1)} %get-tuple-element.29), channel_id=1, source_target_pairs={{0,1},{1,0},{2,3},{3,2},{4,5},{5,4},{6,7},{7,6},{8,9},{9,8},{10,11... | collective-permute-start | bytes 774152 | tf_op jit(solution)/shard_map/ppermute | solution.py:63
  51.3 16.5 %collective-permute-done.11 = bf16[72,1536]{1,0:T(8,128)(2,1)S(1)} collective-permute-done((bf16[72,1536]{1,0:T(8,128)(2,1)S(1)}, bf16[72,1536]{1,0:T(8,128)(2,1)S(1)}, u32[]{:S(2)}, u32[]{:S(2)}) %collective-permute-start.11) | collective-permute-done | bytes 221216 | tf_op jit(solution)/shard_map/ppermute | solution.py:498
  67.8 0.7 broadcast_select_fusion
  68.6 1.2 %shard_map.140 = bf16[64,4096]{1,0:T(8,128)(2,1)} custom-call(bf16[72,1792]{1,0:T(8,128)(2,1)S(1)} %get-tuple-element.28.refs_0_, bf16[72,1792]{1,0:T(8,128)(2,1)S(1)} %collective-permute-done.4.refs_1_, bf16[72,1792]{1,0:T(8,128)(2,1)S(1)} %get-tuple-element.34.refs_2_, bf16[72,1792]{1,0:T(8,128)(2,1)S(1)} %collective-permute-done.6.refs_3_), custom_call_target="tpu_custom_call" | custom-call | bytes 1556480 | tf_op jit(solution)/shard_map/pallas_call | solution.py:124
  69.8 5.1 %all-to-all-start.1 = ((bf16[8,8,4096]{2,1,0:T(8,128)(2,1)}), bf16[8,8,4096]{2,1,0:T(8,128)(2,1)S(1)}, u32[]{:S(2)}, u32[]{:S(2)}) async-start(bf16[8,8,4096]{2,1,0:T(8,128)(2,1)} %bitcast.7), calls=%async_computation.1 | async-start | bytes 1048576 | tf_op jit(solution)/shard_map/all_to_all | solution.py:117
  74.9 7.1 %collective-permute-done.8.moved = bf16[64,4096]{1,0:T(8,128)(2,1)S(1)} collective-permute-done((bf16[64,4096]{1,0:T(8,128)(2,1)S(1)}, bf16[64,4096]{1,0:T(8,128)(2,1)S(1)}, u32[]{:S(2)}, u32[]{:S(2)}) %collective-permute-start.8) | collective-permute-done | bytes 524320 | tf_op jit(solution)/shard_map/ppermute | solution.py:487
  81.9 0.7 shard_map.143
  82.7 2.6 %collective-permute-start.9 = (bf16[72,3584]{1,0:T(8,128)(2,1)S(1)}, bf16[72,3584]{1,0:T(8,128)(2,1)S(1)}, u32[]{:S(2)}, u32[]{:S(2)}) collective-permute-start(bf16[72,3584]{1,0:T(8,128)(2,1)S(1)} %shard_map.143), channel_id=1, source_target_pairs={{0,0},{2,1},{1,2},{3,3},{4,4},{6,5},{5,6},{7,7},{8,8},{10,9},{9,10... | collective-permute-start | bytes 1548296 | tf_op jit(solution)/shard_map/ppermute | solution.py:56
  85.3 1.1 %broadcast_select_fusion.2 = (bf16[72,1536]{1,0:T(8,128)(2,1)S(1)}, bf16[72,1536]{1,0:T(8,128)(2,1)S(1)}) fusion(bf16[72,1536]{1,0:T(8,128)(2,1)} %broadcast_select_fusion, bf16[72,1536]{1,0:T(8,128)(2,1)} %collective-permute-done.12, pred[]{:T(512)S(6)} %eq.14), kind=kLoop, calls=%fused_computation.3 | loop fusion | flops 221184 | bytes 884737 | tf_op jit(solution)/shard_map/jit(_where)/select_n | solution.py:77
  86.5 2.3 %all-to-all-done.1 = bf16[8,8,4096]{2,1,0:T(8,128)(2,1)S(1)} async-done(((bf16[8,8,4096]{2,1,0:T(8,128)(2,1)}), bf16[8,8,4096]{2,1,0:T(8,128)(2,1)S(1)}, u32[]{:S(2)}, u32[]{:S(2)}) %all-to-all-start.1) | async-done | bytes 524320 | tf_op jit(solution)/shard_map/all_to_all | solution.py:117
  88.8 1.1 %shard_map.142 = f32[8,192]{1,0:T(8,128)S(1)} custom-call(s32[8]{0:T(128)S(1)} %copy-done.4, s32[8,192]{1,0:T(8,128)S(1)} %bitcast.20, bf16[72,192]{1,0:T(8,128)(2,1)S(1)} %copy-done.1, bf16[192,1792]{1,0:T(8,128)(2,1)S(1)} %copy-done, bf16[64,4096]{1,0:T(8,128)(2,1)S(1)} %bitcast.17), custom_call_target="tpu_custom_call" | custom-call | bytes 1252384 | tf_op jit(solution)/shard_map/pallas_call | solution.py:124
  90.0 0.6 collective-permute-start.7
  90.5 5.5 %collective-permute-done.10.refs_1_.refs_3_ = bf16[72,3584]{1,0:T(8,128)(2,1)S(1)} collective-permute-done((bf16[72,3584]{1,0:T(8,128)(2,1)S(1)}, bf16[72,3584]{1,0:T(8,128)(2,1)S(1)}, u32[]{:S(2)}, u32[]{:S(2)}) %collective-permute-start.10) | collective-permute-done | bytes 516128 | tf_op jit(solution)/shard_map/ppermute | solution.py:56
  96.0 1.4 %collective-permute-done.9.refs_0_.refs_2_ = bf16[72,3584]{1,0:T(8,128)(2,1)S(1)} collective-permute-done((bf16[72,3584]{1,0:T(8,128)(2,1)S(1)}, bf16[72,3584]{1,0:T(8,128)(2,1)S(1)}, u32[]{:S(2)}, u32[]{:S(2)}) %collective-permute-start.9) | collective-permute-done | bytes 516128 | tf_op jit(solution)/shard_map/ppermute | solution.py:56
  97.4 3.3 %weight_grads.1 = (bf16[1792,512]{1,0:T(8,128)(2,1)}, bf16[1792,512]{1,0:T(8,128)(2,1)}, bf16[1792,512]{1,0:T(8,128)(2,1)}) custom-call(bf16[72,3584]{1,0:T(8,128)(2,1)S(1)} %collective-permute-done.9.refs_0_.refs_2_, bf16[72,3584]{1,0:T(8,128)(2,1)S(1)} %collective-permute-done.10.refs_1_.refs_3_, ...), custom_call_target="tpu_custom_call" | custom-call | flops 792723456 | bytes 5505024 | tf_op jit(solution)/shard_map/weight_grads/pallas_call | solution.py:368
  100.7 1.8 %shard_map.141 = (bf16[192,1792]{1,0:T(8,128)(2,1)}, bf16[192,1792]{1,0:T(8,128)(2,1)}) custom-call(bf16[72,192]{1,0:T(8,128)(2,1)S(1)} %copy-done.1, bf16[72,192]{1,0:T(8,128)(2,1)S(1)} %copy-done.2, bf16[64,4096]{1,0:T(8,128)(2,1)S(1)} %bitcast.18), custom_call_target="tpu_custom_call" | custom-call | bytes 1955840 | tf_op jit(solution)/shard_map/pallas_call | solution.py:124
  102.6 0.6 add_bitcast_fusion
  (25 shorter events, 0.2 us)
Async XLA Ops:
  0.6 31.1 %collective-permute-start = (bf16[1792,512]{1,0:T(8,128)(2,1)}, bf16[1792,512]{1,0:T(8,128)(2,1)S(1)}, u32[]{:S(2)}, u32[]{:S(2)}) collective-permute-start(bf16[1792,512]{1,0:T(8,128)(2,1)} %bitcast.21), channel_id=1, source_target_pairs={{0,2},{2,0},{1,3},{3,1},{4,6},{6,4},{5,7},{7,5},{8,10},{10,8},{9,1... | collective-permute-start | bytes 5505032 | tf_op jit(solution)/shard_map/ppermute | solution.py:70
  0.7 31.0 %collective-permute-start.1 = (bf16[1792,512]{1,0:T(8,128)(2,1)}, bf16[1792,512]{1,0:T(8,128)(2,1)}, u32[]{:S(2)}, u32[]{:S(2)}) collective-permute-start(bf16[1792,512]{1,0:T(8,128)(2,1)} %bitcast.24), channel_id=1, source_target_pairs={{0,2},{2,0},{1,3},{3,1},{4,6},{6,4},{5,7},{7,5},{8,10},{10,8},{9,1... | collective-permute-start | bytes 5505032 | tf_op jit(solution)/shard_map/ppermute | solution.py:70
  1.2 31.7 %collective-permute-start.2 = (bf16[1792,512]{1,0:T(8,128)(2,1)}, bf16[1792,512]{1,0:T(8,128)(2,1)}, u32[]{:S(2)}, u32[]{:S(2)}) collective-permute-start(bf16[1792,512]{1,0:T(8,128)(2,1)} %bitcast.27), channel_id=1, source_target_pairs={{0,2},{2,0},{1,3},{3,1},{4,6},{6,4},{5,7},{7,5},{8,10},{10,8},{9,1... | collective-permute-start | bytes 5505032 | tf_op jit(solution)/shard_map/ppermute | solution.py:70
  22.6 9.2 %collective-permute-start.3 = (bf16[72,1792]{1,0:T(8,128)(2,1)S(1)}, bf16[72,1792]{1,0:T(8,128)(2,1)S(1)}, u32[]{:S(2)}, u32[]{:S(2)}) collective-permute-start(bf16[72,1792]{1,0:T(8,128)(2,1)S(1)} %get-tuple-element.27.refs_6_), channel_id=1, source_target_pairs={{0,1},{1,0},{2,3},{3,2},{4,5},{5,4},{6,7},{7,6},{8,9},{9,8},{10,11... | collective-permute-start | bytes 774152 | tf_op jit(solution)/shard_map/ppermute | solution.py:63
  23.1 15.3 %collective-permute-start.5 = (bf16[72,1792]{1,0:T(8,128)(2,1)S(1)}, bf16[72,1792]{1,0:T(8,128)(2,1)S(1)}, u32[]{:S(2)}, u32[]{:S(2)}) collective-permute-start(bf16[72,1792]{1,0:T(8,128)(2,1)S(1)} %get-tuple-element.30.refs_6_), channel_id=1, source_target_pairs={{0,1},{1,0},{2,3},{3,2},{4,5},{5,4},{6,7},{7,6},{8,9},{9,8},{10,11... | collective-permute-start | bytes 774152 | tf_op jit(solution)/shard_map/ppermute | solution.py:63
  31.7 1.2 %copy-start.6 = (bf16[1792,512]{1,0:T(8,128)(2,1)}, bf16[1792,512]{1,0:T(8,128)(2,1)S(1)}, u32[]{:S(2)}) copy-start(bf16[1792,512]{1,0:T(8,128)(2,1)S(1)} %collective-permute-done.refs_1_) | copy-start | bytes 5505028
  38.4 8.8 %copy-start.5 = (s32[8]{0:T(128)S(1)}, s32[8]{0:T(128)}, u32[]{:S(2)}) copy-start(s32[8]{0:T(128)} %flag.1) | copy-start | bytes 100
  44.9 22.9 %collective-permute-start.11 = (bf16[72,1536]{1,0:T(8,128)(2,1)S(1)}, bf16[72,1536]{1,0:T(8,128)(2,1)S(1)}, u32[]{:S(2)}, u32[]{:S(2)}) collective-permute-start(bf16[72,1536]{1,0:T(8,128)(2,1)S(1)} %get-tuple-element.38), channel_id=1, source_target_pairs={{0,16},{4,20},{8,24},{12,28},{16,0},{20,4},{24,8},{28,12},{1,17},{... | collective-permute-start | bytes 663560 | tf_op jit(solution)/shard_map/ppermute | solution.py:498
  48.6 33.4 %collective-permute-start.8 = (bf16[64,4096]{1,0:T(8,128)(2,1)S(1)}, bf16[64,4096]{1,0:T(8,128)(2,1)S(1)}, u32[]{:S(2)}, u32[]{:S(2)}) collective-permute-start(bf16[64,4096]{1,0:T(8,128)(2,1)S(1)} %bitcast.15), channel_id=1, source_target_pairs={{0,16},{4,20},{8,24},{12,28},{16,0},{20,4},{24,8},{28,12},{1,17},{... | collective-permute-start | bytes 1572872 | tf_op jit(solution)/shard_map/ppermute | solution.py:487
  49.3 19.3 %collective-permute-start.6 = (bf16[72,1792]{1,0:T(8,128)(2,1)S(1)}, bf16[72,1792]{1,0:T(8,128)(2,1)S(1)}, u32[]{:S(2)}, u32[]{:S(2)}) collective-permute-start(bf16[72,1792]{1,0:T(8,128)(2,1)S(1)} %get-tuple-element.35), channel_id=1, source_target_pairs={{0,1},{1,0},{2,3},{3,2},{4,5},{5,4},{6,7},{7,6},{8,9},{9,8},{10,11... | collective-permute-start | bytes 774152 | tf_op jit(solution)/shard_map/ppermute | solution.py:63
  49.8 18.8 %collective-permute-start.4 = (bf16[72,1792]{1,0:T(8,128)(2,1)S(1)}, bf16[72,1792]{1,0:T(8,128)(2,1)S(1)}, u32[]{:S(2)}, u32[]{:S(2)}) collective-permute-start(bf16[72,1792]{1,0:T(8,128)(2,1)S(1)} %get-tuple-element.29), channel_id=1, source_target_pairs={{0,1},{1,0},{2,3},{3,2},{4,5},{5,4},{6,7},{7,6},{8,9},{9,8},{10,11... | collective-permute-start | bytes 774152 | tf_op jit(solution)/shard_map/ppermute | solution.py:63
  68.5 16.8 %collective-permute-start.12 = (bf16[72,1536]{1,0:T(8,128)(2,1)}, bf16[72,1536]{1,0:T(8,128)(2,1)}, u32[]{:S(2)}, u32[]{:S(2)}) collective-permute-start(bf16[72,1536]{1,0:T(8,128)(2,1)} %broadcast_select_fusion), channel_id=1, source_target_pairs={{0,2},{2,0},{1,3},{3,1},{4,6},{6,4},{5,7},{7,5},{8,10},{10,8},{9,1... | collective-permute-start | bytes 663560 | tf_op jit(solution)/shard_map/ppermute | solution.py:75
  69.8 19.0 %all-to-all-start.1 = ((bf16[8,8,4096]{2,1,0:T(8,128)(2,1)}), bf16[8,8,4096]{2,1,0:T(8,128)(2,1)S(1)}, u32[]{:S(2)}, u32[]{:S(2)}) async-start(bf16[8,8,4096]{2,1,0:T(8,128)(2,1)} %bitcast.7), calls=%async_computation.1 | async-start | bytes 1048576 | tf_op jit(solution)/shard_map/all_to_all | solution.py:117
  74.9 13.9 %copy-start = (bf16[192,1792]{1,0:T(8,128)(2,1)S(1)}, bf16[192,1792]{1,0:T(8,128)(2,1)}, u32[]{:S(2)}) copy-start(bf16[192,1792]{1,0:T(8,128)(2,1)} %cot.1) | copy-start | bytes 2064388
  74.9 13.9 %copy-start.1 = (bf16[72,192]{1,0:T(8,128)(2,1)S(1)}, bf16[72,192]{1,0:T(8,128)(2,1)}, u32[]{:S(2)}) copy-start(bf16[72,192]{1,0:T(8,128)(2,1)} %get-tuple-element.24.select) | copy-start | bytes 82948
  74.9 13.9 %copy-start.3 = (s32[192,8]{0,1:T(8,128)S(1)}, s32[192,8]{0,1:T(8,128)}, u32[]{:S(2)}) copy-start(s32[192,8]{0,1:T(8,128)} %param.10) | copy-start | bytes 18436
  74.9 13.9 %copy-start.4 = (s32[8]{0:T(128)S(1)}, s32[8]{0:T(128)}, u32[]{:S(2)}) copy-start(s32[8]{0:T(128)} %placement.1) | copy-start | bytes 100
  82.7 13.3 %collective-permute-start.10 = (bf16[72,3584]{1,0:T(8,128)(2,1)S(1)}, bf16[72,3584]{1,0:T(8,128)(2,1)S(1)}, u32[]{:S(2)}, u32[]{:S(2)}) collective-permute-start(bf16[72,3584]{1,0:T(8,128)(2,1)S(1)} %shard_map.143), channel_id=1, source_target_pairs={{2,0},{0,1},{3,2},{1,3},{6,4},{4,5},{7,6},{5,7},{10,8},{8,9},{11,1... | collective-permute-start | bytes 1548296 | tf_op jit(solution)/shard_map/ppermute | solution.py:56
  82.7 14.7 %collective-permute-start.9 = (bf16[72,3584]{1,0:T(8,128)(2,1)S(1)}, bf16[72,3584]{1,0:T(8,128)(2,1)S(1)}, u32[]{:S(2)}, u32[]{:S(2)}) collective-permute-start(bf16[72,3584]{1,0:T(8,128)(2,1)S(1)} %shard_map.143), channel_id=1, source_target_pairs={{0,0},{2,1},{1,2},{3,3},{4,4},{6,5},{5,6},{7,7},{8,8},{10,9},{9,10... | collective-permute-start | bytes 1548296 | tf_op jit(solution)/shard_map/ppermute | solution.py:56
  88.8 11.9 %copy-start.2 = (bf16[72,192]{1,0:T(8,128)(2,1)S(1)}, bf16[72,192]{1,0:T(8,128)(2,1)}, u32[]{:S(2)}) copy-start(bf16[72,192]{1,0:T(8,128)(2,1)} %get-tuple-element.25.weighted) | copy-start | bytes 82948
  90.0 12.6 %collective-permute-start.7 = (f32[8,192]{1,0:T(8,128)S(1)}, f32[8,192]{1,0:T(8,128)S(1)}, u32[]{:S(2)}, u32[]{:S(2)}) collective-permute-start(f32[8,192]{1,0:T(8,128)S(1)} %shard_map.142), channel_id=1, source_target_pairs={{0,1},{1,0},{2,3},{3,2},{4,5},{5,4},{6,7},{7,6},{8,9},{9,8},{10,11... | collective-permute-start | bytes 18440 | tf_op jit(solution)/shard_map/ppermute | solution.py:476

commit v6 on v5

--- a/solution.py
+++ b/solution.py
@@ -201,21 +201,24 @@
         out[main:] = last[:, side * half : (side + 1) * half]
 
 
-def held_kernel(flag, moved, own, out):
+def held_kernel(flag, moved, near, own, out, both):
     main, cols = own.shape[0], out.shape[1]
-    mine = flag[lax.axis_index("expert")] != 1
-
-    def put(ref):
-        out[:main] = ref[:, :cols]
-        out[main:] = unfold(ref[:, cols:], cols).astype(BF)
+    half = main // 2
+    me = lax.axis_index("expert")
+    mine = flag[me] != 1
+    side = me // (lax.axis_size("expert") // 2)
 
     @pl.when(mine)
     def _():
-        put(own)
+        both[...] = own[...]
 
     @pl.when(jnp.logical_not(mine))
     def _():
-        put(moved)
+        both[pl.ds(pl.multiple_of(side * half, half), half)] = near[...]
+        both[pl.ds(pl.multiple_of((1 - side) * half, half), half)] = moved[...]
+
+    out[:main] = both[:, :cols]
+    out[main:] = unfold(both[:, cols:], cols).astype(BF)
 
 
 class Rows:
@@ -417,6 +420,21 @@
         ],
     )
     arrived = exchanged(outgoing)
+    half_axis = experts // 2
+    side = myself // half_axis
+
+    def of_half(rows, which):
+        count = half_axis * MAIN
+        return lax.dynamic_slice_in_dim(rows, which * count, count, axis=0)
+
+    near = lax.all_to_all(
+        of_half(outgoing, 1 - side),
+        "expert",
+        split_axis=0,
+        concat_axis=0,
+        axis_index_groups=[list(range(half_axis)), list(range(half_axis, experts))],
+        tiled=True,
+    )
     sides = [shape((slots_all, half_width), BF)] * 2
     x_own, d_own = call(split_kernel, sides, (arrived,), room_for(*sides, *sides))
 
@@ -484,10 +502,15 @@
     )
 
     partner = [(i, (i + experts // 2) % experts) for i in range(experts)]
-    moved = lax.ppermute(arrived, "expert", partner)
+    moved = lax.ppermute(of_half(arrived, side), "expert", partner)
     both = shape((slots_all, 2 * half_width), BF)
     (held,) = call(
-        held_kernel, [both], (swap_flag, moved, arrived), room_for(both, both, both), smem=1
+        held_kernel,
+        [both],
+        (swap_flag, moved, near, arrived),
+        room_for(both, both, both, both),
+        smem=1,
+        scratch=[pltpu.VMEM(arrived.shape, BF)],
     )
     if lay.group == 1:
         pieces = held[None]

time: 104 us -> 95.4 us (0.917)
  the two profiles are of different devices: /device:TPU:28 before, /device:TPU:0 now
where the time goes in v6:
time: 95.4 us; the launch traced here: 94.9 us
  waiting for transfers between devices  39.6 us (42%)
  starting transfers between devices  26.9 us (28%)
  Pallas kernels  23.9 us (25%)
  local copies, waits for them, and re-layouts  1.72 us (2%)
  between operations  1.48 us (2%)
  other arithmetic  1.34 us (1%)
    all_to_all x2, waiting for transfers between devices, exchanged(): lax.all_to_all(rows, 'expert', split_axis=0, concat_axis=0, tiled=True)  26.3 us
    pallas_call x8, Pallas kernels, call(): pl.pallas_call(kernel, out_shape=outs, in_specs=[pl.BlockSpec(memory_spac...  19.7 us
    ppermute x1, waiting for transfers between devices, on_device(): units_moved = lax.ppermute(units_own, 'expert', partner)  12.6 us
    all_to_all x2, starting transfers between devices, exchanged(): lax.all_to_all(rows, 'expert', split_axis=0, concat_axis=0, tiled=True)  10.6 us
    pallas_call x1, Pallas kernels, weight_grads(): pl.pallas_call(lambda *refs: grads_kernel(count, *refs), grid=(steps,), o...  4.19 us
    ppermute x4, starting transfers between devices, flipped(): got.append(lax.ppermute(values[step - 1], 'tensor', route))  4.12 us
    all_to_all x1, starting transfers between devices, on_device(): lax.all_to_all(of_half(outgoing, 1 - side), 'expert', split_axis=0, conca...  3.41 us
    ppermute x2, starting transfers between devices, spread(): blocks.append(lax.ppermute(chunk, ('dp', 'tensor'), self.pairs(step)))  2.97 us
  transfers between devices with their start and end apart: 16, of which 4 were waited for; matrix products, arithmetic and copies ran while one was open for 3% of the time, Pallas kernels for 25%

profile of v6, /device:TPU:0, one launch (start us, length us, event | category | flops | bytes accessed | tf_op | source)
XLA Modules:
  0.0 94.9 jit_solution(9310668911546525824)
XLA Ops:
  0.6 0.6 collective-permute-start
  1.2 0.1 collective-permute-start.1
  1.3 0.4 collective-permute-start.2
  1.7 2.6 %shard_map.136 = (bf16[64,4096]{1,0:T(8,128)(2,1)}, bf16[72,192]{1,0:T(8,128)(2,1)}, bf16[72,192]{1,0:T(8,128)(2,1)}) custom-call(s32[8]{0:T(128)} %placement.1, s32[8,192]{1,0:T(8,128)} %bitcast.23, bf16[8,192]{1,0:T(8,128)(2,1)} %bitcast.35, bf16[192,1792]{1,0:T(8,128)(2,1)} %refs_3_.1, bf16[192,1792]{1,0:T(8,128)(2,1)} %cot.1), custom_call_target="tpu_custom_call" | custom-call | bytes 1965088 | tf_op jit(solution)/shard_map/pallas_call | solution.py:124
  4.3 6.9 %all-to-all-start = ((bf16[8,8,4096]{2,1,0:T(8,128)(2,1)}), bf16[8,8,4096]{2,1,0:T(8,128)(2,1)S(1)}, u32[]{:S(2)}, u32[]{:S(2)}) async-start(bf16[8,8,4096]{2,1,0:T(8,128)(2,1)} %bitcast.34), calls=%async_computation | async-start | bytes 1048576 | tf_op jit(solution)/shard_map/all_to_all | solution.py:117
  11.2 15.1 %all-to-all-done = bf16[8,8,4096]{2,1,0:T(8,128)(2,1)S(1)} async-done(((bf16[8,8,4096]{2,1,0:T(8,128)(2,1)}), bf16[8,8,4096]{2,1,0:T(8,128)(2,1)S(1)}, u32[]{:S(2)}, u32[]{:S(2)}) %all-to-all-start) | async-done | bytes 524320 | tf_op jit(solution)/shard_map/all_to_all | solution.py:117
  26.3 0.2 shard_map.137
  26.5 1.6 %collective-permute-start.3 = (bf16[72,1792]{1,0:T(8,128)(2,1)S(1)}, bf16[72,1792]{1,0:T(8,128)(2,1)S(1)}, u32[]{:S(2)}, u32[]{:S(2)}) collective-permute-start(bf16[72,1792]{1,0:T(8,128)(2,1)S(1)} %get-tuple-element.27.refs_6_), channel_id=1, source_target_pairs={{0,1},{1,0},{2,3},{3,2},{4,5},{5,4},{6,7},{7,6},{8,9},{9,8},{10,11... | collective-permute-start | bytes 774152 | tf_op jit(solution)/shard_map/ppermute | solution.py:63
  28.0 0.5 collective-permute-start.5
  28.6 1.7 %dynamic-slice_bitcast_fusion = bf16[4,8,4096]{2,1,0:T(8,128)(2,1)} fusion(bf16[64,4096]{1,0:T(8,128)(2,1)} %get-tuple-element.26, s32[]{:T(128)S(6)} %select_n.39), kind=kLoop, calls=%fused_computation.1 | loop fusion | bytes 524292 | tf_op jit(solution)/shard_map/all_to_all | solution.py:430
  30.2 3.4 %all-to-all-start.2 = ((bf16[4,8,4096]{2,1,0:T(8,128)(2,1)}), bf16[4,8,4096]{2,1,0:T(8,128)(2,1)S(1)}, u32[]{:S(2)}, u32[]{:S(2)}) async-start(bf16[4,8,4096]{2,1,0:T(8,128)(2,1)} %dynamic-slice_bitcast_fusion), calls=%async_computation.2 | async-start | bytes 524288 | tf_op jit(solution)/shard_map/all_to_all | solution.py:430
  33.7 0.6 fusion
  34.9 0.7 collective-permute-done.3.refs_7_
  35.6 5.5 %shard_map.138 = (f32[72,512]{1,0:T(8,128)S(1)}, f32[72,512]{1,0:T(8,128)S(1)}, bf16[72,512]{1,0:T(8,128)(2,1)S(1)}, bf16[72,1792]{1,0:T(8,128)(2,1)S(1)}, bf16[72,1792]{1,0:T(8,128)(2,1)S(1)}) custom-call(bf16[1792,512]{1,0:T(8,128)(2,1)} %bitcast.26, bf16[1792,512]{1,0:T(8,128)(2,1)} %collective-permute-done.refs_1_, bf16[1792,512]{1,0:T(8,128)(2,1)} %bitcast.29, ...), custom_call_target="tpu_custom_call" | custom-call | flops 792723456 | bytes 12410880 | tf_op jit(solution)/shard_map/pallas_call | solution.py:124
  41.1 6.5 %shard_map.139 = (bf16[72,1536]{1,0:T(8,128)(2,1)S(1)}, bf16[72,1792]{1,0:T(8,128)(2,1)S(1)}, bf16[72,1792]{1,0:T(8,128)(2,1)S(1)}) custom-call(bf16[1792,512]{1,0:T(8,128)(2,1)} %bitcast.27, bf16[1792,512]{1,0:T(8,128)(2,1)} %collective-permute-done.refs_1_, bf16[1792,512]{1,0:T(8,128)(2,1)} %bitcast.30, bf16[1792,512]{1,0:T(8,128)(2,1)} %collective-permute-done.1.refs_3_, ...), custom_call_target="tpu_custom_call" | custom-call | flops 792723456 | bytes 12632064 | tf_op jit(solution)/shard_map/pallas_call | solution.py:124
  47.6 0.2 collective-permute-start.11
  47.8 2.9 %collective-permute-start.8 = (bf16[32,4096]{1,0:T(8,128)(2,1)S(1)}, bf16[32,4096]{1,0:T(8,128)(2,1)S(1)}, u32[]{:S(2)}, u32[]{:S(2)}) collective-permute-start(bf16[32,4096]{1,0:T(8,128)(2,1)S(1)} %constant_dynamic-slice_fusion), channel_id=1, source_target_pairs={{0,16},{4,20},{8,24},{12,28},{16,0},{20,4},{24,8},{28,12},{1,17},{... | collective-permute-start | bytes 786440 | tf_op jit(solution)/shard_map/ppermute | solution.py:505
  50.7 1.5 %collective-permute-start.4 = (bf16[72,1792]{1,0:T(8,128)(2,1)S(1)}, bf16[72,1792]{1,0:T(8,128)(2,1)S(1)}, u32[]{:S(2)}, u32[]{:S(2)}) collective-permute-start(bf16[72,1792]{1,0:T(8,128)(2,1)S(1)} %get-tuple-element.29), channel_id=1, source_target_pairs={{0,1},{1,0},{2,3},{3,2},{4,5},{5,4},{6,7},{7,6},{8,9},{9,8},{10,11... | collective-permute-start | bytes 774152 | tf_op jit(solution)/shard_map/ppermute | solution.py:63
  52.2 0.5 collective-permute-start.6
  52.7 12.6 %collective-permute-done.11 = bf16[72,1536]{1,0:T(8,128)(2,1)S(1)} collective-permute-done((bf16[72,1536]{1,0:T(8,128)(2,1)S(1)}, bf16[72,1536]{1,0:T(8,128)(2,1)S(1)}, u32[]{:S(2)}, u32[]{:S(2)}) %collective-permute-start.11) | collective-permute-done | bytes 221216 | tf_op jit(solution)/shard_map/ppermute | solution.py:521
  65.3 0.1 collective-permute-start.12
  65.4 1.2 %shard_map.140 = bf16[64,4096]{1,0:T(8,128)(2,1)} custom-call(bf16[72,1792]{1,0:T(8,128)(2,1)S(1)} %get-tuple-element.28.refs_0_, bf16[72,1792]{1,0:T(8,128)(2,1)S(1)} %collective-permute-done.4.refs_1_, bf16[72,1792]{1,0:T(8,128)(2,1)S(1)} %get-tuple-element.34.refs_2_, bf16[72,1792]{1,0:T(8,128)(2,1)S(1)} %collective-permute-done.6.refs_3_), custom_call_target="tpu_custom_call" | custom-call | bytes 1556480 | tf_op jit(solution)/shard_map/pallas_call | solution.py:124
  66.6 3.7 %all-to-all-start.1 = ((bf16[8,8,4096]{2,1,0:T(8,128)(2,1)}), bf16[8,8,4096]{2,1,0:T(8,128)(2,1)S(1)}, u32[]{:S(2)}, u32[]{:S(2)}) async-start(bf16[8,8,4096]{2,1,0:T(8,128)(2,1)} %bitcast.7), calls=%async_computation.1 | async-start | bytes 1048576 | tf_op jit(solution)/shard_map/all_to_all | solution.py:117
  70.4 0.8 shard_map.143
  71.2 1.5 %collective-permute-start.10 = (bf16[72,3584]{1,0:T(8,128)(2,1)S(1)}, bf16[72,3584]{1,0:T(8,128)(2,1)S(1)}, u32[]{:S(2)}, u32[]{:S(2)}) collective-permute-start(bf16[72,3584]{1,0:T(8,128)(2,1)S(1)} %shard_map.143), channel_id=1, source_target_pairs={{2,0},{0,1},{3,2},{1,3},{6,4},{4,5},{7,6},{5,7},{10,8},{8,9},{11,1... | collective-permute-start | bytes 1548296 | tf_op jit(solution)/shard_map/ppermute | solution.py:56
  72.8 1.4 %collective-permute-start.9 = (bf16[72,3584]{1,0:T(8,128)(2,1)S(1)}, bf16[72,3584]{1,0:T(8,128)(2,1)}, u32[]{:S(2)}, u32[]{:S(2)}) collective-permute-start(bf16[72,3584]{1,0:T(8,128)(2,1)S(1)} %shard_map.143), channel_id=1, source_target_pairs={{0,0},{2,1},{1,2},{3,3},{4,4},{6,5},{5,6},{7,7},{8,8},{10,9},{9,10... | collective-permute-start | bytes 1548296 | tf_op jit(solution)/shard_map/ppermute | solution.py:56
  74.3 11.2 %all-to-all-done.1 = bf16[8,8,4096]{2,1,0:T(8,128)(2,1)S(1)} async-done(((bf16[8,8,4096]{2,1,0:T(8,128)(2,1)}), bf16[8,8,4096]{2,1,0:T(8,128)(2,1)S(1)}, u32[]{:S(2)}, u32[]{:S(2)}) %all-to-all-start.1) | async-done | bytes 524320 | tf_op jit(solution)/shard_map/all_to_all | solution.py:117
  85.5 1.1 %shard_map.142 = f32[8,192]{1,0:T(8,128)S(1)} custom-call(s32[8]{0:T(128)S(1)} %copy-done.4, s32[8,192]{1,0:T(8,128)S(1)} %bitcast.24, bf16[72,192]{1,0:T(8,128)(2,1)S(1)} %copy-done.1, bf16[192,1792]{1,0:T(8,128)(2,1)S(1)} %copy-done, bf16[64,4096]{1,0:T(8,128)(2,1)S(1)} %bitcast.20), custom_call_target="tpu_custom_call" | custom-call | bytes 1252384 | tf_op jit(solution)/shard_map/pallas_call | solution.py:124
  86.7 1.6 %collective-permute-start.7 = (f32[8,192]{1,0:T(8,128)S(1)}, f32[8,192]{1,0:T(8,128)S(1)}, u32[]{:S(2)}, u32[]{:S(2)}) collective-permute-start(f32[8,192]{1,0:T(8,128)S(1)} %shard_map.142), channel_id=1, source_target_pairs={{0,1},{1,0},{2,3},{3,2},{4,5},{5,4},{6,7},{7,6},{8,9},{9,8},{10,11... | collective-permute-start | bytes 18440 | tf_op jit(solution)/shard_map/ppermute | solution.py:494
  88.3 4.2 %weight_grads.1 = (bf16[1792,512]{1,0:T(8,128)(2,1)}, bf16[1792,512]{1,0:T(8,128)(2,1)}, bf16[1792,512]{1,0:T(8,128)(2,1)}) custom-call(bf16[72,3584]{1,0:T(8,128)(2,1)} %collective-permute-done.9.refs_0_.refs_2_, bf16[72,3584]{1,0:T(8,128)(2,1)S(1)} %collective-permute-done.10.refs_1_.refs_3_, bf16[72,3584]{1,0:T(8,128)(2,1)} %collective-permute-done.9.refs_0_.refs_2_, ...), custom_call_target="tpu_custom_call" | custom-call | flops 792723456 | bytes 5505024 | tf_op jit(solution)/shard_map/weight_grads/pallas_call | solution.py:371
  92.5 1.8 %shard_map.141 = (bf16[192,1792]{1,0:T(8,128)(2,1)}, bf16[192,1792]{1,0:T(8,128)(2,1)}) custom-call(bf16[72,192]{1,0:T(8,128)(2,1)S(1)} %copy-done.1, bf16[72,192]{1,0:T(8,128)(2,1)S(1)} %copy-done.2, bf16[64,4096]{1,0:T(8,128)(2,1)S(1)} %bitcast.21), custom_call_target="tpu_custom_call" | custom-call | bytes 1955840 | tf_op jit(solution)/shard_map/pallas_call | solution.py:124
  94.3 0.6 add_bitcast_fusion
  (28 shorter events, 0.2 us)
Async XLA Ops:
  0.6 35.0 %collective-permute-start = (bf16[1792,512]{1,0:T(8,128)(2,1)}, bf16[1792,512]{1,0:T(8,128)(2,1)}, u32[]{:S(2)}, u32[]{:S(2)}) collective-permute-start(bf16[1792,512]{1,0:T(8,128)(2,1)} %bitcast.25), channel_id=1, source_target_pairs={{0,2},{2,0},{1,3},{3,1},{4,6},{6,4},{5,7},{7,5},{8,10},{10,8},{9,1... | collective-permute-start | bytes 5505032 | tf_op jit(solution)/shard_map/ppermute | solution.py:70
  1.2 34.4 %collective-permute-start.1 = (bf16[1792,512]{1,0:T(8,128)(2,1)}, bf16[1792,512]{1,0:T(8,128)(2,1)}, u32[]{:S(2)}, u32[]{:S(2)}) collective-permute-start(bf16[1792,512]{1,0:T(8,128)(2,1)} %bitcast.28), channel_id=1, source_target_pairs={{0,2},{2,0},{1,3},{3,1},{4,6},{6,4},{5,7},{7,5},{8,10},{10,8},{9,1... | collective-permute-start | bytes 5505032 | tf_op jit(solution)/shard_map/ppermute | solution.py:70
  1.3 34.4 %collective-permute-start.2 = (bf16[1792,512]{1,0:T(8,128)(2,1)}, bf16[1792,512]{1,0:T(8,128)(2,1)}, u32[]{:S(2)}, u32[]{:S(2)}) collective-permute-start(bf16[1792,512]{1,0:T(8,128)(2,1)} %bitcast.31), channel_id=1, source_target_pairs={{0,2},{2,0},{1,3},{3,1},{4,6},{6,4},{5,7},{7,5},{8,10},{10,8},{9,1... | collective-permute-start | bytes 5505032 | tf_op jit(solution)/shard_map/ppermute | solution.py:70
  1.7 31.9 %copy-start.5 = (s32[8]{0:T(128)S(1)}, s32[8]{0:T(128)}, u32[]{:S(2)}) copy-start(s32[8]{0:T(128)} %flag.1) | copy-start | bytes 100
  4.3 22.0 %all-to-all-start = ((bf16[8,8,4096]{2,1,0:T(8,128)(2,1)}), bf16[8,8,4096]{2,1,0:T(8,128)(2,1)S(1)}, u32[]{:S(2)}, u32[]{:S(2)}) async-start(bf16[8,8,4096]{2,1,0:T(8,128)(2,1)} %bitcast.34), calls=%async_computation | async-start | bytes 1048576 | tf_op jit(solution)/shard_map/all_to_all | solution.py:117
  26.5 9.2 %collective-permute-start.3 = (bf16[72,1792]{1,0:T(8,128)(2,1)S(1)}, bf16[72,1792]{1,0:T(8,128)(2,1)S(1)}, u32[]{:S(2)}, u32[]{:S(2)}) collective-permute-start(bf16[72,1792]{1,0:T(8,128)(2,1)S(1)} %get-tuple-element.27.refs_6_), channel_id=1, source_target_pairs={{0,1},{1,0},{2,3},{3,2},{4,5},{5,4},{6,7},{7,6},{8,9},{9,8},{10,11... | collective-permute-start | bytes 774152 | tf_op jit(solution)/shard_map/ppermute | solution.py:63
  28.0 13.1 %collective-permute-start.5 = (bf16[72,1792]{1,0:T(8,128)(2,1)S(1)}, bf16[72,1792]{1,0:T(8,128)(2,1)S(1)}, u32[]{:S(2)}, u32[]{:S(2)}) collective-permute-start(bf16[72,1792]{1,0:T(8,128)(2,1)S(1)} %get-tuple-element.30.refs_6_), channel_id=1, source_target_pairs={{0,1},{1,0},{2,3},{3,2},{4,5},{5,4},{6,7},{7,6},{8,9},{9,8},{10,11... | collective-permute-start | bytes 774152 | tf_op jit(solution)/shard_map/ppermute | solution.py:63
  30.2 36.4 %all-to-all-start.2 = ((bf16[4,8,4096]{2,1,0:T(8,128)(2,1)}), bf16[4,8,4096]{2,1,0:T(8,128)(2,1)S(1)}, u32[]{:S(2)}, u32[]{:S(2)}) async-start(bf16[4,8,4096]{2,1,0:T(8,128)(2,1)} %dynamic-slice_bitcast_fusion), calls=%async_computation.2 | async-start | bytes 524288 | tf_op jit(solution)/shard_map/all_to_all | solution.py:430
  47.6 17.7 %collective-permute-start.11 = (bf16[72,1536]{1,0:T(8,128)(2,1)S(1)}, bf16[72,1536]{1,0:T(8,128)(2,1)S(1)}, u32[]{:S(2)}, u32[]{:S(2)}) collective-permute-start(bf16[72,1536]{1,0:T(8,128)(2,1)S(1)} %get-tuple-element.38), channel_id=1, source_target_pairs={{0,16},{4,20},{8,24},{12,28},{16,0},{20,4},{24,8},{28,12},{1,17},{... | collective-permute-start | bytes 663560 | tf_op jit(solution)/shard_map/ppermute | solution.py:521
  47.8 22.6 %collective-permute-start.8 = (bf16[32,4096]{1,0:T(8,128)(2,1)S(1)}, bf16[32,4096]{1,0:T(8,128)(2,1)S(1)}, u32[]{:S(2)}, u32[]{:S(2)}) collective-permute-start(bf16[32,4096]{1,0:T(8,128)(2,1)S(1)} %constant_dynamic-slice_fusion), channel_id=1, source_target_pairs={{0,16},{4,20},{8,24},{12,28},{16,0},{20,4},{24,8},{28,12},{1,17},{... | collective-permute-start | bytes 786440 | tf_op jit(solution)/shard_map/ppermute | solution.py:505
  50.7 14.7 %collective-permute-start.4 = (bf16[72,1792]{1,0:T(8,128)(2,1)S(1)}, bf16[72,1792]{1,0:T(8,128)(2,1)S(1)}, u32[]{:S(2)}, u32[]{:S(2)}) collective-permute-start(bf16[72,1792]{1,0:T(8,128)(2,1)S(1)} %get-tuple-element.29), channel_id=1, source_target_pairs={{0,1},{1,0},{2,3},{3,2},{4,5},{5,4},{6,7},{7,6},{8,9},{9,8},{10,11... | collective-permute-start | bytes 774152 | tf_op jit(solution)/shard_map/ppermute | solution.py:63
  52.2 13.2 %collective-permute-start.6 = (bf16[72,1792]{1,0:T(8,128)(2,1)S(1)}, bf16[72,1792]{1,0:T(8,128)(2,1)S(1)}, u32[]{:S(2)}, u32[]{:S(2)}) collective-permute-start(bf16[72,1792]{1,0:T(8,128)(2,1)S(1)} %get-tuple-element.35), channel_id=1, source_target_pairs={{0,1},{1,0},{2,3},{3,2},{4,5},{5,4},{6,7},{7,6},{8,9},{9,8},{10,11... | collective-permute-start | bytes 774152 | tf_op jit(solution)/shard_map/ppermute | solution.py:63
  65.3 8.9 %collective-permute-start.12 = (bf16[72,1536]{1,0:T(8,128)(2,1)S(1)}, bf16[72,1536]{1,0:T(8,128)(2,1)S(1)}, u32[]{:S(2)}, u32[]{:S(2)}) collective-permute-start(bf16[72,1536]{1,0:T(8,128)(2,1)S(1)} %broadcast_select_fusion), channel_id=1, source_target_pairs={{0,2},{2,0},{1,3},{3,1},{4,6},{6,4},{5,7},{7,5},{8,10},{10,8},{9,1... | collective-permute-start | bytes 663560 | tf_op jit(solution)/shard_map/ppermute | solution.py:75
  66.6 18.9 %all-to-all-start.1 = ((bf16[8,8,4096]{2,1,0:T(8,128)(2,1)}), bf16[8,8,4096]{2,1,0:T(8,128)(2,1)S(1)}, u32[]{:S(2)}, u32[]{:S(2)}) async-start(bf16[8,8,4096]{2,1,0:T(8,128)(2,1)} %bitcast.7), calls=%async_computation.1 | async-start | bytes 1048576 | tf_op jit(solution)/shard_map/all_to_all | solution.py:117
  70.4 15.1 %copy-start = (bf16[192,1792]{1,0:T(8,128)(2,1)S(1)}, bf16[192,1792]{1,0:T(8,128)(2,1)}, u32[]{:S(2)}) copy-start(bf16[192,1792]{1,0:T(8,128)(2,1)} %cot.1) | copy-start | bytes 2064388
  70.4 15.1 %copy-start.1 = (bf16[72,192]{1,0:T(8,128)(2,1)S(1)}, bf16[72,192]{1,0:T(8,128)(2,1)}, u32[]{:S(2)}) copy-start(bf16[72,192]{1,0:T(8,128)(2,1)} %get-tuple-element.24.select) | copy-start | bytes 82948
  70.4 15.1 %copy-start.3 = (s32[192,8]{0,1:T(8,128)S(1)}, s32[192,8]{0,1:T(8,128)}, u32[]{:S(2)}) copy-start(s32[192,8]{0,1:T(8,128)} %param.10) | copy-start | bytes 18436
  70.4 15.1 %copy-start.4 = (s32[8]{0:T(128)S(1)}, s32[8]{0:T(128)}, u32[]{:S(2)}) copy-start(s32[8]{0:T(128)} %placement.1) | copy-start | bytes 100
  71.2 17.0 %collective-permute-start.10 = (bf16[72,3584]{1,0:T(8,128)(2,1)S(1)}, bf16[72,3584]{1,0:T(8,128)(2,1)S(1)}, u32[]{:S(2)}, u32[]{:S(2)}) collective-permute-start(bf16[72,3584]{1,0:T(8,128)(2,1)S(1)} %shard_map.143), channel_id=1, source_target_pairs={{2,0},{0,1},{3,2},{1,3},{6,4},{4,5},{7,6},{5,7},{10,8},{8,9},{11,1... | collective-permute-start | bytes 1548296 | tf_op jit(solution)/shard_map/ppermute | solution.py:56
  72.8 15.5 %collective-permute-start.9 = (bf16[72,3584]{1,0:T(8,128)(2,1)S(1)}, bf16[72,3584]{1,0:T(8,128)(2,1)}, u32[]{:S(2)}, u32[]{:S(2)}) collective-permute-start(bf16[72,3584]{1,0:T(8,128)(2,1)S(1)} %shard_map.143), channel_id=1, source_target_pairs={{0,0},{2,1},{1,2},{3,3},{4,4},{6,5},{5,6},{7,7},{8,8},{10,9},{9,10... | collective-permute-start | bytes 1548296 | tf_op jit(solution)/shard_map/ppermute | solution.py:56
  85.5 6.9 %copy-start.2 = (bf16[72,192]{1,0:T(8,128)(2,1)S(1)}, bf16[72,192]{1,0:T(8,128)(2,1)}, u32[]{:S(2)}) copy-start(bf16[72,192]{1,0:T(8,128)(2,1)} %get-tuple-element.25.weighted) | copy-start | bytes 82948
  86.7 7.6 %collective-permute-start.7 = (f32[8,192]{1,0:T(8,128)S(1)}, f32[8,192]{1,0:T(8,128)S(1)}, u32[]{:S(2)}, u32[]{:S(2)}) collective-permute-start(f32[8,192]{1,0:T(8,128)S(1)} %shard_map.142), channel_id=1, source_target_pairs={{0,1},{1,0},{2,3},{3,2},{4,5},{5,4},{6,7},{7,6},{8,9},{9,8},{10,11... | collective-permute-start | bytes 18440 | tf_op jit(solution)/shard_map/ppermute | solution.py:494

commit v7 on v6

--- a/solution.py
+++ b/solution.py
@@ -161,8 +161,8 @@
 
 
 def head_kernel(*refs):
-    given, (rows, select, weighted), kept = refs[:5], refs[5:8], refs[8:13]
-    copies = fetch(zip(given, kept), refs[13])
+    given, (rows, select, weighted, other_side), kept = refs[:5], refs[5:9], refs[9:14]
+    copies = fetch(zip(given, kept), refs[14])
     placement, routes, gates, tokens, cot = kept
     for copy in copies[:3]:
         copy.wait()
@@ -191,10 +191,18 @@
     both = jnp.concatenate([x, d], axis=1)
     main = rows.shape[0]
     fold(both[:main], both[main:], rows)
-
-
-def split_kernel(rows, x, d):
+    other_side[...] = rows[half_rows(rows, other=True)]
+
+
+def half_rows(rows, other):
+    count = rows.shape[0] // 2
+    side = lax.axis_index("expert") // (lax.axis_size("expert") // 2)
+    return pl.ds(pl.multiple_of((1 - side if other else side) * count, count), count)
+
+
+def split_kernel(rows, x, d, my_side):
     main, half = rows.shape[0], x.shape[1]
+    my_side[...] = rows[half_rows(rows, other=False)]
     last = unfold(rows[:, 2 * half :], 2 * half).astype(BF)
     for side, out in ((0, x), (1, d)):
         out[:main] = rows[:, side * half : (side + 1) * half]
@@ -401,13 +409,15 @@
     half_width = tokens.shape[1]
     routes_t, gates_t = routes.T, gates.T
 
+    folded = folded_shape(experts, 2 * half_width)
     outs = [
-        folded_shape(experts, 2 * half_width),
+        folded,
         shape((slots_all, tok_count), BF),
         shape((slots_all, tok_count), BF),
+        shape((folded.shape[0] // 2, folded.shape[1]), BF),
     ]
     given = (placement, routes_t, gates_t, tokens, cotangent)
-    outgoing, select, weighted = call(
+    outgoing, select, weighted, other_side = call(
         head_kernel,
         outs,
         given,
@@ -421,23 +431,16 @@
     )
     arrived = exchanged(outgoing)
     half_axis = experts // 2
-    side = myself // half_axis
-
-    def of_half(rows, which):
-        count = half_axis * MAIN
-        return lax.dynamic_slice_in_dim(rows, which * count, count, axis=0)
-
     near = lax.all_to_all(
-        of_half(outgoing, 1 - side),
+        other_side,
         "expert",
         split_axis=0,
         concat_axis=0,
         axis_index_groups=[list(range(half_axis)), list(range(half_axis, experts))],
         tiled=True,
     )
-    sides = [shape((slots_all, half_width), BF)] * 2
-    x_own, d_own = call(split_kernel, sides, (arrived,), room_for(*sides, *sides))
-
+    sides = [shape((slots_all, half_width), BF)] * 2 + [shape(other_side.shape, BF)]
+    x_own, d_own, my_side = call(split_kernel, sides, (arrived,), room_for(*sides, *sides))
     own_weights = (wg, wu, wd)
     shards = []
     for own in own_weights:
@@ -502,7 +505,7 @@
     )
 
     partner = [(i, (i + experts // 2) % experts) for i in range(experts)]
-    moved = lax.ppermute(of_half(arrived, side), "expert", partner)
+    moved = lax.ppermute(my_side, "expert", partner)
     both = shape((slots_all, 2 * half_width), BF)
     (held,) = call(
         held_kernel,

time: 95.4 us -> 97.3 us (1.020)
  blocking collectives: 0 us -> 22 us
  waiting for transfers between devices: 39.6 us -> 22.7 us
  starting transfers between devices: 26.9 us -> 21.6 us
  other arithmetic: 1.34 us -> 3.99 us
    all_to_all x0 -> x1, blocking collectives: none -> 22 us  [exchanged(): lax.all_to_all(rows, 'expert', split_axis=0, concat_axis=0, tiled=True)]
    all_to_all x2 -> x1, waiting for transfers between devices: 26.3 us -> 9.4 us  [exchanged(): lax.all_to_all(rows, 'expert', split_axis=0, concat_axis=0, tiled=True)]
    ppermute x1, waiting for transfers between devices: 12.6 us -> 2.69 us  [on_device(): units_moved = lax.ppermute(units_own, 'expert', partner)]
    ppermute x4, waiting for transfers between devices: 0.68 us -> 10.5 us  [flipped(): got.append(lax.ppermute(values[step - 1], 'tensor', route))]
    all_to_all x2 -> x1, starting transfers between devices: 10.6 us -> 5.36 us  [exchanged(): lax.all_to_all(rows, 'expert', split_axis=0, concat_axis=0, tiled=True)]
    all_to_all x1 -> x0, local copies, waits for them, and re-layouts: 1.67 us -> none  [on_device(): lax.all_to_all(of_half(outgoing, 1 - side), 'expert', split_axis=0, conca...]
    select_n x1, other arithmetic: 0.03 us -> 1.65 us  [on_device(): units_held = jnp.where(my_flag, units_moved, units_own)]
    unnamed x12 -> x14, local copies, waits for them, and re-layouts: 0.03 us -> 1.26 us
  transfers between devices with their start and end apart: 16 -> 15, of which waited for: 4 -> 5; matrix products, arithmetic and copies ran while one was open for 3% -> 4% of each run, Pallas kernels for 25% -> 18%
where the time goes in v7:
time: 97.3 us; the launch traced here: 96.8 us
  Pallas kernels  23.9 us (25%)
  waiting for transfers between devices  22.7 us (23%)
  blocking collectives  22 us (23%)
  starting transfers between devices  21.6 us (22%)
  other arithmetic  3.99 us (4%)
  between operations  1.45 us (1%)
  local copies, waits for them, and re-layouts  1.26 us (1%)
    all_to_all x1, blocking collectives, exchanged(): lax.all_to_all(rows, 'expert', split_axis=0, concat_axis=0, tiled=True)  22 us
    pallas_call x8, Pallas kernels, call(): pl.pallas_call(kernel, out_shape=outs, in_specs=[pl.BlockSpec(memory_spac...  19.8 us
    ppermute x4, waiting for transfers between devices, flipped(): got.append(lax.ppermute(values[step - 1], 'tensor', route))  10.5 us
    all_to_all x1, waiting for transfers between devices, exchanged(): lax.all_to_all(rows, 'expert', split_axis=0, concat_axis=0, tiled=True)  9.4 us
    all_to_all x1, starting transfers between devices, exchanged(): lax.all_to_all(rows, 'expert', split_axis=0, concat_axis=0, tiled=True)  5.36 us
    pallas_call x1, Pallas kernels, weight_grads(): pl.pallas_call(lambda *refs: grads_kernel(count, *refs), grid=(steps,), o...  4.17 us
    ppermute x4, starting transfers between devices, flipped(): got.append(lax.ppermute(values[step - 1], 'tensor', route))  4.12 us
    all_to_all x1, starting transfers between devices, on_device(): lax.all_to_all(other_side, 'expert', split_axis=0, concat_axis=0, axis_in...  3.41 us
  transfers between devices with their start and end apart: 15, of which 5 were waited for; matrix products, arithmetic and copies ran while one was open for 4% of the time, Pallas kernels for 18%

profile of v7, /device:TPU:0, one launch (start us, length us, event | category | flops | bytes accessed | tf_op | source)
XLA Modules:
  0.0 96.8 jit_solution(5368337923195233902)
XLA Ops:
  0.6 0.6 collective-permute-start
  1.3 0.4 collective-permute-start.2
  1.7 2.7 %shard_map.136 = (bf16[64,4096]{1,0:T(8,128)(2,1)}, bf16[72,192]{1,0:T(8,128)(2,1)}, bf16[72,192]{1,0:T(8,128)(2,1)}, bf16[32,4096]{1,0:T(8,128)(2,1)}) custom-call(s32[8]{0:T(128)} %placement.1, s32[8,192]{1,0:T(8,128)} %bitcast.21, bf16[8,192]{1,0:T(8,128)(2,1)} %bitcast.33, bf16[192,1792]{1,0:T(8,128)(2,1)} %refs_3_.1, bf16[192,1792]{1,0:T(8,128)(2,1)} %cot.1), custom_call_target="tpu_custom_call" | custom-call | bytes 2227232 | tf_op jit(solution)/shard_map/pallas_call | solution.py:124
  4.4 22.0 %all_to_all.33 = bf16[8,8,4096]{2,1,0:T(8,128)(2,1)S(1)} all-to-all(bf16[8,8,4096]{2,1,0:T(8,128)(2,1)} %bitcast.32), channel_id=1, replica_groups=mesh['expert'=8,'dp'=2,'tensor'=2] {'expert'}, dimensions={0} | all-to-all | bytes 1048576 | tf_op jit(solution)/shard_map/all_to_all | solution.py:117
  26.5 1.6 %collective-permute-start.3 = (bf16[72,1792]{1,0:T(8,128)(2,1)S(1)}, bf16[72,1792]{1,0:T(8,128)(2,1)S(1)}, u32[]{:S(2)}, u32[]{:S(2)}) collective-permute-start(bf16[72,1792]{1,0:T(8,128)(2,1)S(1)} %get-tuple-element.29.refs_6_), channel_id=1, source_target_pairs={{0,1},{1,0},{2,3},{3,2},{4,5},{5,4},{6,7},{7,6},{8,9},{9,8},{10,11... | collective-permute-start | bytes 774152 | tf_op jit(solution)/shard_map/ppermute | solution.py:63
  28.1 0.5 collective-permute-start.5
  28.6 7.1 %collective-permute-done.3.refs_7_ = bf16[72,1792]{1,0:T(8,128)(2,1)S(1)} collective-permute-done((bf16[72,1792]{1,0:T(8,128)(2,1)S(1)}, bf16[72,1792]{1,0:T(8,128)(2,1)S(1)}, u32[]{:S(2)}, u32[]{:S(2)}) %collective-permute-start.3) | collective-permute-done | bytes 258080 | tf_op jit(solution)/shard_map/ppermute | solution.py:63
  35.7 1.2 %copy-done.6 = bf16[1792,512]{1,0:T(8,128)(2,1)} copy-done((bf16[1792,512]{1,0:T(8,128)(2,1)}, bf16[1792,512]{1,0:T(8,128)(2,1)S(1)}, u32[]{:S(2)}) %copy-start.6) | copy-done | bytes 1835032
  36.9 5.5 %shard_map.138 = (f32[72,512]{1,0:T(8,128)S(1)}, f32[72,512]{1,0:T(8,128)S(1)}, bf16[72,512]{1,0:T(8,128)(2,1)S(1)}, bf16[72,1792]{1,0:T(8,128)(2,1)S(1)}, bf16[72,1792]{1,0:T(8,128)(2,1)S(1)}) custom-call(bf16[1792,512]{1,0:T(8,128)(2,1)} %bitcast.24, bf16[1792,512]{1,0:T(8,128)(2,1)} %copy-done.6, bf16[1792,512]{1,0:T(8,128)(2,1)} %bitcast.27, ...), custom_call_target="tpu_custom_call" | custom-call | flops 792723456 | bytes 12410880 | tf_op jit(solution)/shard_map/pallas_call | solution.py:124
  42.4 6.5 %shard_map.139 = (bf16[72,1536]{1,0:T(8,128)(2,1)S(1)}, bf16[72,1792]{1,0:T(8,128)(2,1)S(1)}, bf16[72,1792]{1,0:T(8,128)(2,1)S(1)}) custom-call(bf16[1792,512]{1,0:T(8,128)(2,1)} %bitcast.25, bf16[1792,512]{1,0:T(8,128)(2,1)} %copy-done.6, bf16[1792,512]{1,0:T(8,128)(2,1)} %bitcast.28, bf16[1792,512]{1,0:T(8,128)(2,1)} %collective-permute-done.1.refs_3_, ...), custom_call_target="tpu_custom_call" | custom-call | flops 792723456 | bytes 12632064 | tf_op jit(solution)/shard_map/pallas_call | solution.py:124
  48.9 0.9 collective-permute-start.11
  49.8 3.4 %all-to-all-start.2 = ((bf16[4,8,4096]{2,1,0:T(8,128)(2,1)}), bf16[4,8,4096]{2,1,0:T(8,128)(2,1)S(1)}, u32[]{:S(2)}, u32[]{:S(2)}) async-start(bf16[4,8,4096]{2,1,0:T(8,128)(2,1)} %bitcast.10), calls=%async_computation.2 | async-start | bytes 524288 | tf_op jit(solution)/shard_map/all_to_all | solution.py:434
  53.3 0.6 fusion
  54.6 2.1 %collective-permute-start.8 = (bf16[32,4096]{1,0:T(8,128)(2,1)S(1)}, bf16[32,4096]{1,0:T(8,128)(2,1)S(1)}, u32[]{:S(2)}, u32[]{:S(2)}) collective-permute-start(bf16[32,4096]{1,0:T(8,128)(2,1)S(1)} %get-tuple-element.40), channel_id=1, source_target_pairs={{0,16},{4,20},{8,24},{12,28},{16,0},{20,4},{24,8},{28,12},{1,17},{... | collective-permute-start | bytes 786440 | tf_op jit(solution)/shard_map/ppermute | solution.py:508
  56.7 1.5 %collective-permute-start.4 = (bf16[72,1792]{1,0:T(8,128)(2,1)S(1)}, bf16[72,1792]{1,0:T(8,128)(2,1)S(1)}, u32[]{:S(2)}, u32[]{:S(2)}) collective-permute-start(bf16[72,1792]{1,0:T(8,128)(2,1)S(1)} %get-tuple-element.31), channel_id=1, source_target_pairs={{0,1},{1,0},{2,3},{3,2},{4,5},{5,4},{6,7},{7,6},{8,9},{9,8},{10,11... | collective-permute-start | bytes 774152 | tf_op jit(solution)/shard_map/ppermute | solution.py:63
  58.2 0.5 collective-permute-start.6
  58.7 2.7 %collective-permute-done.11 = bf16[72,1536]{1,0:T(8,128)(2,1)} collective-permute-done((bf16[72,1536]{1,0:T(8,128)(2,1)S(1)}, bf16[72,1536]{1,0:T(8,128)(2,1)}, u32[]{:S(2)}, u32[]{:S(2)}) %collective-permute-start.11) | collective-permute-done | bytes 221216 | tf_op jit(solution)/shard_map/ppermute | solution.py:524
  61.4 1.7 %broadcast_select_fusion = bf16[72,1536]{1,0:T(8,128)(2,1)} fusion(bf16[72,1536]{1,0:T(8,128)(2,1)} %collective-permute-done.11, bf16[72,1536]{1,0:T(8,128)(2,1)S(1)} %get-tuple-element.42, pred[]{:T(512)S(6)} %eq.17), kind=kLoop, calls=%fused_computation.1 | loop fusion | flops 110592 | bytes 663553 | tf_op jit(solution)/shard_map/jit(_where)/select_n | solution.py:525
  63.0 0.7 collective-permute-done.4.refs_1_
  63.8 2.8 %collective-permute-done.6.refs_3_ = bf16[72,1792]{1,0:T(8,128)(2,1)S(1)} collective-permute-done((bf16[72,1792]{1,0:T(8,128)(2,1)S(1)}, bf16[72,1792]{1,0:T(8,128)(2,1)S(1)}, u32[]{:S(2)}, u32[]{:S(2)}) %collective-permute-start.6) | collective-permute-done | bytes 258080 | tf_op jit(solution)/shard_map/ppermute | solution.py:63
  66.5 1.2 %shard_map.140 = bf16[64,4096]{1,0:T(8,128)(2,1)} custom-call(bf16[72,1792]{1,0:T(8,128)(2,1)S(1)} %get-tuple-element.30.refs_0_, bf16[72,1792]{1,0:T(8,128)(2,1)S(1)} %collective-permute-done.4.refs_1_, bf16[72,1792]{1,0:T(8,128)(2,1)S(1)} %get-tuple-element.36.refs_2_, bf16[72,1792]{1,0:T(8,128)(2,1)S(1)} %collective-permute-done.6.refs_3_), custom_call_target="tpu_custom_call" | custom-call | bytes 1556480 | tf_op jit(solution)/shard_map/pallas_call | solution.py:124
  67.7 5.4 %all-to-all-start.1 = ((bf16[8,8,4096]{2,1,0:T(8,128)(2,1)}), bf16[8,8,4096]{2,1,0:T(8,128)(2,1)S(1)}, u32[]{:S(2)}, u32[]{:S(2)}) async-start(bf16[8,8,4096]{2,1,0:T(8,128)(2,1)} %bitcast.7), calls=%async_computation.1 | async-start | bytes 1048576 | tf_op jit(solution)/shard_map/all_to_all | solution.py:117
  73.2 0.8 shard_map.143
  74.0 1.5 %collective-permute-start.10 = (bf16[72,3584]{1,0:T(8,128)(2,1)S(1)}, bf16[72,3584]{1,0:T(8,128)(2,1)S(1)}, u32[]{:S(2)}, u32[]{:S(2)}) collective-permute-start(bf16[72,3584]{1,0:T(8,128)(2,1)S(1)} %shard_map.143), channel_id=1, source_target_pairs={{2,0},{0,1},{3,2},{1,3},{6,4},{4,5},{7,6},{5,7},{10,8},{8,9},{11,1... | collective-permute-start | bytes 1548296 | tf_op jit(solution)/shard_map/ppermute | solution.py:56
  75.5 1.5 %collective-permute-start.9 = (bf16[72,3584]{1,0:T(8,128)(2,1)S(1)}, bf16[72,3584]{1,0:T(8,128)(2,1)}, u32[]{:S(2)}, u32[]{:S(2)}) collective-permute-start(bf16[72,3584]{1,0:T(8,128)(2,1)S(1)} %shard_map.143), channel_id=1, source_target_pairs={{0,0},{2,1},{1,2},{3,3},{4,4},{6,5},{5,6},{7,7},{8,8},{10,9},{9,10... | collective-permute-start | bytes 1548296 | tf_op jit(solution)/shard_map/ppermute | solution.py:56
  77.0 1.1 %broadcast_select_fusion.2 = (bf16[72,1536]{1,0:T(8,128)(2,1)S(1)}, bf16[72,1536]{1,0:T(8,128)(2,1)S(1)}) fusion(bf16[72,1536]{1,0:T(8,128)(2,1)} %broadcast_select_fusion, bf16[72,1536]{1,0:T(8,128)(2,1)} %collective-permute-done.12, pred[]{:T(512)S(6)} %eq.14), kind=kLoop, calls=%fused_computation.3 | loop fusion | flops 221184 | bytes 884737 | tf_op jit(solution)/shard_map/jit(_where)/select_n | solution.py:77
  78.1 9.4 %all-to-all-done.1 = bf16[8,8,4096]{2,1,0:T(8,128)(2,1)S(1)} async-done(((bf16[8,8,4096]{2,1,0:T(8,128)(2,1)}), bf16[8,8,4096]{2,1,0:T(8,128)(2,1)S(1)}, u32[]{:S(2)}, u32[]{:S(2)}) %all-to-all-start.1) | async-done | bytes 524320 | tf_op jit(solution)/shard_map/all_to_all | solution.py:117
  87.5 1.1 %shard_map.142 = f32[8,192]{1,0:T(8,128)S(1)} custom-call(s32[8]{0:T(128)S(1)} %copy-done.4, s32[8,192]{1,0:T(8,128)S(1)} %bitcast.22, bf16[72,192]{1,0:T(8,128)(2,1)S(1)} %copy-done.1, bf16[192,1792]{1,0:T(8,128)(2,1)S(1)} %copy-done, bf16[64,4096]{1,0:T(8,128)(2,1)S(1)} %bitcast.18), custom_call_target="tpu_custom_call" | custom-call | bytes 1252384 | tf_op jit(solution)/shard_map/pallas_call | solution.py:124
  88.6 1.6 %collective-permute-start.7 = (f32[8,192]{1,0:T(8,128)S(1)}, f32[8,192]{1,0:T(8,128)S(1)}, u32[]{:S(2)}, u32[]{:S(2)}) collective-permute-start(f32[8,192]{1,0:T(8,128)S(1)} %shard_map.142), channel_id=1, source_target_pairs={{0,1},{1,0},{2,3},{3,2},{4,5},{5,4},{6,7},{7,6},{8,9},{9,8},{10,11... | collective-permute-start | bytes 18440 | tf_op jit(solution)/shard_map/ppermute | solution.py:497
  90.2 4.2 %weight_grads.1 = (bf16[1792,512]{1,0:T(8,128)(2,1)}, bf16[1792,512]{1,0:T(8,128)(2,1)}, bf16[1792,512]{1,0:T(8,128)(2,1)}) custom-call(bf16[72,3584]{1,0:T(8,128)(2,1)} %collective-permute-done.9.refs_0_.refs_2_, bf16[72,3584]{1,0:T(8,128)(2,1)S(1)} %collective-permute-done.10.refs_1_.refs_3_, bf16[72,3584]{1,0:T(8,128)(2,1)} %collective-permute-done.9.refs_0_.refs_2_, ...), custom_call_target="tpu_custom_call" | custom-call | flops 792723456 | bytes 5505024 | tf_op jit(solution)/shard_map/weight_grads/pallas_call | solution.py:379
  94.4 1.8 %shard_map.141 = (bf16[192,1792]{1,0:T(8,128)(2,1)}, bf16[192,1792]{1,0:T(8,128)(2,1)}) custom-call(bf16[72,192]{1,0:T(8,128)(2,1)S(1)} %copy-done.1, bf16[72,192]{1,0:T(8,128)(2,1)S(1)} %copy-done.2, bf16[64,4096]{1,0:T(8,128)(2,1)S(1)} %bitcast.19), custom_call_target="tpu_custom_call" | custom-call | bytes 1955840 | tf_op jit(solution)/shard_map/pallas_call | solution.py:124
  96.2 0.6 add_bitcast_fusion
  (27 shorter events, 0.3 us)
Async XLA Ops:
  0.6 35.0 %collective-permute-start = (bf16[1792,512]{1,0:T(8,128)(2,1)}, bf16[1792,512]{1,0:T(8,128)(2,1)S(1)}, u32[]{:S(2)}, u32[]{:S(2)}) collective-permute-start(bf16[1792,512]{1,0:T(8,128)(2,1)} %bitcast.23), channel_id=1, source_target_pairs={{0,2},{2,0},{1,3},{3,1},{4,6},{6,4},{5,7},{7,5},{8,10},{10,8},{9,1... | collective-permute-start | bytes 5505032 | tf_op jit(solution)/shard_map/ppermute | solution.py:70
  1.2 34.5 %collective-permute-start.1 = (bf16[1792,512]{1,0:T(8,128)(2,1)}, bf16[1792,512]{1,0:T(8,128)(2,1)}, u32[]{:S(2)}, u32[]{:S(2)}) collective-permute-start(bf16[1792,512]{1,0:T(8,128)(2,1)} %bitcast.26), channel_id=1, source_target_pairs={{0,2},{2,0},{1,3},{3,1},{4,6},{6,4},{5,7},{7,5},{8,10},{10,8},{9,1... | collective-permute-start | bytes 5505032 | tf_op jit(solution)/shard_map/ppermute | solution.py:70
  1.3 35.6 %collective-permute-start.2 = (bf16[1792,512]{1,0:T(8,128)(2,1)}, bf16[1792,512]{1,0:T(8,128)(2,1)}, u32[]{:S(2)}, u32[]{:S(2)}) collective-permute-start(bf16[1792,512]{1,0:T(8,128)(2,1)} %bitcast.29), channel_id=1, source_target_pairs={{0,2},{2,0},{1,3},{3,1},{4,6},{6,4},{5,7},{7,5},{8,10},{10,8},{9,1... | collective-permute-start | bytes 5505032 | tf_op jit(solution)/shard_map/ppermute | solution.py:70
  26.5 9.2 %collective-permute-start.3 = (bf16[72,1792]{1,0:T(8,128)(2,1)S(1)}, bf16[72,1792]{1,0:T(8,128)(2,1)S(1)}, u32[]{:S(2)}, u32[]{:S(2)}) collective-permute-start(bf16[72,1792]{1,0:T(8,128)(2,1)S(1)} %get-tuple-element.29.refs_6_), channel_id=1, source_target_pairs={{0,1},{1,0},{2,3},{3,2},{4,5},{5,4},{6,7},{7,6},{8,9},{9,8},{10,11... | collective-permute-start | bytes 774152 | tf_op jit(solution)/shard_map/ppermute | solution.py:63
  28.1 14.3 %collective-permute-start.5 = (bf16[72,1792]{1,0:T(8,128)(2,1)S(1)}, bf16[72,1792]{1,0:T(8,128)(2,1)S(1)}, u32[]{:S(2)}, u32[]{:S(2)}) collective-permute-start(bf16[72,1792]{1,0:T(8,128)(2,1)S(1)} %get-tuple-element.32.refs_6_), channel_id=1, source_target_pairs={{0,1},{1,0},{2,3},{3,2},{4,5},{5,4},{6,7},{7,6},{8,9},{9,8},{10,11... | collective-permute-start | bytes 774152 | tf_op jit(solution)/shard_map/ppermute | solution.py:63
  35.7 1.2 %copy-start.6 = (bf16[1792,512]{1,0:T(8,128)(2,1)}, bf16[1792,512]{1,0:T(8,128)(2,1)S(1)}, u32[]{:S(2)}) copy-start(bf16[1792,512]{1,0:T(8,128)(2,1)S(1)} %collective-permute-done.refs_1_) | copy-start | bytes 5505028
  42.4 10.8 %copy-start.5 = (s32[8]{0:T(128)S(1)}, s32[8]{0:T(128)}, u32[]{:S(2)}) copy-start(s32[8]{0:T(128)} %flag.1) | copy-start | bytes 100
  48.9 12.5 %collective-permute-start.11 = (bf16[72,1536]{1,0:T(8,128)(2,1)S(1)}, bf16[72,1536]{1,0:T(8,128)(2,1)}, u32[]{:S(2)}, u32[]{:S(2)}) collective-permute-start(bf16[72,1536]{1,0:T(8,128)(2,1)S(1)} %get-tuple-element.42), channel_id=1, source_target_pairs={{0,16},{4,20},{8,24},{12,28},{16,0},{20,4},{24,8},{28,12},{1,17},{... | collective-permute-start | bytes 663560 | tf_op jit(solution)/shard_map/ppermute | solution.py:524
  49.8 17.9 %all-to-all-start.2 = ((bf16[4,8,4096]{2,1,0:T(8,128)(2,1)}), bf16[4,8,4096]{2,1,0:T(8,128)(2,1)S(1)}, u32[]{:S(2)}, u32[]{:S(2)}) async-start(bf16[4,8,4096]{2,1,0:T(8,128)(2,1)} %bitcast.10), calls=%async_computation.2 | async-start | bytes 524288 | tf_op jit(solution)/shard_map/all_to_all | solution.py:434
  54.6 18.6 %collective-permute-start.8 = (bf16[32,4096]{1,0:T(8,128)(2,1)S(1)}, bf16[32,4096]{1,0:T(8,128)(2,1)S(1)}, u32[]{:S(2)}, u32[]{:S(2)}) collective-permute-start(bf16[32,4096]{1,0:T(8,128)(2,1)S(1)} %get-tuple-element.40), channel_id=1, source_target_pairs={{0,16},{4,20},{8,24},{12,28},{16,0},{20,4},{24,8},{28,12},{1,17},{... | collective-permute-start | bytes 786440 | tf_op jit(solution)/shard_map/ppermute | solution.py:508
  56.7 7.1 %collective-permute-start.4 = (bf16[72,1792]{1,0:T(8,128)(2,1)S(1)}, bf16[72,1792]{1,0:T(8,128)(2,1)S(1)}, u32[]{:S(2)}, u32[]{:S(2)}) collective-permute-start(bf16[72,1792]{1,0:T(8,128)(2,1)S(1)} %get-tuple-element.31), channel_id=1, source_target_pairs={{0,1},{1,0},{2,3},{3,2},{4,5},{5,4},{6,7},{7,6},{8,9},{9,8},{10,11... | collective-permute-start | bytes 774152 | tf_op jit(solution)/shard_map/ppermute | solution.py:63
  58.2 8.3 %collective-permute-start.6 = (bf16[72,1792]{1,0:T(8,128)(2,1)S(1)}, bf16[72,1792]{1,0:T(8,128)(2,1)S(1)}, u32[]{:S(2)}, u32[]{:S(2)}) collective-permute-start(bf16[72,1792]{1,0:T(8,128)(2,1)S(1)} %get-tuple-element.37), channel_id=1, source_target_pairs={{0,1},{1,0},{2,3},{3,2},{4,5},{5,4},{6,7},{7,6},{8,9},{9,8},{10,11... | collective-permute-start | bytes 774152 | tf_op jit(solution)/shard_map/ppermute | solution.py:63
  63.0 13.9 %collective-permute-start.12 = (bf16[72,1536]{1,0:T(8,128)(2,1)}, bf16[72,1536]{1,0:T(8,128)(2,1)}, u32[]{:S(2)}, u32[]{:S(2)}) collective-permute-start(bf16[72,1536]{1,0:T(8,128)(2,1)} %broadcast_select_fusion), channel_id=1, source_target_pairs={{0,2},{2,0},{1,3},{3,1},{4,6},{6,4},{5,7},{7,5},{8,10},{10,8},{9,1... | collective-permute-start | bytes 663560 | tf_op jit(solution)/shard_map/ppermute | solution.py:75
  67.7 19.7 %all-to-all-start.1 = ((bf16[8,8,4096]{2,1,0:T(8,128)(2,1)}), bf16[8,8,4096]{2,1,0:T(8,128)(2,1)S(1)}, u32[]{:S(2)}, u32[]{:S(2)}) async-start(bf16[8,8,4096]{2,1,0:T(8,128)(2,1)} %bitcast.7), calls=%async_computation.1 | async-start | bytes 1048576 | tf_op jit(solution)/shard_map/all_to_all | solution.py:117
  73.1 14.4 %copy-start = (bf16[192,1792]{1,0:T(8,128)(2,1)S(1)}, bf16[192,1792]{1,0:T(8,128)(2,1)}, u32[]{:S(2)}) copy-start(bf16[192,1792]{1,0:T(8,128)(2,1)} %cot.1) | copy-start | bytes 2064388
  73.1 14.4 %copy-start.1 = (bf16[72,192]{1,0:T(8,128)(2,1)S(1)}, bf16[72,192]{1,0:T(8,128)(2,1)}, u32[]{:S(2)}) copy-start(bf16[72,192]{1,0:T(8,128)(2,1)} %get-tuple-element.26.select) | copy-start | bytes 82948
  73.1 14.4 %copy-start.3 = (s32[192,8]{0,1:T(8,128)S(1)}, s32[192,8]{0,1:T(8,128)}, u32[]{:S(2)}) copy-start(s32[192,8]{0,1:T(8,128)} %param.10) | copy-start | bytes 18436
  73.1 14.4 %copy-start.4 = (s32[8]{0:T(128)S(1)}, s32[8]{0:T(128)}, u32[]{:S(2)}) copy-start(s32[8]{0:T(128)} %placement.1) | copy-start | bytes 100
  74.0 16.3 %collective-permute-start.10 = (bf16[72,3584]{1,0:T(8,128)(2,1)S(1)}, bf16[72,3584]{1,0:T(8,128)(2,1)S(1)}, u32[]{:S(2)}, u32[]{:S(2)}) collective-permute-start(bf16[72,3584]{1,0:T(8,128)(2,1)S(1)} %shard_map.143), channel_id=1, source_target_pairs={{2,0},{0,1},{3,2},{1,3},{6,4},{4,5},{7,6},{5,7},{10,8},{8,9},{11,1... | collective-permute-start | bytes 1548296 | tf_op jit(solution)/shard_map/ppermute | solution.py:56
  75.5 14.7 %collective-permute-start.9 = (bf16[72,3584]{1,0:T(8,128)(2,1)S(1)}, bf16[72,3584]{1,0:T(8,128)(2,1)}, u32[]{:S(2)}, u32[]{:S(2)}) collective-permute-start(bf16[72,3584]{1,0:T(8,128)(2,1)S(1)} %shard_map.143), channel_id=1, source_target_pairs={{0,0},{2,1},{1,2},{3,3},{4,4},{6,5},{5,6},{7,7},{8,8},{10,9},{9,10... | collective-permute-start | bytes 1548296 | tf_op jit(solution)/shard_map/ppermute | solution.py:56
  87.5 6.9 %copy-start.2 = (bf16[72,192]{1,0:T(8,128)(2,1)S(1)}, bf16[72,192]{1,0:T(8,128)(2,1)}, u32[]{:S(2)}) copy-start(bf16[72,192]{1,0:T(8,128)(2,1)} %get-tuple-element.27.weighted) | copy-start | bytes 82948
  88.6 7.6 %collective-permute-start.7 = (f32[8,192]{1,0:T(8,128)S(1)}, f32[8,192]{1,0:T(8,128)S(1)}, u32[]{:S(2)}, u32[]{:S(2)}) collective-permute-start(f32[8,192]{1,0:T(8,128)S(1)} %shard_map.142), channel_id=1, source_target_pairs={{0,1},{1,0},{2,3},{3,2},{4,5},{5,4},{6,7},{7,6},{8,9},{9,8},{10,11... | collective-permute-start | bytes 18440 | tf_op jit(solution)/shard_map/ppermute | solution.py:497
